TPU v7x, 32 devices: a whole 2x2x4 slice. The times are simulated.
32 devices in a mesh: dp: 8 (over z, x), tensor: 4 (over y, core).
Axes of the slice: x: 2, y: 2, z: 4, core: 2. Of those that a mesh axis runs over, the one named last changes fastest.
Arguments:
- tokens: bfloat16 [4096, 2048], P('dp'), may hold values from -6 to 6
- cotangent: bfloat16 [4096, 2048], P('dp'), may hold values from -6 to 6
- routes: int32 [4096, 6], P('dp'), may hold values from 0 to 15, all different within a row
- seq_ids: int32 [4096], P('dp'), may hold values from 0 to 31, as said below
- positions: int32 [4096], P('dp'), may hold values from 0 to 4095, as said below
- gain_attn: bfloat16 [2048], P('dp'), may hold values from 0.5 to 1.5
- w_query: bfloat16 [2048, 3072], P('dp', 'tensor'), may hold values from -0.125 to 0.125
- w_latent: bfloat16 [2048, 576], P('dp'), may hold values from -0.125 to 0.125
- gain_latent: bfloat16 [512], P('dp'), may hold values from 0.5 to 1.5
- w_expand: bfloat16 [512, 4096], P('dp', 'tensor'), may hold values from -0.25 to 0.25
- w_output: bfloat16 [2048, 2048], P('tensor', 'dp'), may hold values from -0.75 to 0.75
- gain_ffn: bfloat16 [2048], P('dp'), may hold values from 0.5 to 1.5
- w_router: bfloat16 [2048, 16], P('dp'), may hold values from -0.0625 to 0.0625
- w_shared_gate: bfloat16 [2048, 2816], P('dp', 'tensor'), may hold values from -0.125 to 0.125
- w_shared_up: bfloat16 [2048, 2816], P('dp', 'tensor'), may hold values from -0.125 to 0.125
- w_shared_down: bfloat16 [2816, 2048], P('tensor', 'dp'), may hold values from -0.21875 to 0.21875
- w_gate: bfloat16 [16, 2048, 1408], P('dp', None, 'tensor'), may hold values from -0.125 to 0.125
- w_up: bfloat16 [16, 2048, 1408], P('dp', None, 'tensor'), may hold values from -0.125 to 0.125
- w_down: bfloat16 [16, 1408, 2048], P('dp', 'tensor'), may hold values from -0.4375 to 0.4375
Outputs:
- result: bfloat16 [4096, 2048], P('dp')
- tokens_grad: bfloat16 [4096, 2048], P('dp')
- gain_attn_grad: float32 [2048], P('dp')
- w_query_grad: float32 [2048, 3072], P('dp', 'tensor')
- w_latent_grad: float32 [2048, 576], P('dp')
- gain_latent_grad: float32 [512], P('dp')
- w_expand_grad: float32 [512, 4096], P('dp', 'tensor')
- w_output_grad: float32 [2048, 2048], P('tensor', 'dp')
- gain_ffn_grad: float32 [2048], P('dp')
- w_router_grad: float32 [2048, 16], P('dp')
- w_shared_gate_grad: float32 [2048, 2816], P('dp', 'tensor')
- w_shared_up_grad: float32 [2048, 2816], P('dp', 'tensor')
- w_shared_down_grad: float32 [2816, 2048], P('tensor', 'dp')
- w_gate_grad: float32 [16, 2048, 1408], P('dp', None, 'tensor')
- w_up_grad: float32 [16, 2048, 1408], P('dp', None, 'tensor')
- w_down_grad: float32 [16, 1408, 2048], P('dp', 'tensor')
Inputs may be any that keep to these rules, and one draw needn't show every extreme that they name: `routes`: each token names 6 different experts. `seq_ids`: ids never fall along the tokens, and every sequence lies inside one block of 512 tokens. Within a sequence, positions rise by one from token to token.
All inputs are finite; a program needn't handle non-finite values.
Results may differ from a plain program's by a relative error of at most 0.02.
Values may be sent and summed in bfloat16 or wider, within the bound.
No kernel may reach another device: no remote copies, remote signals or barrier semaphores. Data moves between devices by JAX's collectives and lax.ppermute only.
A program may use at most 384 MiB of HBM per device.

v0:
```python
import jax
import jax.numpy as jnp
from jax import lax
from jax.sharding import PartitionSpec as P

QK_NOPE = 128
QK_ROPE = 64
V_HEAD = 128
KV_RANK = 512
TOP = 6


EPSILON = 1e-06
MASKED = -1e30


def norm_forward(values, gain_full):
    inverse = lax.rsqrt(jnp.mean(values * values, axis=-1, keepdims=True) + EPSILON)
    return (values * inverse * gain_full, inverse)


def norm_backward(values, inverse, gain_full, grad_out):
    normed = values * inverse
    scaled = grad_out * gain_full
    grad_in = inverse * (scaled - normed * jnp.mean(scaled * normed, axis=-1, keepdims=True))
    return (grad_in, jnp.sum(grad_out * normed, axis=0))


def rope_tables(positions, width):
    half_width = width // 2
    frequency = jnp.power(10000.0, -jnp.arange(half_width, dtype=jnp.float32) / half_width)
    angles = positions.astype(jnp.float32)[:, None] * frequency[None, :]
    return (jnp.cos(angles), jnp.sin(angles))


def rotate(values, cosine, sine_part):
    half_width = values.shape[-1] // 2
    front_half = values[..., :half_width]
    back_half = values[..., half_width:]
    return jnp.concatenate(
        [front_half * cosine - back_half * sine_part, back_half * cosine + front_half * sine_part],
        axis=-1,
    )


def slot_layout(routes, experts, capacity):
    flat_routes = routes.reshape(-1)
    onehot = (flat_routes[:, None] == jnp.arange(experts, dtype=jnp.int32)[None, :]).astype(
        jnp.int32
    )
    before = jnp.cumsum(onehot, axis=0) - onehot
    slot_rank = jnp.sum(before * onehot, axis=1)
    route_kept = slot_rank < capacity
    slot_index = flat_routes * capacity + jnp.minimum(slot_rank, capacity - 1)
    return (slot_index.reshape(routes.shape), route_kept.reshape(routes.shape))


def slot_owner(slot_index, route_kept, kept_gates, slot_total):
    pair_count = slot_index.size
    target = jnp.where(route_kept.reshape(-1), slot_index.reshape(-1), slot_total)
    token_rows = jnp.arange(pair_count, dtype=jnp.int32) // slot_index.shape[-1]
    slot_token = jnp.zeros((slot_total,), jnp.int32).at[target].set(token_rows, mode="drop")
    slot_live = jnp.zeros((slot_total,), jnp.bool_).at[target].set(True, mode="drop")
    slot_gate = (
        jnp.zeros((slot_total,), jnp.float32).at[target].set(kept_gates.reshape(-1), mode="drop")
    )
    return (slot_token, slot_live, slot_gate)


def block_scores(query_block, key_block, seq_ids, row_start):
    row_count = query_block.shape[0]
    key_count = key_block.shape[0]
    raw_scores = jnp.einsum(
        "qhc,khc->hqk", query_block, key_block, preferred_element_type=jnp.float32
    ) * (QK_NOPE + QK_ROPE) ** (-0.5)
    query_index = row_start + jnp.arange(row_count, dtype=jnp.int32)
    key_index = jnp.arange(key_count, dtype=jnp.int32)
    allowed = (seq_ids[:, None] == seq_ids[None, :]) & (key_index[None, :] <= query_index[:, None])
    return jnp.where(allowed[None], raw_scores, MASKED)


def body(
    tokens,
    cotangent,
    routes,
    seq_ids,
    positions,
    gain_attn,
    w_query,
    w_latent,
    gain_latent,
    w_expand,
    w_output,
    gain_ffn,
    w_router,
    w_shared_gate,
    w_shared_up,
    w_shared_down,
    w_gate,
    w_up,
    w_down,
):
    (
        gain_attn_all,
        query_weight,
        latent_weight,
        gain_latent_all,
        expand_weight,
        output_weight,
        gain_ffn_all,
        router_weight,
        shared_gate_weight,
        shared_up_weight,
        shared_down_weight,
    ) = (
        lax.all_gather(gain_attn, "dp", axis=0, tiled=True),
        lax.all_gather(w_query, "dp", axis=0, tiled=True),
        lax.all_gather(w_latent, "dp", axis=0, tiled=True),
        lax.all_gather(gain_latent, "dp", axis=0, tiled=True),
        lax.all_gather(w_expand, "dp", axis=0, tiled=True),
        lax.all_gather(w_output, "dp", axis=1, tiled=True),
        lax.all_gather(gain_ffn, "dp", axis=0, tiled=True),
        lax.all_gather(w_router, "dp", axis=0, tiled=True),
        lax.all_gather(w_shared_gate, "dp", axis=0, tiled=True),
        lax.all_gather(w_shared_up, "dp", axis=0, tiled=True),
        lax.all_gather(w_shared_down, "dp", axis=1, tiled=True),
    )
    tok_count = tokens.shape[0]
    head_width = QK_NOPE + QK_ROPE
    heads_here = query_weight.shape[1] // head_width
    softmax_scale = head_width ** (-0.5)
    gain_attn_f = gain_attn_all.astype(jnp.float32)
    gain_latent_f = gain_latent_all.astype(jnp.float32)
    resid_in = tokens.astype(jnp.float32)
    normed_attn, inverse_attn = norm_forward(resid_in, gain_attn_f)
    normed_attn_low = normed_attn.astype(jnp.bfloat16)
    cosine, sine_part = rope_tables(positions, QK_ROPE)
    query_raw = jnp.dot(normed_attn_low, query_weight, preferred_element_type=jnp.float32).reshape(
        tok_count, heads_here, head_width
    )
    query_low = jnp.concatenate(
        [
            query_raw[..., :QK_NOPE],
            rotate(query_raw[..., QK_NOPE:], cosine[:, None, :], sine_part[:, None, :]),
        ],
        axis=-1,
    ).astype(jnp.bfloat16)
    latent_raw = jnp.dot(normed_attn_low, latent_weight, preferred_element_type=jnp.float32)
    latent_part = latent_raw[:, :KV_RANK]
    latent_normed, inverse_latent = norm_forward(latent_part, gain_latent_f)
    latent_low = latent_normed.astype(jnp.bfloat16)
    key_rope_low = rotate(latent_raw[:, KV_RANK:], cosine, sine_part).astype(jnp.bfloat16)
    expanded = (
        jnp.dot(latent_low, expand_weight, preferred_element_type=jnp.float32)
        .astype(jnp.bfloat16)
        .reshape(tok_count, heads_here, QK_NOPE + V_HEAD)
    )
    value_low = expanded[..., QK_NOPE:]
    key_full = jnp.concatenate(
        [
            expanded[..., :QK_NOPE],
            jnp.broadcast_to(key_rope_low[:, None, :], (tok_count, heads_here, QK_ROPE)),
        ],
        axis=-1,
    )
    row_start = 0
    row_stop = row_start + tok_count
    masked = block_scores(query_low, key_full, seq_ids, row_start)
    row_max = jnp.max(masked, axis=-1, keepdims=True)
    exponent = jnp.exp(masked - row_max)
    exp_total = jnp.sum(exponent, axis=-1, keepdims=True)
    attn_probs = (exponent / exp_total).astype(jnp.bfloat16)
    log_totals = [row_max + jnp.log(exp_total)]
    head_blocks = jnp.einsum(
        "hqk,khc->qhc", attn_probs, value_low, preferred_element_type=jnp.float32
    )
    heads_low = head_blocks.astype(jnp.bfloat16).reshape(tok_count, heads_here * V_HEAD)
    attn_part = jnp.dot(heads_low, output_weight, preferred_element_type=jnp.float32)
    resid_mid = resid_in + lax.psum(attn_part, "tensor")
    gain_ffn_f = gain_ffn_all.astype(jnp.float32)
    normed_ffn, inverse_ffn = norm_forward(resid_mid, gain_ffn_f)
    normed_ffn_low = normed_ffn.astype(jnp.bfloat16)
    experts = router_weight.shape[1]
    router_probs = jax.nn.softmax(
        jnp.dot(normed_ffn_low, router_weight, preferred_element_type=jnp.float32), axis=-1
    )
    route_hits = routes[:, :, None] == jnp.arange(experts, dtype=jnp.int32)[None, None, :]
    picked = jnp.sum(jnp.where(route_hits, router_probs[:, None, :], 0.0), axis=-1)
    picked_total = jnp.sum(picked, axis=-1, keepdims=True)
    gates = picked / picked_total
    tensor_size = lax.axis_size("tensor")
    dp_size = lax.axis_size("dp")
    exp_here = w_gate.shape[0]
    model_width = tokens.shape[1]
    capacity = tensor_size * -(-(5 * tok_count * TOP) // (4 * experts * tensor_size))
    slot_index, route_kept = slot_layout(routes, experts, capacity)
    kept_gates = jnp.where(route_kept, gates, 0.0)
    kept_float = route_kept.astype(jnp.float32)
    slot_token, slot_live, slot_gate = slot_owner(
        slot_index, route_kept, kept_gates, experts * capacity
    )
    send_rows = jnp.where(
        slot_live[:, None], normed_ffn_low[slot_token], jnp.zeros((), jnp.bfloat16)
    ).reshape(dp_size, exp_here, capacity, model_width)
    grad_send = (
        (cotangent[slot_token].astype(jnp.float32) * slot_gate[:, None])
        .astype(jnp.bfloat16)
        .reshape(dp_size, exp_here, capacity, model_width)
    )
    received, grad_recv = (
        lax.all_to_all(send_rows, "dp", split_axis=0, concat_axis=0, tiled=True),
        lax.all_to_all(grad_send, "dp", split_axis=0, concat_axis=0, tiled=True),
    )
    gate_pre = jnp.einsum("secd,edf->secf", received, w_gate, preferred_element_type=jnp.float32)
    up_pre = jnp.einsum("secd,edf->secf", received, w_up, preferred_element_type=jnp.float32)
    gate_sigmoid = jax.nn.sigmoid(gate_pre)
    gate_silu = gate_pre * gate_sigmoid
    expert_act = (gate_silu * up_pre).astype(jnp.bfloat16)
    expert_out = jnp.einsum(
        "secf,efd->secd", expert_act, w_down, preferred_element_type=jnp.float32
    ).astype(jnp.bfloat16)
    returned = lax.all_to_all(expert_out, "dp", split_axis=0, concat_axis=0, tiled=True).reshape(
        experts * capacity, model_width
    )
    gathered = returned[slot_index].astype(jnp.float32)
    routed_part = jnp.sum(gathered * kept_gates[:, :, None], axis=1)
    shared_gate = jnp.dot(normed_ffn_low, shared_gate_weight, preferred_element_type=jnp.float32)
    shared_up = jnp.dot(normed_ffn_low, shared_up_weight, preferred_element_type=jnp.float32)
    shared_sigmoid = jax.nn.sigmoid(shared_gate)
    shared_silu = shared_gate * shared_sigmoid
    shared_act = (shared_silu * shared_up).astype(jnp.bfloat16)
    shared_part = jnp.dot(shared_act, shared_down_weight, preferred_element_type=jnp.float32)
    moe_total = lax.psum((routed_part + shared_part).astype(jnp.bfloat16), "tensor").astype(
        jnp.float32
    )
    result = (resid_mid + moe_total).astype(jnp.bfloat16)
    cot_float = cotangent.astype(jnp.float32)
    act_grad = jnp.einsum("secd,efd->secf", grad_recv, w_down, preferred_element_type=jnp.float32)
    w_down_grad = jnp.einsum(
        "secf,secd->efd", expert_act, grad_recv, preferred_element_type=jnp.float32
    )
    gate_grad = (act_grad * up_pre * gate_sigmoid * (1.0 + gate_pre * (1.0 - gate_sigmoid))).astype(
        jnp.bfloat16
    )
    up_grad = (act_grad * gate_silu).astype(jnp.bfloat16)
    w_gate_grad = jnp.einsum(
        "secd,secf->edf", received, gate_grad, preferred_element_type=jnp.float32
    )
    w_up_grad = jnp.einsum("secd,secf->edf", received, up_grad, preferred_element_type=jnp.float32)
    rows_grad = (
        jnp.einsum("secf,edf->secd", gate_grad, w_gate, preferred_element_type=jnp.float32)
        + jnp.einsum("secf,edf->secd", up_grad, w_up, preferred_element_type=jnp.float32)
    ).astype(jnp.bfloat16)
    grad_back = lax.all_to_all(rows_grad, "dp", split_axis=0, concat_axis=0, tiled=True).reshape(
        experts * capacity, model_width
    )
    routed_in_grad = jnp.sum(
        grad_back[slot_index].astype(jnp.float32) * kept_float[:, :, None], axis=1
    )
    gate_grad_part = jnp.sum(gathered * cot_float[:, None, :], axis=-1) * kept_float
    shared_act_grad = jnp.einsum(
        "td,fd->tf", cotangent, shared_down_weight, preferred_element_type=jnp.float32
    )
    shared_down_grad = jnp.einsum(
        "tf,td->fd", shared_act, cotangent, preferred_element_type=jnp.float32
    )
    shared_gate_grad = (
        shared_act_grad * shared_up * shared_sigmoid * (1.0 + shared_gate * (1.0 - shared_sigmoid))
    ).astype(jnp.bfloat16)
    shared_up_grad = (shared_act_grad * shared_silu).astype(jnp.bfloat16)
    shared_gate_weight_grad = jnp.einsum(
        "td,tf->df", normed_ffn_low, shared_gate_grad, preferred_element_type=jnp.float32
    )
    shared_up_weight_grad = jnp.einsum(
        "td,tf->df", normed_ffn_low, shared_up_grad, preferred_element_type=jnp.float32
    )
    shared_in_grad = jnp.einsum(
        "tf,df->td", shared_gate_grad, shared_gate_weight, preferred_element_type=jnp.float32
    ) + jnp.einsum(
        "tf,df->td", shared_up_grad, shared_up_weight, preferred_element_type=jnp.float32
    )
    ffn_in_sum, gate_grad_sum = lax.psum(
        (routed_in_grad + shared_in_grad, gate_grad_part), "tensor"
    )
    picked_grad = (
        gate_grad_sum - jnp.sum(gate_grad_sum * gates, axis=-1, keepdims=True)
    ) / picked_total
    probs_grad = jnp.sum(jnp.where(route_hits, picked_grad[:, :, None], 0.0), axis=1)
    logit_grad = (
        router_probs * (probs_grad - jnp.sum(router_probs * probs_grad, axis=-1, keepdims=True))
    ).astype(jnp.bfloat16)
    router_grad = jnp.einsum(
        "td,te->de", normed_ffn_low, logit_grad, preferred_element_type=jnp.float32
    )
    ffn_in = ffn_in_sum + jnp.einsum(
        "te,de->td", logit_grad, router_weight, preferred_element_type=jnp.float32
    )
    ffn_resid_grad, gain_ffn_grad = norm_backward(resid_mid, inverse_ffn, gain_ffn_f, ffn_in)
    mid_grad = cot_float + ffn_resid_grad
    mid_low = mid_grad.astype(jnp.bfloat16)
    output_weight_grad = jnp.einsum(
        "th,td->hd", heads_low, mid_low, preferred_element_type=jnp.float32
    )
    heads_grad = (
        jnp.einsum("td,hd->th", mid_low, output_weight, preferred_element_type=jnp.float32)
        .astype(jnp.bfloat16)
        .reshape(tok_count, heads_here, V_HEAD)
    )
    query_grad_blocks = []
    key_grad = jnp.zeros((tok_count, heads_here, head_width), jnp.float32)
    value_grad = jnp.zeros((tok_count, heads_here, V_HEAD), jnp.float32)
    for block_number, row_start in enumerate(range(0, tok_count, tok_count)):
        row_stop = row_start + tok_count
        masked = block_scores(query_low, key_full, seq_ids, row_start)
        attn_probs = jnp.exp(masked - log_totals[block_number])
        probs_low = attn_probs.astype(jnp.bfloat16)
        prob_grad = jnp.einsum(
            "qhc,khc->hqk", heads_grad, value_low, preferred_element_type=jnp.float32
        )
        row_dot = jnp.sum(attn_probs * prob_grad, axis=-1, keepdims=True)
        score_grad = (attn_probs * (prob_grad - row_dot)).astype(jnp.bfloat16)
        query_grad_blocks.append(
            jnp.einsum("hqk,khc->qhc", score_grad, key_full, preferred_element_type=jnp.float32)
            * softmax_scale
        )
        key_grad = key_grad.at[:row_stop].add(
            jnp.einsum("hqk,qhc->khc", score_grad, query_low, preferred_element_type=jnp.float32)
            * softmax_scale
        )
        value_grad = value_grad.at[:row_stop].add(
            jnp.einsum("hqk,qhc->khc", probs_low, heads_grad, preferred_element_type=jnp.float32)
        )
    query_grad = query_grad_blocks[0]
    query_pre_grad = jnp.concatenate(
        [
            query_grad[..., :QK_NOPE],
            rotate(query_grad[..., QK_NOPE:], cosine[:, None, :], -sine_part[:, None, :]),
        ],
        axis=-1,
    )
    query_pre_grad = query_pre_grad.astype(jnp.bfloat16).reshape(tok_count, heads_here * head_width)
    attn_in_part = jnp.einsum(
        "tq,dq->td", query_pre_grad, query_weight, preferred_element_type=jnp.float32
    )
    query_weight_grad = jnp.einsum(
        "td,tq->dq", normed_attn_low, query_pre_grad, preferred_element_type=jnp.float32
    )
    expand_grad = (
        jnp.concatenate([key_grad[..., :QK_NOPE], value_grad], axis=-1)
        .astype(jnp.bfloat16)
        .reshape(tok_count, heads_here * (QK_NOPE + V_HEAD))
    )
    latent_part_grad = jnp.einsum(
        "te,re->tr", expand_grad, expand_weight, preferred_element_type=jnp.float32
    )
    expand_weight_grad = jnp.einsum(
        "tr,te->re", latent_low, expand_grad, preferred_element_type=jnp.float32
    )
    rope_part_grad = jnp.sum(key_grad[..., QK_NOPE:], axis=1)
    attn_in_sum, latent_sum, rope_sum = lax.psum(
        (attn_in_part, latent_part_grad, rope_part_grad), "tensor"
    )
    latent_pre_grad, gain_latent_grad = norm_backward(
        latent_part, inverse_latent, gain_latent_f, latent_sum
    )
    latent_all_grad = jnp.concatenate(
        [latent_pre_grad, rotate(rope_sum, cosine, -sine_part)], axis=-1
    ).astype(jnp.bfloat16)
    attn_in = attn_in_sum + jnp.einsum(
        "tc,dc->td", latent_all_grad, latent_weight, preferred_element_type=jnp.float32
    )
    latent_weight_grad = jnp.einsum(
        "td,tc->dc", normed_attn_low, latent_all_grad, preferred_element_type=jnp.float32
    )
    input_grad, gain_attn_grad = norm_backward(resid_in, inverse_attn, gain_attn_f, attn_in)
    tokens_grad = (mid_grad + input_grad).astype(jnp.bfloat16)
    (
        gain_attn_share,
        query_share,
        latent_share,
        gain_latent_share,
        expand_share,
        output_share,
        gain_ffn_share,
        router_share,
        shared_gate_share,
        shared_up_share,
        shared_down_share,
    ) = (
        lax.psum_scatter(
            gain_attn_grad.astype(jnp.bfloat16), "dp", scatter_dimension=0, tiled=True
        ).astype(jnp.float32),
        lax.psum_scatter(
            query_weight_grad.astype(jnp.bfloat16), "dp", scatter_dimension=0, tiled=True
        ).astype(jnp.float32),
        lax.psum_scatter(
            latent_weight_grad.astype(jnp.bfloat16), "dp", scatter_dimension=0, tiled=True
        ).astype(jnp.float32),
        lax.psum_scatter(
            gain_latent_grad.astype(jnp.bfloat16), "dp", scatter_dimension=0, tiled=True
        ).astype(jnp.float32),
        lax.psum_scatter(
            expand_weight_grad.astype(jnp.bfloat16), "dp", scatter_dimension=0, tiled=True
        ).astype(jnp.float32),
        lax.psum_scatter(
            output_weight_grad.astype(jnp.bfloat16), "dp", scatter_dimension=1, tiled=True
        ).astype(jnp.float32),
        lax.psum_scatter(
            gain_ffn_grad.astype(jnp.bfloat16), "dp", scatter_dimension=0, tiled=True
        ).astype(jnp.float32),
        lax.psum_scatter(
            router_grad.astype(jnp.bfloat16), "dp", scatter_dimension=0, tiled=True
        ).astype(jnp.float32),
        lax.psum_scatter(
            shared_gate_weight_grad.astype(jnp.bfloat16), "dp", scatter_dimension=0, tiled=True
        ).astype(jnp.float32),
        lax.psum_scatter(
            shared_up_weight_grad.astype(jnp.bfloat16), "dp", scatter_dimension=0, tiled=True
        ).astype(jnp.float32),
        lax.psum_scatter(
            shared_down_grad.astype(jnp.bfloat16), "dp", scatter_dimension=1, tiled=True
        ).astype(jnp.float32),
    )
    return (
        result,
        tokens_grad,
        gain_attn_share,
        query_share,
        latent_share,
        gain_latent_share,
        expand_share,
        output_share,
        gain_ffn_share,
        router_share,
        shared_gate_share,
        shared_up_share,
        shared_down_share,
        w_gate_grad,
        w_up_grad,
        w_down_grad,
    )


def solution(mesh):
    return jax.shard_map(
        body,
        mesh=mesh,
        in_specs=(
            P("dp", None),
            P("dp", None),
            P("dp", None),
            P("dp"),
            P("dp"),
            P("dp"),
            P("dp", "tensor"),
            P("dp", None),
            P("dp"),
            P("dp", "tensor"),
            P("tensor", "dp"),
            P("dp"),
            P("dp", None),
            P("dp", "tensor"),
            P("dp", "tensor"),
            P("tensor", "dp"),
            P("dp", None, "tensor"),
            P("dp", None, "tensor"),
            P("dp", "tensor", None),
        ),
        out_specs=(
            P("dp", None),
            P("dp", None),
            P("dp"),
            P("dp", "tensor"),
            P("dp", None),
            P("dp"),
            P("dp", "tensor"),
            P("tensor", "dp"),
            P("dp"),
            P("dp", None),
            P("dp", "tensor"),
            P("dp", "tensor"),
            P("tensor", "dp"),
            P("dp", None, "tensor"),
            P("dp", None, "tensor"),
            P("dp", "tensor", None),
        ),
        check_vma=False,
    )
```

profile of v0, /device:TPU:0, one launch (start us, length us, event | category | flops | bytes accessed | tf_op | source)
XLA Modules:
  0.0 2923.4 jit_solution(1285146385822788760)
XLA Ops:
  13.6 23.6 all-reduce
  39.9 16.7 all-gather
  72.5 35.7 %all-gather.12.cloned.1.call-done = bf16[512,1024]{1,0:T(8,128)(2,1)} async-done(((bf16[64,1024]{1,0:T(8,128)(2,1)}), bf16[512,1024]{1,0:T(8,128)(2,1)}) %all-gather.12.cloned.1.call-update) | async-done | bytes 1048592 | tf_op jit(solution)/shard_map/all_gather | solution.py:120
  117.6 51.5 %all-gather.14.cloned.1.call-done = bf16[2048,768]{1,0:T(8,128)(2,1)} async-done(((bf16[256,768]{1,0:T(8,128)(2,1)}), bf16[2048,768]{1,0:T(8,128)(2,1)}) %all-gather.14.cloned.1.call-update) | async-done | bytes 3145744 | tf_op jit(solution)/shard_map/all_gather | solution.py:117
  179.3 40.7 %all-gather.16.cloned.1.call-done = bf16[512,2048]{1,0:T(8,128)(2,1)} async-done(((bf16[512,256]{1,0:T(8,128)(2,1)}), bf16[512,2048]{1,0:T(8,128)(2,1)}) %all-gather.16.cloned.1.call-update) | async-done | bytes 2097168 | tf_op jit(solution)/shard_map/all_gather | solution.py:121
  226.1 17.7 all-gather.1
  253.4 30.9 %all_gather.40 = bf16[2048,16]{0,1:T(8,128)(2,1)S(1)} all-gather(bf16[256,16]{0,1:T(8,128)(2,1)} %param.39), channel_id=1, replica_groups=mesh['dp'=8,'tensor'=4] {'dp'}, dimensions={0}, use_global_device_ids=true | all-gather | bytes 73728 | tf_op jit(solution)/shard_map/all_gather | solution.py:123
  284.3 24.5 all-reduce.11.cloned.1.call-done
  317.4 13.4 scatter_custom_fusion
  330.9 11.8 scatter_custom_fusion.1
  342.7 31.3 %gather_fusion = bf16[3840,2048]{1,0:T(8,128)(2,1)} fusion(bf16[512,2048]{1,0:T(8,128)(2,1)} %copy-done.2, s32[4096]{0:T(1024)S(1)} %pad_clamp_fusion), kind=kCustom, calls=%fused_computation | custom fusion | bytes 31472640 | tf_op jit(solution)/shard_map/gather | solution.py:203
  374.0 13.4 broadcast_select_fusion
  393.1 12.0 scatter_custom_fusion.2
  405.2 31.4 %gather_fusion.2 = bf16[3840,2048]{1,0:T(8,128)(2,1)} fusion(bf16[512,2048]{1,0:T(8,128)(2,1)} %param.28, s32[4096]{0:T(1024)S(1)} %pad_clamp_fusion), kind=kCustom, calls=%fused_computation.2 | custom fusion | bytes 31472640 | tf_op jit(solution)/shard_map/gather | solution.py:206
  436.6 14.1 fusion
  450.7 282.7 %all-to-all-done = bf16[8,2,240,2048]{3,2,1,0:T(8,128)(2,1)} async-done(((bf16[8,2,240,2048]{3,2,1,0:T(8,128)(2,1)}), bf16[8,2,240,2048]{3,2,1,0:T(8,128)(2,1)}, u32[]{:S(2)}, u32[]{:S(2)}) %all-to-all-start) | async-done | bytes 15728672 | tf_op jit(solution)/shard_map/all_to_all | solution.py:211
  739.2 12.1 fusion.6
  762.5 316.2 %all-to-all-done.2 = bf16[8,2,240,2048]{3,2,1,0:T(8,128)(2,1)} async-done(((bf16[8,2,240,2048]{3,2,1,0:T(8,128)(2,1)}), bf16[8,2,240,2048]{3,2,1,0:T(8,128)(2,1)}, u32[]{:S(2)}, u32[]{:S(2)}) %all-to-all-start.2) | async-done | bytes 15728672 | tf_op jit(solution)/shard_map/all_to_all | solution.py:212
  1078.7 15.3 fusion.17
  1093.9 13.9 convert_bitcast_fusion
  1107.8 13.5 copy.127
  1127.2 16.3 fusion.38
  1143.5 15.0 fusion.1
  1164.9 301.0 %all-to-all-done.1 = bf16[8,2,240,2048]{3,2,1,0:T(8,128)(2,1)} async-done(((bf16[8,2,240,2048]{3,2,1,0:T(8,128)(2,1)}), bf16[8,2,240,2048]{3,2,1,0:T(8,128)(2,1)}, u32[]{:S(2)}, u32[]{:S(2)}) %all-to-all-start.1) | async-done | bytes 15728672 | tf_op jit(solution)/shard_map/all_to_all | solution.py:222
  1478.8 296.4 %all-gather.20.cloned.1.call-done = bf16[2048,704]{0,1:T(8,128)(2,1)} async-done(((bf16[256,704]{0,1:T(8,128)(2,1)}), bf16[2048,704]{0,1:T(8,128)(2,1)}) %all-gather.20.cloned.1.call-update) | async-done | bytes 2883600 | tf_op jit(solution)/shard_map/all_gather | solution.py:125
  1779.8 114.7 %all-gather.18.cloned.1.call-done = bf16[2048,704]{0,1:T(8,128)(2,1)} async-done(((bf16[256,704]{0,1:T(8,128)(2,1)}), bf16[2048,704]{0,1:T(8,128)(2,1)}) %all-gather.18.cloned.1.call-update) | async-done | bytes 2883600 | tf_op jit(solution)/shard_map/all_gather | solution.py:124
  1899.2 55.2 %all-gather.22.cloned.1.call-done = bf16[704,2048]{1,0:T(8,128)(2,1)} async-done(((bf16[704,256]{1,0:T(8,128)(2,1)}), bf16[704,2048]{1,0:T(8,128)(2,1)}) %all-gather.22.cloned.1.call-update) | async-done | bytes 2883600 | tf_op jit(solution)/shard_map/all_gather | solution.py:126
  1965.0 31.5 %gather_fusion.1 = bf16[3072,2048]{1,0:T(8,128)(2,1)} fusion(bf16[3840,2048]{1,0:T(8,128)(2,1)} %bitcast.19, s32[3072]{0:T(1024)S(1)} %broadcast_clamp_fusion), kind=kCustom, calls=%fused_computation.1 | custom fusion | bytes 25178112 | tf_op jit(solution)/shard_map/gather | solution.py:225
  1996.6 22.2 reshape.493
  2018.8 31.3 %gather_fusion.3 = bf16[3072,2048]{1,0:T(8,128)(2,1)} fusion(bf16[3840,2048]{1,0:T(8,128)(2,1)} %bitcast.26, s32[3072]{0:T(1024)S(1)} %broadcast_clamp_fusion), kind=kCustom, calls=%fused_computation.3 | custom fusion | bytes 25178112 | tf_op jit(solution)/shard_map/gather | solution.py:258
  2050.1 22.1 reshape.494
  2072.2 17.9 multiply_reduce_fusion.1
  2094.3 21.3 multiply_reduce_fusion
  2146.6 31.5 %all-reduce.15.cloned.1.call-done = f32[512,2048]{1,0:T(8,128)} async-done(((f32[512,2048]{1,0:T(8,128)}), f32[512,2048]{1,0:T(8,128)}) %all-reduce.15.cloned.1.call-update) | async-done | bytes 4194320 | tf_op jit(solution)/shard_map/psum | solution.py:282
  2184.8 47.5 %all-reduce.13.cloned.1.call-done = bf16[512,2048]{1,0:T(8,128)(2,1)} async-done(((bf16[512,2048]{1,0:T(8,128)(2,1)}), bf16[512,2048]{1,0:T(8,128)(2,1)}) %all-reduce.13.cloned.1.call-update) | async-done | bytes 2097168 | tf_op jit(solution)/shard_map/psum | solution.py:233
  2270.6 39.0 %reduce-scatter.19.cloned.1.call-done = bf16[256,704]{0,1:T(8,128)(2,1)} async-done(((bf16[2048,704]{0,1:T(8,128)(2,1)}), bf16[256,704]{0,1:T(8,128)(2,1)}) %reduce-scatter.19.cloned.1.call-update) | async-done | bytes 360464 | tf_op jit(solution)/shard_map/reduce_scatter | solution.py:414
  2311.5 73.7 %reduce-scatter.21.cloned.1.call-done = bf16[256,704]{0,1:T(8,128)(2,1)} async-done(((bf16[2048,704]{0,1:T(8,128)(2,1)}), bf16[256,704]{0,1:T(8,128)(2,1)}) %reduce-scatter.21.cloned.1.call-update) | async-done | bytes 360464 | tf_op jit(solution)/shard_map/reduce_scatter | solution.py:417
  2387.0 73.8 %reduce-scatter.23.cloned.1.call-done = bf16[704,256]{1,0:T(8,128)(2,1)} async-done(((bf16[704,2048]{1,0:T(8,128)(2,1)}), bf16[704,256]{1,0:T(8,128)(2,1)}) %reduce-scatter.23.cloned.1.call-update) | async-done | bytes 360464 | tf_op jit(solution)/shard_map/reduce_scatter | solution.py:420
  2462.8 15.1 convolution_bitcast_fusion
  2477.9 90.5 %all-reduce.17.cloned.1.call-done = (f32[512,2048]{1,0:T(8,128)}, f32[512,64]{0,1:T(8,128)}, f32[512,512]{0,1:T(8,128)}) async-done(((f32[512,2048]{1,0:T(8,128)}, f32[512,64]{0,1:T(8,128)}, f32[512,512]{0,1:T(8,128)}), (f32[512,2048]{1,0:T(8,128)}, f32[512,64]{0,1:T(8,128)}, f32[512,512]{0,1:T(8,128)})) %all-reduce.17.cloned.1.call-update) | async-done | bytes 5373968 | tf_op jit(solution)/shard_map/psum | solution.py:360
  2576.2 15.2 fusion.32
  2591.5 13.8 convolution_bitcast_fusion.1
  2605.2 21.6 reduce-scatter.17.cloned.1.call-done
  2628.2 65.2 %reduce-scatter.13.cloned.1.call-done = bf16[64,1024]{1,0:T(8,128)(2,1)} async-done(((bf16[512,1024]{1,0:T(8,128)(2,1)}), bf16[64,1024]{1,0:T(8,128)(2,1)}) %reduce-scatter.13.cloned.1.call-update) | async-done | bytes 131088 | tf_op jit(solution)/shard_map/reduce_scatter | solution.py:402
  2702.5 20.3 all-reduce.5
  2730.8 34.2 %reduce-scatter.15.cloned.1.call-done = bf16[512,256]{1,0:T(8,128)(2,1)} async-done(((bf16[512,2048]{1,0:T(8,128)(2,1)}), bf16[512,256]{1,0:T(8,128)(2,1)}) %reduce-scatter.15.cloned.1.call-update) | async-done | bytes 262160 | tf_op jit(solution)/shard_map/reduce_scatter | solution.py:405
  2766.8 75.0 %reduce-scatter.9.cloned.1.call-done = bf16[256,768]{1,0:T(8,128)(2,1)} async-done(((bf16[2048,768]{1,0:T(8,128)(2,1)}), bf16[256,768]{1,0:T(8,128)(2,1)}) %reduce-scatter.9.cloned.1.call-update) | async-done | bytes 393232 | tf_op jit(solution)/shard_map/reduce_scatter | solution.py:393
  2843.8 70.8 %reduce-scatter.11.cloned.1.call-done = bf16[256,576]{0,1:T(8,128)(2,1)} async-done(((bf16[2048,576]{0,1:T(8,128)(2,1)}), bf16[256,576]{0,1:T(8,128)(2,1)}) %reduce-scatter.11.cloned.1.call-update) | async-done | bytes 294928 | tf_op jit(solution)/shard_map/reduce_scatter | solution.py:396
  (345 shorter events, 250.9 us)
Async XLA Ops:
  7.2 1071.5 %copy-start = (bf16[2,352,2048]{2,1,0:T(8,128)(2,1)S(1)}, bf16[2,352,2048]{2,1,0:T(8,128)(2,1)}, u32[]{:S(2)}) copy-start(bf16[2,352,2048]{2,1,0:T(8,128)(2,1)} %param.45) | copy-start | bytes 8650756
  7.2 60.3 %all-gather.10.cloned.1.call-start = ((), (), s32[]{:S(2)}) async-start(), calls=%async_computation.12 | async-start | bytes 2654208 | tf_op jit(solution)/shard_map/all_gather | solution.py:118
  7.9 100.2 %all-gather.12.cloned.1.call-start = ((), (), s32[]{:S(2)}) async-start(), calls=%async_computation.13 | async-start | bytes 1179648 | tf_op jit(solution)/shard_map/all_gather | solution.py:120
  8.7 160.4 %all-gather.14.cloned.1.call-start = ((), (), s32[]{:S(2)}) async-start(), calls=%async_computation.14 | async-start | bytes 3538944 | tf_op jit(solution)/shard_map/all_gather | solution.py:117
  9.4 210.6 %all-gather.16.cloned.1.call-start = ((), (), s32[]{:S(2)}) async-start(), calls=%async_computation.15 | async-start | bytes 2359296 | tf_op jit(solution)/shard_map/all_gather | solution.py:121
  10.0 298.8 %all-reduce.11.cloned.1.call-start = ((), (), s32[]{:S(2)}) async-start(), calls=%async_computation.16 | async-start | bytes 8388608 | tf_op jit(solution)/shard_map/psum | solution.py:179
  37.1 71.0 %copy-start.72 = (f32[512]{0:T(512)}, f32[512]{0:T(512)S(1)}, u32[]{:S(2)}) copy-start(f32[512]{0:T(512)S(1)} %convert_element_type.213) | copy-start | bytes 6148
  37.8 77.1 %copy-start.78 = (f32[512]{0:T(512)}, f32[512]{0:T(512)S(1)}, u32[]{:S(2)}) copy-start(f32[512]{0:T(512)S(1)} %convert_element_type.216) | copy-start | bytes 6148
  39.9 129.2 %copy-start.80 = (f32[512]{0:T(512)}, f32[512]{0:T(512)S(1)}, u32[]{:S(2)}) copy-start(f32[512]{0:T(512)S(1)} %add_rsqrt_fusion.2) | copy-start | bytes 6148
  56.6 112.5 %copy-start.68 = (f32[8,1,256]{2,1,0:T(1,128)}, f32[8,1,256]{2,1,0:T(1,128)S(1)}, u32[]{:S(2)}) copy-start(f32[8,1,256]{2,1,0:T(1,128)S(1)} %convert_element_type.277) | copy-start | bytes 24580
  72.5 41.4 %copy-start.74 = (f32[512]{0:T(512)}, f32[512]{0:T(512)S(1)}, u32[]{:S(2)}) copy-start(f32[512]{0:T(512)S(1)} %add_rsqrt_fusion.1) | copy-start | bytes 6148
  114.9 59.0 %copy-start.20 = (bf16[512,4,128]{0,2,1:T(8,128)(2,1)}, bf16[512,4,128]{0,2,1:T(8,128)(2,1)S(1)}, u32[]{:S(2)}) copy-start(bf16[512,4,128]{0,2,1:T(8,128)(2,1)S(1)} %slice.131) | copy-start | bytes 1572868
  117.0 56.8 %copy-start.35 = (f32[512,32]{0,1:T(8,128)}, f32[512,32]{0,1:T(8,128)S(1)}, u32[]{:S(2)}) copy-start(f32[512,32]{0,1:T(8,128)S(1)} %get-tuple-element.98) | copy-start | bytes 196612
  179.3 45.6 %copy-start.39 = (bf16[4,128,512]{2,1,0:T(8,128)(2,1)}, bf16[4,128,512]{2,1,0:T(8,128)(2,1)S(1)}, u32[]{:S(2)}) copy-start(bf16[4,128,512]{2,1,0:T(8,128)(2,1)S(1)} %fusion.53) | copy-start | bytes 1572868
  284.3 29.1 copy-start.33
  284.3 28.6 copy-start.49
  315.7 58.4 %copy-start.55 = (f32[512]{0:T(512)}, f32[512]{0:T(512)S(1)}, u32[]{:S(2)}) copy-start(f32[512]{0:T(512)S(1)} %get-tuple-element.103) | copy-start | bytes 6148
  316.4 57.7 %copy-start.57 = (f32[512]{0:T(512)}, f32[512]{0:T(512)S(1)}, u32[]{:S(2)}) copy-start(f32[512]{0:T(512)S(1)} %get-tuple-element.64) | copy-start | bytes 6148
  317.3 56.7 %copy-start.76 = (pred[3072]{0:T(1024)(128)(4,1)}, pred[3072]{0:T(1024)(128)(4,1)S(1)}, u32[]{:S(2)}) copy-start(pred[3072]{0:T(1024)(128)(4,1)S(1)} %get-tuple-element.73) | copy-start | bytes 9220
  387.4 346.0 %all-to-all-start = ((bf16[8,2,240,2048]{3,2,1,0:T(8,128)(2,1)}), bf16[8,2,240,2048]{3,2,1,0:T(8,128)(2,1)}, u32[]{:S(2)}, u32[]{:S(2)}) async-start(bf16[8,2,240,2048]{3,2,1,0:T(8,128)(2,1)} %broadcast_select_fusion), calls=%async_computation | async-start | bytes 31457280 | tf_op jit(solution)/shard_map/all_to_all | solution.py:211
  733.5 345.2 %all-to-all-start.2 = ((bf16[8,2,240,2048]{3,2,1,0:T(8,128)(2,1)}), bf16[8,2,240,2048]{3,2,1,0:T(8,128)(2,1)}, u32[]{:S(2)}, u32[]{:S(2)}) async-start(bf16[8,2,240,2048]{3,2,1,0:T(8,128)(2,1)} %fusion), calls=%async_computation.2 | async-start | bytes 31457280 | tf_op jit(solution)/shard_map/all_to_all | solution.py:212
  1121.3 344.6 %all-to-all-start.1 = ((bf16[8,2,240,2048]{3,2,1,0:T(8,128)(2,1)}), bf16[8,2,240,2048]{3,2,1,0:T(8,128)(2,1)}, u32[]{:S(2)}, u32[]{:S(2)}) async-start(bf16[8,2,240,2048]{3,2,1,0:T(8,128)(2,1)} %copy.127), calls=%async_computation.1 | async-start | bytes 31457280 | tf_op jit(solution)/shard_map/all_to_all | solution.py:222
  1465.9 552.9 %all-to-all-start.3 = ((bf16[8,2,240,2048]{3,2,1,0:T(8,128)(2,1)}), bf16[8,2,240,2048]{3,2,1,0:T(8,128)(2,1)}, u32[]{:S(2)}, u32[]{:S(2)}) async-start(bf16[8,2,240,2048]{3,2,1,0:T(8,128)(2,1)} %copy.132), calls=%async_computation.3 | async-start | bytes 31457280 | tf_op jit(solution)/shard_map/all_to_all | solution.py:254
  1471.5 303.7 %copy-start.3 = (bf16[512,2048]{1,0:T(8,128)(2,1)S(1)}, bf16[512,2048]{1,0:T(8,128)(2,1)}, u32[]{:S(2)}) copy-start(bf16[512,2048]{1,0:T(8,128)(2,1)} %copy-done.2) | copy-start | bytes 6291460
  1471.6 303.7 %all-gather.20.cloned.1.call-start = ((), (), s32[]{:S(2)}) async-start(), calls=%async_computation.18 | async-start | bytes 3244032 | tf_op jit(solution)/shard_map/all_gather | solution.py:125
  1472.1 422.4 %all-gather.18.cloned.1.call-start = ((), (), s32[]{:S(2)}) async-start(), calls=%async_computation.17 | async-start | bytes 3244032 | tf_op jit(solution)/shard_map/all_gather | solution.py:124
  1472.9 481.5 %all-gather.22.cloned.1.call-start = ((), (), s32[]{:S(2)}) async-start(), calls=%async_computation.19 | async-start | bytes 3244032 | tf_op jit(solution)/shard_map/all_gather | solution.py:126
  1473.6 704.5 %all-reduce.15.cloned.1.call-start = ((), (), s32[]{:S(2)}) async-start(), calls=%async_computation.21 | async-start | bytes 8388608 | tf_op jit(solution)/shard_map/psum | solution.py:282
  1478.6 301.3 %copy-start.60 = (pred[512,6]{0,1:T(8,128)(4,1)}, pred[512,6]{0,1:T(8,128)(4,1)S(1)}, u32[]{:S(2)}) copy-start(pred[512,6]{0,1:T(8,128)(4,1)S(1)} %copy.128) | copy-start | bytes 9220
  1961.1 35.4 %copy-start.32 = (bf16[512,704]{0,1:T(8,128)(2,1)}, bf16[512,704]{0,1:T(8,128)(2,1)S(1)}, u32[]{:S(2)}) copy-start(bf16[512,704]{0,1:T(8,128)(2,1)S(1)} %get-tuple-element.82) | copy-start | bytes 2162692
  2072.2 17.9 copy-start.23
  2094.2 21.4 copy-start.86
  2094.2 138.2 %all-reduce.13.cloned.1.call-start = ((), (), s32[]{:S(2)}) async-start(), calls=%async_computation.20 | async-start | bytes 4194304 | tf_op jit(solution)/shard_map/psum | solution.py:233
  2122.0 187.6 %reduce-scatter.19.cloned.1.call-start = ((), (), s32[]{:S(2)}) async-start(), calls=%async_computation.27 | async-start | bytes 3244032 | tf_op jit(solution)/shard_map/reduce_scatter | solution.py:414
  2126.5 258.6 %reduce-scatter.21.cloned.1.call-start = ((), (), s32[]{:S(2)}) async-start(), calls=%async_computation.28 | async-start | bytes 3244032 | tf_op jit(solution)/shard_map/reduce_scatter | solution.py:417
  2129.8 331.0 %reduce-scatter.23.cloned.1.call-start = ((), (), s32[]{:S(2)}) async-start(), calls=%async_computation.29 | async-start | bytes 3244032 | tf_op jit(solution)/shard_map/reduce_scatter | solution.py:420
  2130.0 48.1 %copy-start.34 = (bf16[2048,16]{0,1:T(8,128)(2,1)S(1)}, bf16[2048,16]{0,1:T(8,128)(2,1)}, u32[]{:S(2)}) copy-start(bf16[2048,16]{0,1:T(8,128)(2,1)} %copy-done.33) | copy-start | bytes 196612
  2130.0 48.1 %copy-start.50 = (f32[8,1,256]{2,1,0:T(1,128)S(1)}, f32[8,1,256]{2,1,0:T(1,128)}, u32[]{:S(2)}) copy-start(f32[8,1,256]{2,1,0:T(1,128)} %convert_element_type.278) | copy-start | bytes 24580
  2130.0 48.1 %copy-start.63 = (f32[512]{0:T(512)S(1)}, f32[512]{0:T(512)}, u32[]{:S(2)}) copy-start(f32[512]{0:T(512)} %copy-done.62) | copy-start | bytes 6148
  2135.1 433.2 %all-reduce.17.cloned.1.call-start = ((), (), s32[]{:S(2)}) async-start(), calls=%async_computation.30 | async-start | bytes 10747904 | tf_op jit(solution)/shard_map/psum | solution.py:360
  2255.5 371.4 %reduce-scatter.17.cloned.1.call-start = ((), (), s32[]{:S(2)}) async-start(), calls=%async_computation.26 | async-start | bytes 73728 | tf_op jit(solution)/shard_map/reduce_scatter | solution.py:411
  2256.6 436.9 %reduce-scatter.13.cloned.1.call-start = ((), (), s32[]{:S(2)}) async-start(), calls=%async_computation.24 | async-start | bytes 1179648 | tf_op jit(solution)/shard_map/reduce_scatter | solution.py:402
  2260.2 504.9 %reduce-scatter.15.cloned.1.call-start = ((), (), s32[]{:S(2)}) async-start(), calls=%async_computation.25 | async-start | bytes 2359296 | tf_op jit(solution)/shard_map/reduce_scatter | solution.py:405
  2265.5 576.4 %reduce-scatter.9.cloned.1.call-start = ((), (), s32[]{:S(2)}) async-start(), calls=%async_computation.22 | async-start | bytes 3538944 | tf_op jit(solution)/shard_map/reduce_scatter | solution.py:393
  2269.3 645.3 %reduce-scatter.11.cloned.1.call-start = ((), (), s32[]{:S(2)}) async-start(), calls=%async_computation.23 | async-start | bytes 2654208 | tf_op jit(solution)/shard_map/reduce_scatter | solution.py:396
  2462.8 107.5 %copy-start.79 = (f32[512]{0:T(512)S(1)}, f32[512]{0:T(512)}, u32[]{:S(2)}) copy-start(f32[512]{0:T(512)} %copy-done.78) | copy-start | bytes 6148
  2462.8 107.5 %copy-start.82 = (f32[32]{0:T(128)S(1)}, f32[32]{0:T(128)}, u32[]{:S(2)}) copy-start(f32[32]{0:T(128)} %multiply_power_fusion) | copy-start | bytes 388
  2724.1 192.3 %copy-start.1 = (bf16[2,352,2048]{2,1,0:T(8,128)(2,1)S(1)}, bf16[2,352,2048]{2,1,0:T(8,128)(2,1)}, u32[]{:S(2)}) copy-start(bf16[2,352,2048]{2,1,0:T(8,128)(2,1)} %param.45) | copy-start | bytes 8650756
  (62 other events, 329.2 us)
Sparse Core Ops, SparseCore 0:
  10.0 57.4 all-gather.9
  69.6 38.4 all-gather.11
  110.4 58.7 all-gather.13
  171.0 48.9 all-gather.15
  225.1 83.6 all-reduce.10
  1474.1 301.0 all-gather.19
  1777.3 117.2 all-gather.17
  1896.6 57.7 all-gather.21
  2094.3 83.7 all-reduce.14
  2180.9 51.4 all-reduce.12
  2236.5 72.9 reduce-scatter.18
  2313.0 72.1 reduce-scatter.20
  2388.7 72.1 reduce-scatter.22
  2464.4 103.9 all-reduce.16
  2571.9 54.9 reduce-scatter.16
  2630.1 63.2 reduce-scatter.12
  2696.8 68.1 reduce-scatter.14
  2768.5 73.3 reduce-scatter.8
  2845.4 69.1 reduce-scatter.10
where the time goes:
time: 2930 us; the launch traced here: 2920 us
  waiting for transfers between devices  2160 us (74%)
  local copies, waits for them, and re-layouts  249 us (8%)
  matrix products  230 us (8%)
  other arithmetic  127 us (4%)
  blocking collectives  120 us (4%)
    all_to_all x1, waiting for transfers between devices, body(): lax.all_to_all(grad_send, 'dp', split_axis=0, concat_axis=0, tiled=True)  316 us
    all_to_all x1, waiting for transfers between devices, body(): lax.all_to_all(expert_out, 'dp', split_axis=0, concat_axis=0, tiled=True)  301 us
    all_gather x1, waiting for transfers between devices, body(): lax.all_gather(w_shared_up, 'dp', axis=0, tiled=True)  296 us
    all_to_all x1, waiting for transfers between devices, body(): lax.all_to_all(send_rows, 'dp', split_axis=0, concat_axis=0, tiled=True)  283 us
    all_gather x1, waiting for transfers between devices, body(): lax.all_gather(w_shared_gate, 'dp', axis=0, tiled=True)  115 us
    psum x1, waiting for transfers between devices, body(): lax.psum((attn_in_part, latent_part_grad, rope_part_grad), 'tensor')  90.5 us
    reduce_scatter x1, waiting for transfers between devices, body(): lax.psum_scatter(query_weight_grad.astype(jnp.bfloat16), 'dp', scatter_di...  75 us
    reduce_scatter x1, waiting for transfers between devices, body(): lax.psum_scatter(shared_down_grad.astype(jnp.bfloat16), 'dp', scatter_dim...  73.8 us
  transfers between devices with their start and end apart: 23, of which 22 were waited for; matrix products, arithmetic and copies ran while one was open for 14% of the time, Pallas kernels for 0%

commit v1 on v0

--- a/solution.py
+++ b/solution.py
@@ -440,10 +440,516 @@
         w_down_grad,
     )
 
+def hop(values, axis, bit):
+    return lax.ppermute(values, axis, [(i, i ^ bit) for i in range(lax.axis_size(axis))])
+
+
+def core_hop(values):
+    return hop(values, "tensor", 1)
+
+
+def y_hop(values):
+    return hop(values, "tensor", 2)
+
+
+def x_hop(values):
+    return hop(values, "dp", 1)
+
+
+def z_hop(values):
+    count = lax.axis_size("dp")
+    return lax.ppermute(values, "dp", [(i, (i + 2) % count) for i in range(count)])
+
+
+def low(values):
+    return values.astype(jnp.bfloat16)
+
+
+def plane_gather(own):
+    half = own.shape[0] // 2
+    first, second = own[:half], own[half:]
+    first_x = x_hop(first)
+    second_y = y_hop(second)
+    first_pair = jnp.concatenate([first, first_x])
+    second_pair = jnp.concatenate([second, second_y])
+    first_y = y_hop(first_pair)
+    second_x = x_hop(second_pair)
+    parts = [
+        first,
+        second,
+        first_x,
+        second_x[:half],
+        first_y[:half],
+        second_y,
+        first_y[half:],
+        second_x[half:],
+    ]
+    quarter = jnp.concatenate(parts)
+    return quarter, core_hop(quarter)
+
+
+def slice_gather(own):
+    chunks = []
+    piece = own
+    planes = lax.axis_size("dp") // 2
+    for step in range(planes):
+        chunks.append(plane_gather(piece))
+        if step + 1 < planes:
+            piece = z_hop(piece)
+    return chunks
+
+
+def plane_scatter(part):
+    received = core_hop(part[1])
+    total = part[0].astype(jnp.float32) + received.astype(jnp.float32)
+    first, second = total[:, :, 0], total[:, :, 1]
+    first_in = y_hop(low(first[1])).astype(jnp.float32)
+    second_in = x_hop(low(second[:, 1])).astype(jnp.float32)
+    first_near = first[0] + first_in
+    second_near = second[:, 0] + second_in
+    first_in = x_hop(low(first_near[1])).astype(jnp.float32)
+    second_in = y_hop(low(second_near[1])).astype(jnp.float32)
+    return jnp.concatenate([first_near[0] + first_in, second_near[0] + second_in])
+
+
+def slice_scatter(parts):
+    own = parts[0].shape[0] // 8
+    width = parts[0].shape[1]
+    pieces = [plane_scatter(part.reshape(2, 2, 2, 2, own // 2, width)) for part in parts]
+    moving = pieces[1]
+    for piece in pieces[2:] + pieces[:1]:
+        moving = piece + z_hop(low(moving)).astype(jnp.float32)
+    return moving
+
+
+def tensor_scatter(values, tensor_index):
+    rows = values.shape[0] // 4
+    width = values.shape[1]
+    core = tensor_index % 2
+    level = tensor_index // 2
+    blocks = values.reshape(2, 2, rows, width)
+    mine = lax.dynamic_index_in_dim(blocks, core, 1, keepdims=False)
+    other = lax.dynamic_index_in_dim(blocks, 1 - core, 1, keepdims=False)
+    total = mine.astype(jnp.float32) + core_hop(low(other)).astype(jnp.float32)
+    near = lax.dynamic_index_in_dim(total, level, 0, keepdims=False)
+    far = lax.dynamic_index_in_dim(total, 1 - level, 0, keepdims=False)
+    return near + y_hop(low(far)).astype(jnp.float32)
+
+
+def tensor_gather(own, tensor_index):
+    own_y = y_hop(own)
+    pair = jnp.stack([own, own_y])
+    pair_core = core_hop(pair)
+    core = tensor_index % 2
+    level = tensor_index // 2
+    even = jnp.where(core == 0, pair, pair_core)
+    odd = jnp.where(core == 0, pair_core, pair)
+    near = jnp.concatenate([even[0], odd[0]])
+    far = jnp.concatenate([even[1], odd[1]])
+    return jnp.concatenate(
+        [jnp.where(level == 0, near, far), jnp.where(level == 0, far, near)]
+    )
+
+
+def padded(values, axis, size):
+    pads = [(0, 0)] * values.ndim
+    pads[axis] = (0, size - values.shape[axis])
+    return jnp.pad(values, pads)
+
+
+def lanes(size):
+    return -(-size // 128) * 128
+
+
+def body_dense(
+    tokens,
+    cotangent,
+    routes,
+    seq_ids,
+    positions,
+    gain_attn,
+    w_query,
+    w_latent,
+    gain_latent,
+    w_expand,
+    w_output,
+    gain_ffn,
+    w_router,
+    w_shared_gate,
+    w_shared_up,
+    w_shared_down,
+    w_gate,
+    w_up,
+    w_down,
+):
+    tensor_size = lax.axis_size("tensor")
+    dp_size = lax.axis_size("dp")
+    dp_index = lax.axis_index("dp")
+    tensor_index = lax.axis_index("tensor")
+    tok_count, width = tokens.shape
+    own_count = tok_count // tensor_size
+    own_start = tensor_index * own_count
+    experts = w_router.shape[1]
+    exp_here = w_gate.shape[0]
+    capacity = tensor_size * -(-(5 * tok_count * TOP) // (4 * experts * tensor_size))
+
+    def own_rows(values):
+        return lax.dynamic_slice_in_dim(values, own_start, own_count, 0)
+
+    lat_width = w_latent.shape[1]
+    lat_rows = w_latent.shape[0] // tensor_size
+    lat_piece = lax.dynamic_slice_in_dim(w_latent, tensor_index * lat_rows, lat_rows, 0)
+    gains = jnp.concatenate([gain_attn, gain_ffn, gain_latent])[None]
+    gain_rows = gain_attn.shape[0]
+    router_piece = lax.dynamic_slice_in_dim(
+        w_router, tensor_index * lat_rows, lat_rows, 0
+    ).reshape(2, lat_rows * experts // 2)
+    pack = jnp.concatenate([lat_piece, gains, padded(router_piece, 1, lat_width)])
+    pack_rows = -(-pack.shape[0] // 8) * 8
+    packed = lax.all_gather(padded(pack, 0, pack_rows), ("dp", "tensor"), axis=0, tiled=False)
+    latent_weight = packed[:, :lat_rows].reshape(width, lat_width)
+    gains_all = packed[::tensor_size, lat_rows].astype(jnp.float32)
+    gain_attn_f = gains_all[:, :gain_rows].reshape(width)
+    gain_ffn_f = gains_all[:, gain_rows : 2 * gain_rows].reshape(width)
+    gain_latent_f = gains_all[:, 2 * gain_rows :].reshape(KV_RANK)
+    router_weight = packed[:, lat_rows + 1 : lat_rows + 3, : router_piece.shape[1]].reshape(
+        width, experts
+    )
+
+    query_weight = lax.all_gather(w_query, "dp", axis=0, tiled=True)
+    expand_weight = lax.all_gather(w_expand, "dp", axis=0, tiled=True)
+    output_weight = lax.all_gather(w_output, "dp", axis=1, tiled=True)
+
+    routed = jnp.sum(
+        (routes[:, :, None] == jnp.arange(experts, dtype=jnp.int32)[None, None, :]).astype(
+            jnp.float32
+        ),
+        axis=1,
+    )
+    order = jnp.arange(tok_count, dtype=jnp.int32)
+    earlier = (order[None, :] < order[:, None]).astype(jnp.bfloat16)
+    rank = jnp.dot(earlier, low(routed), preferred_element_type=jnp.float32)
+    standing = routed * (1.0 + (rank < capacity).astype(jnp.float32))
+    cot_own = own_rows(cotangent)
+    standing_own = own_rows(standing)
+    cot_sent = jnp.concatenate([cot_own, padded(low(standing_own), 1, 128)], axis=1)
+    cot_chunks = slice_gather(cot_sent)
+
+    shared_here = w_shared_gate.shape[1] // dp_size
+    shared_in = lax.all_to_all(
+        jnp.stack([w_shared_gate, w_shared_up]), "dp", split_axis=2, concat_axis=1, tiled=True
+    )
+    shared_out = lax.all_to_all(w_shared_down, "dp", split_axis=0, concat_axis=1, tiled=True)
+    group = w_gate.shape[2]
+    group_lanes = lanes(group)
+    shared_lanes = lanes(shared_here)
+
+    def joined(routed_weight, shared_weight, axis):
+        pieces = [padded(routed_weight[e], axis, group_lanes) for e in range(exp_here)]
+        return jnp.concatenate(pieces + [padded(shared_weight, axis, shared_lanes)], axis=axis)
+
+    gate_weight = joined(w_gate, shared_in[0], 1)
+    up_weight = joined(w_up, shared_in[1], 1)
+    down_weight = joined(w_down, shared_out, 0)
+    hidden = gate_weight.shape[1]
+
+    head_width = QK_NOPE + QK_ROPE
+    heads_here = query_weight.shape[1] // head_width
+    softmax_scale = head_width ** (-0.5)
+    resid_in = tokens.astype(jnp.float32)
+    normed_attn, inverse_attn = norm_forward(resid_in, gain_attn_f)
+    normed_attn_low = low(normed_attn)
+    cosine, sine_part = rope_tables(positions, QK_ROPE)
+    query_raw = jnp.dot(normed_attn_low, query_weight, preferred_element_type=jnp.float32).reshape(
+        tok_count, heads_here, head_width
+    )
+    query_low = low(
+        jnp.concatenate(
+            [
+                query_raw[..., :QK_NOPE],
+                rotate(query_raw[..., QK_NOPE:], cosine[:, None, :], sine_part[:, None, :]),
+            ],
+            axis=-1,
+        )
+    )
+    latent_raw = jnp.dot(normed_attn_low, latent_weight, preferred_element_type=jnp.float32)
+    latent_part = latent_raw[:, :KV_RANK]
+    latent_normed, inverse_latent = norm_forward(latent_part, gain_latent_f)
+    latent_low = low(latent_normed)
+    key_rope_low = low(rotate(latent_raw[:, KV_RANK:], cosine, sine_part))
+    expanded = low(
+        jnp.dot(latent_low, expand_weight, preferred_element_type=jnp.float32)
+    ).reshape(tok_count, heads_here, QK_NOPE + V_HEAD)
+    value_low = expanded[..., QK_NOPE:]
+    key_full = jnp.concatenate(
+        [
+            expanded[..., :QK_NOPE],
+            jnp.broadcast_to(key_rope_low[:, None, :], (tok_count, heads_here, QK_ROPE)),
+        ],
+        axis=-1,
+    )
+    masked = block_scores(query_low, key_full, seq_ids, 0)
+    row_max = jnp.max(masked, axis=-1, keepdims=True)
+    exponent = jnp.exp(masked - row_max)
+    exp_total = jnp.sum(exponent, axis=-1, keepdims=True)
+    probs_low = low(exponent / exp_total)
+    log_total = row_max + jnp.log(exp_total)
+    heads_low = low(
+        jnp.einsum("hqk,khc->qhc", probs_low, value_low, preferred_element_type=jnp.float32)
+    ).reshape(tok_count, heads_here * V_HEAD)
+    attn_part = jnp.dot(heads_low, output_weight, preferred_element_type=jnp.float32)
+
+    resid_own = own_rows(tokens).astype(jnp.float32) + tensor_scatter(attn_part, tensor_index)
+    normed_own, inverse_own = norm_forward(resid_own, gain_ffn_f)
+    normed_own_low = low(normed_own)
+    row_chunks = slice_gather(normed_own_low)
+
+    def gating(rows, standing_rows):
+        probs = jax.nn.softmax(
+            jnp.dot(rows, router_weight, preferred_element_type=jnp.float32), axis=-1
+        )
+        gates = jnp.where(standing_rows > 0.5, probs, 0.0)
+        picked = jnp.sum(gates, axis=-1, keepdims=True)
+        return probs, gates / picked, picked
+
+    expert_index = jnp.arange(experts, dtype=jnp.int32)[None, :]
+    column = jnp.arange(hidden, dtype=jnp.int32)[None, :]
+    out_parts, in_parts, gate_parts = [], [], []
+    gate_weight_grad = up_weight_grad = down_weight_grad = 0.0
+    for (near_rows, far_rows), (near_cot, far_cot) in zip(row_chunks, cot_chunks):
+        rows = jnp.concatenate([near_rows, far_rows])
+        cots = jnp.concatenate([near_cot[:, :width], far_cot[:, :width]])
+        marks = jnp.concatenate(
+            [near_cot[:, width : width + experts], far_cot[:, width : width + experts]]
+        ).astype(jnp.float32)
+        _, chunk_gates, _ = gating(rows, marks)
+        chunk_gates = jnp.where(marks > 1.5, chunk_gates, 0.0)
+        scale = jnp.ones((rows.shape[0], hidden), jnp.float32)
+        for e in reversed(range(exp_here)):
+            here = expert_index == dp_index * exp_here + e
+            gate_column = jnp.sum(jnp.where(here, chunk_gates, 0.0), axis=-1, keepdims=True)
+            scale = jnp.where(column < (e + 1) * group_lanes, gate_column, scale)
+        gate_pre = jnp.dot(rows, gate_weight, preferred_element_type=jnp.float32)
+        up_pre = jnp.dot(rows, up_weight, preferred_element_type=jnp.float32)
+        sigmoid = jax.nn.sigmoid(gate_pre)
+        silu = gate_pre * sigmoid
+        act = silu * up_pre
+        act_scaled = low(act * scale)
+        out_parts.append(
+            low(jnp.dot(act_scaled, down_weight, preferred_element_type=jnp.float32))
+        )
+        act_grad = jnp.einsum("td,fd->tf", cots, down_weight, preferred_element_type=jnp.float32)
+        meeting = act * act_grad
+        gate_parts.append(
+            jnp.stack(
+                [
+                    jnp.sum(meeting[:, e * group_lanes : (e + 1) * group_lanes], axis=-1)
+                    for e in range(exp_here)
+                ]
+            )
+        )
+        scaled_grad = act_grad * scale
+        gate_grad = low(scaled_grad * up_pre * sigmoid * (1.0 + gate_pre * (1.0 - sigmoid)))
+        up_grad = low(scaled_grad * silu)
+        in_parts.append(
+            low(
+                jnp.einsum("tf,df->td", gate_grad, gate_weight, preferred_element_type=jnp.float32)
+                + jnp.einsum("tf,df->td", up_grad, up_weight, preferred_element_type=jnp.float32)
+            )
+        )
+        gate_weight_grad += jnp.einsum(
+            "td,tf->df", rows, gate_grad, preferred_element_type=jnp.float32
+        )
+        up_weight_grad += jnp.einsum("td,tf->df", rows, up_grad, preferred_element_type=jnp.float32)
+        down_weight_grad += jnp.einsum(
+            "tf,td->fd", act_scaled, cots, preferred_element_type=jnp.float32
+        )
+
+    ffn_sum = slice_scatter(in_parts)
+    gate_sums = jnp.stack(gate_parts).reshape(-1, exp_here, 2, 2, 2, own_count)
+    gate_sums = gate_sums[:, :, 0] + core_hop(gate_sums[:, :, 1])
+    gate_sums = gate_sums[:, :, 0] + y_hop(gate_sums[:, :, 1])
+    planes = dp_size // 2
+    block = jnp.arange(dp_size, dtype=jnp.int32)
+    place = ((dp_index // 2 - block // 2) % planes) * 2 + (block + dp_index) % 2
+    gate_sums = gate_sums.transpose(0, 2, 1, 3).reshape(dp_size, exp_here, own_count)[place]
+    gate_sums = lax.all_to_all(gate_sums, "dp", split_axis=0, concat_axis=0, tiled=True)
+    gate_sums = gate_sums.reshape(experts, own_count).T
+
+    probs_own, gates_own, picked_own = gating(normed_own_low, standing_own)
+    gate_sums = jnp.where(standing_own > 1.5, gate_sums, 0.0)
+    picked_grad = (
+        gate_sums - jnp.sum(gate_sums * gates_own, axis=-1, keepdims=True)
+    ) / picked_own
+    probs_grad = jnp.where(standing_own > 0.5, picked_grad, 0.0)
+    logit_grad = low(
+        probs_own * (probs_grad - jnp.sum(probs_own * probs_grad, axis=-1, keepdims=True))
+    )
+    router_grad = jnp.einsum(
+        "td,te->de", normed_own_low, logit_grad, preferred_element_type=jnp.float32
+    )
+    ffn_in = ffn_sum + jnp.einsum(
+        "te,de->td", logit_grad, router_weight, preferred_element_type=jnp.float32
+    )
+    ffn_resid_grad, gain_ffn_grad = norm_backward(resid_own, inverse_own, gain_ffn_f, ffn_in)
+    mid_grad_own = cot_own.astype(jnp.float32) + ffn_resid_grad
+    mid_low = tensor_gather(low(mid_grad_own), tensor_index)
+
+    output_weight_grad = jnp.einsum(
+        "th,td->hd", heads_low, mid_low, preferred_element_type=jnp.float32
+    )
+    heads_grad = low(
+        jnp.einsum("td,hd->th", mid_low, output_weight, preferred_element_type=jnp.float32)
+    ).reshape(tok_count, heads_here, V_HEAD)
+    masked = block_scores(query_low, key_full, seq_ids, 0)
+    attn_probs = jnp.exp(masked - log_total)
+    prob_grad = jnp.einsum("qhc,khc->hqk", heads_grad, value_low, preferred_element_type=jnp.float32)
+    row_dot = jnp.sum(attn_probs * prob_grad, axis=-1, keepdims=True)
+    score_grad = low(attn_probs * (prob_grad - row_dot))
+    query_grad = (
+        jnp.einsum("hqk,khc->qhc", score_grad, key_full, preferred_element_type=jnp.float32)
+        * softmax_scale
+    )
+    key_grad = (
+        jnp.einsum("hqk,qhc->khc", score_grad, query_low, preferred_element_type=jnp.float32)
+        * softmax_scale
+    )
+    value_grad = jnp.einsum(
+        "hqk,qhc->khc", low(attn_probs), heads_grad, preferred_element_type=jnp.float32
+    )
+    query_pre_grad = low(
+        jnp.concatenate(
+            [
+                query_grad[..., :QK_NOPE],
+                rotate(query_grad[..., QK_NOPE:], cosine[:, None, :], -sine_part[:, None, :]),
+            ],
+            axis=-1,
+        )
+    ).reshape(tok_count, heads_here * head_width)
+    query_weight_grad = jnp.einsum(
+        "td,tq->dq", normed_attn_low, query_pre_grad, preferred_element_type=jnp.float32
+    )
+    expand_grad = low(jnp.concatenate([key_grad[..., :QK_NOPE], value_grad], axis=-1)).reshape(
+        tok_count, heads_here * (QK_NOPE + V_HEAD)
+    )
+    latent_grad = jnp.einsum(
+        "te,re->tr", expand_grad, expand_weight, preferred_element_type=jnp.float32
+    )
+    expand_weight_grad = jnp.einsum(
+        "tr,te->re", latent_low, expand_grad, preferred_element_type=jnp.float32
+    )
+    rope_grad = jnp.sum(key_grad[..., QK_NOPE:], axis=1)
+    latent_pre_grad, gain_latent_grad = norm_backward(
+        latent_part, inverse_latent, gain_latent_f, latent_grad
+    )
+    latent_all_grad = low(
+        jnp.concatenate([latent_pre_grad, rotate(rope_grad, cosine, -sine_part)], axis=-1)
+    )
+    attn_in = jnp.einsum(
+        "tq,dq->td", query_pre_grad, query_weight, preferred_element_type=jnp.float32
+    ) + jnp.einsum("tc,dc->td", latent_all_grad, latent_weight, preferred_element_type=jnp.float32)
+    latent_weight_grad = jnp.einsum(
+        "td,tc->dc", normed_attn_low, latent_all_grad, preferred_element_type=jnp.float32
+    )
+    gain_attn_grad = jnp.sum(attn_in * (resid_in * inverse_attn), axis=0)
+    attn_in_own = tensor_scatter(attn_in, tensor_index)
+    input_grad, _ = norm_backward(
+        own_rows(resid_in), own_rows(inverse_attn), gain_attn_f, attn_in_own
+    )
+    tokens_grad = tensor_gather(low(mid_grad_own + input_grad), tensor_index)
+
+    out_sum = slice_scatter(out_parts)
+    result = tensor_gather(low(resid_own + out_sum), tensor_index)
+
+    def scattered(values, dimension):
+        return lax.psum_scatter(
+            low(values), "dp", scatter_dimension=dimension, tiled=True
+        ).astype(jnp.float32)
+
+    output_share = scattered(output_weight_grad, 1)
+    query_share = scattered(query_weight_grad, 0)
+    expand_share = scattered(expand_weight_grad, 0)
+
+    gain_shares = jnp.concatenate(
+        [
+            gain_attn_grad.reshape(dp_size, -1),
+            gain_ffn_grad.reshape(dp_size, -1),
+            gain_latent_grad.reshape(dp_size, -1),
+        ],
+        axis=1,
+    )[:, None]
+    router_lanes = 512
+    router_rows = router_grad.reshape(dp_size, -1, router_lanes)
+    lat_block = w_latent.shape[0]
+    grad_pack = jnp.concatenate(
+        [
+            low(latent_weight_grad).reshape(dp_size, lat_block, lat_width),
+            low(gain_shares),
+            padded(low(router_rows), 2, lat_width),
+        ],
+        axis=1,
+    )
+    unit = 8 * tensor_size
+    grad_rows = -(-grad_pack.shape[1] // unit) * unit
+    grad_pack = padded(grad_pack, 1, grad_rows).reshape(dp_size * grad_rows, lat_width)
+    grad_piece = lax.psum_scatter(grad_pack, ("dp", "tensor"), scatter_dimension=0, tiled=True)
+    grad_full = tensor_gather(grad_piece, tensor_index).astype(jnp.float32)
+    latent_share = grad_full[:lat_block]
+    gain_row = grad_full[lat_block]
+    gain_attn_share = gain_row[:gain_rows]
+    gain_ffn_share = gain_row[gain_rows : 2 * gain_rows]
+    gain_latent_share = gain_row[2 * gain_rows :]
+    router_share = grad_full[
+        lat_block + 1 : lat_block + 1 + router_rows.shape[1], :router_lanes
+    ].reshape(lat_block, experts)
+
+    def routed_grad(grad, axis):
+        return jnp.stack(
+            [
+                lax.slice_in_dim(grad, e * group_lanes, e * group_lanes + group, axis=axis)
+                for e in range(exp_here)
+            ]
+        )
+
+    def shared_grad(grad, axis):
+        start = exp_here * group_lanes
+        return low(lax.slice_in_dim(grad, start, start + shared_here, axis=axis))
+
+    shared_in_grad = lax.all_to_all(
+        jnp.stack([shared_grad(gate_weight_grad, 1), shared_grad(up_weight_grad, 1)]),
+        "dp",
+        split_axis=1,
+        concat_axis=2,
+        tiled=True,
+    ).astype(jnp.float32)
+    shared_down_share = lax.all_to_all(
+        shared_grad(down_weight_grad, 0), "dp", split_axis=1, concat_axis=0, tiled=True
+    ).astype(jnp.float32)
+
+    return (
+        result,
+        tokens_grad,
+        gain_attn_share,
+        query_share,
+        latent_share,
+        gain_latent_share,
+        expand_share,
+        output_share,
+        gain_ffn_share,
+        router_share,
+        shared_in_grad[0],
+        shared_in_grad[1],
+        shared_down_share,
+        routed_grad(gate_weight_grad, 1),
+        routed_grad(up_weight_grad, 1),
+        routed_grad(down_weight_grad, 0),
+    )
+
 
 def solution(mesh):
+    dense = mesh.shape["dp"] == 8 and mesh.shape["tensor"] == 4
     return jax.shard_map(
-        body,
+        body_dense if dense else body,
         mesh=mesh,
         in_specs=(
             P("dp", None),

time: 2930 us -> 1460 us (0.50)
  waiting for transfers between devices: 2160 us -> 592 us
  blocking collectives: 120 us -> 0 us
  matrix products: 230 us -> 349 us
  starting transfers between devices: 24 us -> 112 us
    all_to_all x4 -> x5, waiting for transfers between devices: 900 us -> 4.66 us  [the longest x1 4.64 us: body_dense(): lax.all_to_all(jnp.stack([shared_grad(gate_weight_grad, 1), shared_grad(u...]
    all_gather x7 -> x4, waiting for transfers between devices: 603 us -> 169 us  [the longest x1 52.8 us: body_dense(): query_weight = lax.all_gather(w_query, 'dp', axis=0, tiled=True)]
    reduce_scatter x8 -> x3, waiting for transfers between devices: 453 us -> 137 us  [scattered(): lax.psum_scatter(low(values), 'dp', scatter_dimension=dimension, tiled=True)]
    ppermute x0 -> x106, waiting for transfers between devices: none -> 230 us  [the longest x94 164 us: hop(): lax.ppermute(values, axis, [(i, i ^ bit) for i in range(lax.axis_size(axi...]
    psum x4 -> x0, waiting for transfers between devices: 194 us -> none  [the longest x1 90.5 us: body(): lax.psum((attn_in_part, latent_part_grad, rope_part_grad), 'tensor')]
    gather x4 -> x1, local copies, waits for them, and re-layouts: 126 us -> 1.29 us  [body_dense(): gate_sums.transpose(0, 2, 1, 3).reshape(dp_size, exp_here, own_count)[place]]
    dot_general x38 -> x61, matrix products: 229 us -> 348 us  [the longest x4 50.9 us: body_dense(): gate_pre = jnp.dot(rows, gate_weight, preferred_element_type=jnp.float32)]
    ppermute x0 -> x106, starting transfers between devices: none -> 85.5 us  [the longest x94 76.3 us: hop(): lax.ppermute(values, axis, [(i, i ^ bit) for i in range(lax.axis_size(axi...]
  transfers between devices with their start and end apart: 23 -> 119, of which waited for: 22 -> 50; matrix products, arithmetic and copies ran while one was open for 14% -> 32% of each run, Pallas kernels for 0% -> 0%
where the time goes in v1:
time: 1460 us; the launch traced here: 1440 us
  waiting for transfers between devices  592 us (41%)
  matrix products  349 us (24%)
  local copies, waits for them, and re-layouts  253 us (17%)
  other arithmetic  120 us (8%)
  starting transfers between devices  112 us (8%)
  between operations  18.2 us (1%)
    ppermute x94, waiting for transfers between devices, hop(): lax.ppermute(values, axis, [(i, i ^ bit) for i in range(lax.axis_size(axi...  164 us
    reduce_scatter x3, waiting for transfers between devices, scattered(): lax.psum_scatter(low(values), 'dp', scatter_dimension=dimension, tiled=True)  137 us
    unnamed x509, local copies, waits for them, and re-layouts  81.7 us
    ppermute x94, starting transfers between devices, hop(): lax.ppermute(values, axis, [(i, i ^ bit) for i in range(lax.axis_size(axi...  76.3 us
    ppermute x12, waiting for transfers between devices, z_hop(): lax.ppermute(values, 'dp', [(i, (i + 2) % count) for i in range(count)])  66.3 us
    all_gather x1, waiting for transfers between devices, body_dense(): query_weight = lax.all_gather(w_query, 'dp', axis=0, tiled=True)  52.8 us
    unnamed x9, waiting for transfers between devices  50.9 us
    dot_general x4, matrix products, body_dense(): gate_pre = jnp.dot(rows, gate_weight, preferred_element_type=jnp.float32)  50.9 us
  transfers between devices with their start and end apart: 119, of which 50 were waited for; matrix products, arithmetic and copies ran while one was open for 32% of the time, Pallas kernels for 0%

profile of v1, /device:TPU:0, one launch (start us, length us, event | category | flops | bytes accessed | tf_op | source)
XLA Modules:
  0.0 1444.4 jit_solution(16823861527830257802)
XLA Ops:
  11.6 7.3 all-to-all-start.1
  32.4 41.2 %all-gather.12.cloned.1.call-done = bf16[2304,576]{1,0:T(8,128)(2,1)} async-done(((bf16[72,576]{1,0:T(8,128)(2,1)}), bf16[2304,576]{1,0:T(8,128)(2,1)}) %all-gather.12.cloned.1.call-update) | async-done | bytes 2654224 | tf_op jit(solution)/shard_map/all_gather | solution.py:609
  82.5 32.3 %all-gather.6.cloned.1.call-done = bf16[512,1024]{1,0:T(8,128)(2,1)} async-done(((bf16[64,1024]{1,0:T(8,128)(2,1)}), bf16[512,1024]{1,0:T(8,128)(2,1)}) %all-gather.6.cloned.1.call-update) | async-done | bytes 1048592 | tf_op jit(solution)/shard_map/all_gather | solution.py:620
  122.9 52.8 %all-gather.8.cloned.1.call-done = bf16[2048,768]{1,0:T(8,128)(2,1)} async-done(((bf16[256,768]{1,0:T(8,128)(2,1)}), bf16[2048,768]{1,0:T(8,128)(2,1)}) %all-gather.8.cloned.1.call-update) | async-done | bytes 3145744 | tf_op jit(solution)/shard_map/all_gather | solution.py:619
  193.2 43.0 %all-gather.10.cloned.1.call-done = bf16[512,2048]{1,0:T(8,128)(2,1)} async-done(((bf16[512,256]{1,0:T(8,128)(2,1)}), bf16[512,2048]{1,0:T(8,128)(2,1)}) %all-gather.10.cloned.1.call-update) | async-done | bytes 2097168 | tf_op jit(solution)/shard_map/all_gather | solution.py:621
  264.2 9.1 collective-permute-done.1
  313.9 9.3 collective-permute-done.54
  402.2 10.2 collective-permute-done.41
  459.6 13.6 collective-permute-done.31
  479.2 8.3 fusion.233
  498.4 7.4 fusion.36
  509.8 8.3 fusion.237
  518.1 8.1 fusion.236
  543.4 8.1 fusion.235
  572.2 8.6 fusion.234
  582.1 12.8 multiply_convert_fusion.5
  594.9 6.9 fusion.240
  601.8 8.2 fusion.246
  618.5 24.2 %multiply_convert_fusion.7 = (bf16[1024,896]{0,1:T(8,128)(2,1)S(1)}, f32[1024,896]{0,1:T(8,128)}, bf16[1024,896]{0,1:T(8,128)(2,1)}, bf16[1024,896]{0,1:T(8,128)...) fusion(f32[1024,896]{0,1:T(8,128)} %fusion.234, ...), kind=kOutput, calls=%fused_computation.69 | convolution fusion | flops 3813146624 | bytes 64775936 | tf_op jit(solution)/shard_map/dot_general | solution.py:732
  642.7 9.1 fusion.238
  657.9 6.9 fusion.241
  664.8 8.4 fusion.245
  673.2 6.4 convolution_convert_fusion.1
  710.5 7.5 fusion.239
  718.0 13.2 add_add_fusion.2
  733.4 8.2 fusion.249
  747.7 8.4 fusion.248
  756.1 10.8 add_add_fusion.1
  778.6 13.1 add_add_fusion
  802.2 7.8 add_convert_fusion.2
  823.0 7.4 add_convert_fusion
  939.8 8.1 collective-permute-done.86
  962.4 8.0 collective-permute-done.76
  974.8 6.8 collective-permute-done.36
  986.0 6.7 collective-permute-done.51
  996.0 7.9 collective-permute-done.66
  1008.7 6.5 collective-permute-done.15
  1017.1 16.0 %collective-permute-done.92 = bf16[64,2048]{1,0:T(8,128)(2,1)S(1)} collective-permute-done((bf16[64,2048]{1,0:T(8,128)(2,1)S(1)}, bf16[64,2048]{1,0:T(8,128)(2,1)S(1)}, u32[]{:S(2)}, u32[]{:S(2)}) %collective-permute-start.92) | collective-permute-done | bytes 262176 | tf_op jit(solution)/shard_map/ppermute | solution.py:444
  1033.5 6.9 collective-permute-done.90
  1047.9 7.2 collective-permute-done.93
  1057.6 11.3 collective-permute-done.94
  1071.4 10.5 collective-permute-done.95
  1086.6 6.8 collective-permute-done.98
  1163.6 14.8 %collective-permute-done.69 = bf16[128,2048]{1,0:T(8,128)(2,1)S(1)} collective-permute-done((bf16[128,2048]{1,0:T(8,128)(2,1)S(1)}, bf16[128,2048]{1,0:T(8,128)(2,1)S(1)}, u32[]{:S(2)}, u32[]{:S(2)}) %collective-permute-start.69) | collective-permute-done | bytes 524320 | tf_op jit(solution)/shard_map/ppermute | solution.py:461
  1179.9 10.4 collective-permute-done.70
  1237.5 48.9 %reduce-scatter.13.cloned.1.call-done = bf16[72,576]{1,0:T(8,128)(2,1)} async-done(((bf16[2304,576]{1,0:T(8,128)(2,1)}), bf16[72,576]{1,0:T(8,128)(2,1)}) %reduce-scatter.13.cloned.1.call-update) | async-done | bytes 82960
  1296.1 62.2 %reduce-scatter.11.cloned.1.call-done = bf16[512,256]{1,0:T(8,128)(2,1)} async-done(((bf16[512,2048]{1,0:T(8,128)(2,1)}), bf16[512,256]{1,0:T(8,128)(2,1)}) %reduce-scatter.11.cloned.1.call-update) | async-done | bytes 262160 | tf_op jit(solution)/shard_map/reduce_scatter | solution.py:865
  1360.1 75.2 %reduce-scatter.7.cloned.1.call-done = bf16[256,768]{1,0:T(8,128)(2,1)} async-done(((bf16[2048,768]{1,0:T(8,128)(2,1)}), bf16[256,768]{1,0:T(8,128)(2,1)}) %reduce-scatter.7.cloned.1.call-update) | async-done | bytes 393232 | tf_op jit(solution)/shard_map/reduce_scatter | solution.py:865
  (1095 shorter events, 685.2 us)
Async XLA Ops:
  7.3 66.3 %all-gather.12.cloned.1.call-start = ((), (), s32[]{:S(2)}) async-start(), calls=%async_computation.15 | async-start | bytes 3041280 | tf_op jit(solution)/shard_map/all_gather | solution.py:609
  10.1 104.7 %all-gather.6.cloned.1.call-start = ((), (), s32[]{:S(2)}) async-start(), calls=%async_computation.9 | async-start | bytes 1179648 | tf_op jit(solution)/shard_map/all_gather | solution.py:620
  10.9 164.9 %all-gather.8.cloned.1.call-start = ((), (), s32[]{:S(2)}) async-start(), calls=%async_computation.10 | async-start | bytes 3538944 | tf_op jit(solution)/shard_map/all_gather | solution.py:619
  11.6 171.9 %all-to-all-start.1 = ((bf16[8,88,256]{2,1,0:T(8,128)(2,1)}), bf16[8,88,256]{2,1,0:T(8,128)(2,1)}, u32[]{:S(2)}, u32[]{:S(2)}) async-start(bf16[8,88,256]{2,1,0:T(8,128)(2,1)} %bitcast.597), calls=%async_computation.1 | async-start | bytes 720896 | tf_op jit(solution)/shard_map/all_to_all | solution.py:642
  18.9 217.4 %all-gather.10.cloned.1.call-start = ((), (), s32[]{:S(2)}) async-start(), calls=%async_computation.11 | async-start | bytes 2359296 | tf_op jit(solution)/shard_map/all_gather | solution.py:621
  183.5 64.2 %all-to-all-start = ((bf16[2,256,704]{1,0,2:T(2,128)(2,1)}), bf16[2,256,704]{1,0,2:T(2,128)(2,1)}, u32[]{:S(2)}, u32[]{:S(2)}) async-start(bf16[2,256,704]{1,0,2:T(2,128)(2,1)} %copy.319), calls=%async_computation | async-start | bytes 1441792 | tf_op jit(solution)/shard_map/all_to_all | solution.py:639
  278.1 26.1 %collective-permute-start.25 = (bf16[128,2176]{1,0:T(8,128)(2,1)S(1)}, bf16[128,2176]{1,0:T(8,128)(2,1)}, u32[]{:S(2)}, u32[]{:S(2)}) collective-permute-start(bf16[128,2176]{1,0:T(8,128)(2,1)S(1)} %get-tuple-element.217), channel_id=1, source_target_pairs={{0,8},{4,12},{8,16},{12,20},{16,24},{20,28},{24,0},{28,4},{1,9},{5... | collective-permute-start | bytes 1671176 | tf_op jit(solution)/shard_map/ppermute | solution.py:461
  297.0 34.4 %collective-permute-start.9 = (bf16[128,2176]{1,0:T(8,128)(2,1)S(1)}, bf16[128,2176]{1,0:T(8,128)(2,1)S(1)}, u32[]{:S(2)}, u32[]{:S(2)}) collective-permute-start(bf16[128,2176]{1,0:T(8,128)(2,1)S(1)} %pad_maximum_fusion.42), channel_id=1, source_target_pairs={{0,4},{4,0},{8,12},{12,8},{16,20},{20,16},{24,28},{28,24},{1,5},{5... | collective-permute-start | bytes 1671176 | tf_op jit(solution)/shard_map/ppermute | solution.py:444
  297.6 34.2 %collective-permute-start.10 = (bf16[128,2176]{1,0:T(8,128)(2,1)S(1)}, bf16[128,2176]{1,0:T(8,128)(2,1)S(1)}, u32[]{:S(2)}, u32[]{:S(2)}) collective-permute-start(bf16[128,2176]{1,0:T(8,128)(2,1)S(1)} %pad_maximum_fusion.43), channel_id=1, source_target_pairs={{0,2},{1,3},{2,0},{3,1},{4,6},{5,7},{6,4},{7,5},{8,10},{9,11},{10,... | collective-permute-start | bytes 1671176 | tf_op jit(solution)/shard_map/ppermute | solution.py:444
  310.8 27.0 %collective-permute-start.18 = (bf16[128,2048]{1,0:T(8,128)(2,1)}, bf16[128,2048]{1,0:T(8,128)(2,1)}, u32[]{:S(2)}, u32[]{:S(2)}) collective-permute-start(bf16[128,2048]{1,0:T(8,128)(2,1)} %copy-done.79), channel_id=1, source_target_pairs={{0,8},{4,12},{8,16},{12,20},{16,24},{20,28},{24,0},{28,4},{1,9},{5... | collective-permute-start | bytes 1572872 | tf_op jit(solution)/shard_map/ppermute | solution.py:461
  336.7 138.4 %collective-permute-start.6 = (bf16[512,2048]{1,0:T(8,128)(2,1)}, bf16[512,2048]{1,0:T(8,128)(2,1)}, u32[]{:S(2)}, u32[]{:S(2)}) collective-permute-start(bf16[512,2048]{1,0:T(8,128)(2,1)} %get-tuple-element.237), channel_id=1, source_target_pairs={{0,1},{1,0},{2,3},{3,2},{4,5},{5,4},{6,7},{7,6},{8,9},{9,8},{10,11... | collective-permute-start | bytes 6291464 | tf_op jit(solution)/shard_map/ppermute | solution.py:444
  337.8 156.8 %collective-permute-start.11 = (bf16[512,2176]{1,0:T(8,128)(2,1)}, bf16[512,2176]{1,0:T(8,128)(2,1)}, u32[]{:S(2)}, u32[]{:S(2)}) collective-permute-start(bf16[512,2176]{1,0:T(8,128)(2,1)} %copy-done.58), channel_id=1, source_target_pairs={{0,1},{1,0},{2,3},{3,2},{4,5},{5,4},{6,7},{7,6},{8,9},{9,8},{10,11... | collective-permute-start | bytes 6684680 | tf_op jit(solution)/shard_map/ppermute | solution.py:444
  397.2 108.5 %collective-permute-start.57 = (bf16[512,2048]{1,0:T(8,128)(2,1)}, bf16[512,2048]{1,0:T(8,128)(2,1)}, u32[]{:S(2)}, u32[]{:S(2)}) collective-permute-start(bf16[512,2048]{1,0:T(8,128)(2,1)} %get-tuple-element.231), channel_id=1, source_target_pairs={{0,1},{1,0},{2,3},{3,2},{4,5},{5,4},{6,7},{7,6},{8,9},{9,8},{10,11... | collective-permute-start | bytes 6291464 | tf_op jit(solution)/shard_map/ppermute | solution.py:444
  442.1 87.5 %collective-permute-start.62 = (bf16[512,2176]{1,0:T(8,128)(2,1)}, bf16[512,2176]{1,0:T(8,128)(2,1)}, u32[]{:S(2)}, u32[]{:S(2)}) collective-permute-start(bf16[512,2176]{1,0:T(8,128)(2,1)} %copy-done.57), channel_id=1, source_target_pairs={{0,1},{1,0},{2,3},{3,2},{4,5},{5,4},{6,7},{7,6},{8,9},{9,8},{10,11... | collective-permute-start | bytes 6684680 | tf_op jit(solution)/shard_map/ppermute | solution.py:444
  473.3 66.6 %collective-permute-start.42 = (bf16[512,2048]{1,0:T(8,128)(2,1)}, bf16[512,2048]{1,0:T(8,128)(2,1)}, u32[]{:S(2)}, u32[]{:S(2)}) collective-permute-start(bf16[512,2048]{1,0:T(8,128)(2,1)} %get-tuple-element.225), channel_id=1, source_target_pairs={{0,1},{1,0},{2,3},{3,2},{4,5},{5,4},{6,7},{7,6},{8,9},{9,8},{10,11... | collective-permute-start | bytes 6291464 | tf_op jit(solution)/shard_map/ppermute | solution.py:444
  475.1 80.0 %collective-permute-start.47 = (bf16[512,2176]{1,0:T(8,128)(2,1)}, bf16[512,2176]{1,0:T(8,128)(2,1)}, u32[]{:S(2)}, u32[]{:S(2)}) collective-permute-start(bf16[512,2176]{1,0:T(8,128)(2,1)} %slice_dynamic-update-slice_fusion.4), channel_id=1, source_target_pairs={{0,1},{1,0},{2,3},{3,2},{4,5},{5,4},{6,7},{7,6},{8,9},{9,8},{10,11... | collective-permute-start | bytes 6684680 | tf_op jit(solution)/shard_map/ppermute | solution.py:444
  494.6 70.8 %collective-permute-start.24 = (bf16[512,2048]{1,0:T(8,128)(2,1)}, bf16[512,2048]{1,0:T(8,128)(2,1)}, u32[]{:S(2)}, u32[]{:S(2)}) collective-permute-start(bf16[512,2048]{1,0:T(8,128)(2,1)} %get-tuple-element.219), channel_id=1, source_target_pairs={{0,1},{1,0},{2,3},{3,2},{4,5},{5,4},{6,7},{7,6},{8,9},{9,8},{10,11... | collective-permute-start | bytes 6291464 | tf_op jit(solution)/shard_map/ppermute | solution.py:444
  505.8 75.1 %collective-permute-start.32 = (bf16[512,2176]{1,0:T(8,128)(2,1)S(1)}, bf16[512,2176]{1,0:T(8,128)(2,1)}, u32[]{:S(2)}, u32[]{:S(2)}) collective-permute-start(bf16[512,2176]{1,0:T(8,128)(2,1)S(1)} %slice_dynamic-update-slice_fusion.8), channel_id=1, source_target_pairs={{0,1},{1,0},{2,3},{3,2},{4,5},{5,4},{6,7},{7,6},{8,9},{9,8},{10,11... | collective-permute-start | bytes 6684680 | tf_op jit(solution)/shard_map/ppermute | solution.py:444
  800.5 51.9 %collective-permute-start.96 = (f32[4,2,2,2,128]{4,3,0,1,2:T(2,128)S(1)}, f32[4,2,2,2,128]{4,3,0,1,2:T(2,128)S(1)}, u32[]{:S(2)}, u32[]{:S(2)}) collective-permute-start(f32[4,2,2,2,128]{4,3,0,1,2:T(2,128)S(1)} %slice_bitcast_fusion.68), channel_id=1, source_target_pairs={{0,1},{1,0},{2,3},{3,2},{4,5},{5,4},{6,7},{7,6},{8,9},{9,8},{10,11... | collective-permute-start | bytes 49160 | tf_op jit(solution)/shard_map/ppermute | solution.py:444
  813.2 72.9 %collective-permute-start.78 = (bf16[2,2,2,64,2048]{4,3,0,1,2:T(8,128)(2,1)}, bf16[2,2,2,64,2048]{4,3,0,1,2:T(8,128)(2,1)}, u32[]{:S(2)}, u32[]{:S(2)}) collective-permute-start(bf16[2,2,2,64,2048]{4,3,0,1,2:T(8,128)(2,1)} %copy.347), channel_id=1, source_target_pairs={{0,1},{1,0},{2,3},{3,2},{4,5},{5,4},{6,7},{7,6},{8,9},{9,8},{10,11... | collective-permute-start | bytes 6291464 | tf_op jit(solution)/shard_map/ppermute | solution.py:444
  822.0 66.7 %collective-permute-start.83 = (bf16[2,2,2,64,2048]{4,3,0,1,2:T(8,128)(2,1)}, bf16[2,2,2,64,2048]{4,3,0,1,2:T(8,128)(2,1)}, u32[]{:S(2)}, u32[]{:S(2)}) collective-permute-start(bf16[2,2,2,64,2048]{4,3,0,1,2:T(8,128)(2,1)} %copy.350), channel_id=1, source_target_pairs={{0,1},{1,0},{2,3},{3,2},{4,5},{5,4},{6,7},{7,6},{8,9},{9,8},{10,11... | collective-permute-start | bytes 6291464 | tf_op jit(solution)/shard_map/ppermute | solution.py:444
  833.6 58.2 %collective-permute-start.88 = (bf16[2,2,2,64,2048]{4,3,0,1,2:T(8,128)(2,1)}, bf16[2,2,2,64,2048]{4,3,0,1,2:T(8,128)(2,1)}, u32[]{:S(2)}, u32[]{:S(2)}) collective-permute-start(bf16[2,2,2,64,2048]{4,3,0,1,2:T(8,128)(2,1)} %copy.353), channel_id=1, source_target_pairs={{0,1},{1,0},{2,3},{3,2},{4,5},{5,4},{6,7},{7,6},{8,9},{9,8},{10,11... | collective-permute-start | bytes 6291464 | tf_op jit(solution)/shard_map/ppermute | solution.py:444
  842.3 54.0 %collective-permute-start.73 = (bf16[2,2,2,64,2048]{4,3,0,1,2:T(8,128)(2,1)}, bf16[2,2,2,64,2048]{4,3,0,1,2:T(8,128)(2,1)}, u32[]{:S(2)}, u32[]{:S(2)}) collective-permute-start(bf16[2,2,2,64,2048]{4,3,0,1,2:T(8,128)(2,1)} %copy.344), channel_id=1, source_target_pairs={{0,1},{1,0},{2,3},{3,2},{4,5},{5,4},{6,7},{7,6},{8,9},{9,8},{10,11... | collective-permute-start | bytes 6291464 | tf_op jit(solution)/shard_map/ppermute | solution.py:444
  857.8 41.9 %collective-permute-start.33 = (bf16[2,2,2,64,2048]{4,3,0,1,2:T(8,128)(2,1)}, bf16[2,2,2,64,2048]{4,3,0,1,2:T(8,128)(2,1)}, u32[]{:S(2)}, u32[]{:S(2)}) collective-permute-start(bf16[2,2,2,64,2048]{4,3,0,1,2:T(8,128)(2,1)} %copy.331), channel_id=1, source_target_pairs={{0,1},{1,0},{2,3},{3,2},{4,5},{5,4},{6,7},{7,6},{8,9},{9,8},{10,11... | collective-permute-start | bytes 6291464 | tf_op jit(solution)/shard_map/ppermute | solution.py:444
  877.1 316.4 %all-to-all-start.4 = ((bf16[88,8,256]{2,0,1:T(8,128)(2,1)}), bf16[88,8,256]{2,0,1:T(8,128)(2,1)}, u32[]{:S(2)}, u32[]{:S(2)}) async-start(bf16[88,8,256]{2,0,1:T(8,128)(2,1)} %bitcast.578), calls=%async_computation.7 | async-start | bytes 720896 | tf_op jit(solution)/shard_map/all_to_all | solution.py:925
  883.0 346.5 %reduce-scatter.9.cloned.1.call-start = ((), (), s32[]{:S(2)}) async-start(), calls=%async_computation.13 | async-start | bytes 1179648 | tf_op jit(solution)/shard_map/reduce_scatter | solution.py:865
  930.0 29.0 %collective-permute-start.91 = (bf16[2,64,2048]{2,1,0:T(8,128)(2,1)}, bf16[2,64,2048]{2,1,0:T(8,128)(2,1)S(1)}, u32[]{:S(2)}, u32[]{:S(2)}) collective-permute-start(bf16[2,64,2048]{2,1,0:T(8,128)(2,1)} %fusion.100), channel_id=1, source_target_pairs={{0,4},{4,0},{8,12},{12,8},{16,20},{20,16},{24,28},{28,24},{1,5},{5... | collective-permute-start | bytes 1572872 | tf_op jit(solution)/shard_map/ppermute | solution.py:444
  938.5 31.8 %collective-permute-start.76 = (bf16[2,64,2048]{2,1,0:T(8,128)(2,1)}, bf16[2,64,2048]{2,1,0:T(8,128)(2,1)}, u32[]{:S(2)}, u32[]{:S(2)}) collective-permute-start(bf16[2,64,2048]{2,1,0:T(8,128)(2,1)} %fusion.94), channel_id=1, source_target_pairs={{0,4},{4,0},{8,12},{12,8},{16,20},{20,16},{24,28},{28,24},{1,5},{5... | collective-permute-start | bytes 1572872 | tf_op jit(solution)/shard_map/ppermute | solution.py:444
  951.8 29.8 %collective-permute-start.36 = (bf16[2,64,2048]{2,1,0:T(8,128)(2,1)}, bf16[2,64,2048]{2,1,0:T(8,128)(2,1)}, u32[]{:S(2)}, u32[]{:S(2)}) collective-permute-start(bf16[2,64,2048]{2,1,0:T(8,128)(2,1)} %fusion.88), channel_id=1, source_target_pairs={{0,4},{4,0},{8,12},{12,8},{16,20},{20,16},{24,28},{28,24},{1,5},{5... | collective-permute-start | bytes 1572872 | tf_op jit(solution)/shard_map/ppermute | solution.py:444
  961.0 31.7 %collective-permute-start.51 = (bf16[2,64,2048]{2,1,0:T(8,128)(2,1)}, bf16[2,64,2048]{2,1,0:T(8,128)(2,1)S(1)}, u32[]{:S(2)}, u32[]{:S(2)}) collective-permute-start(bf16[2,64,2048]{2,1,0:T(8,128)(2,1)} %fusion.90), channel_id=1, source_target_pairs={{0,4},{4,0},{8,12},{12,8},{16,20},{20,16},{24,28},{28,24},{1,5},{5... | collective-permute-start | bytes 1572872 | tf_op jit(solution)/shard_map/ppermute | solution.py:444
  972.6 31.3 %collective-permute-start.66 = (bf16[2,64,2048]{2,1,0:T(8,128)(2,1)S(1)}, bf16[2,64,2048]{2,1,0:T(8,128)(2,1)S(1)}, u32[]{:S(2)}, u32[]{:S(2)}) collective-permute-start(bf16[2,64,2048]{2,1,0:T(8,128)(2,1)S(1)} %copy-done.136), channel_id=1, source_target_pairs={{0,4},{4,0},{8,12},{12,8},{16,20},{20,16},{24,28},{28,24},{1,5},{5... | collective-permute-start | bytes 1572872 | tf_op jit(solution)/shard_map/ppermute | solution.py:444
  981.6 26.0 %collective-permute-start.64 = (bf16[2,64,2048]{2,1,0:T(8,128)(2,1)S(1)}, bf16[2,64,2048]{2,1,0:T(8,128)(2,1)S(1)}, u32[]{:S(2)}, u32[]{:S(2)}) collective-permute-start(bf16[2,64,2048]{2,1,0:T(8,128)(2,1)S(1)} %copy-done.133), channel_id=1, source_target_pairs={{0,2},{1,3},{2,0},{3,1},{4,6},{5,7},{6,4},{7,5},{8,10},{9,11},{10,... | collective-permute-start | bytes 1572872 | tf_op jit(solution)/shard_map/ppermute | solution.py:444
  983.8 31.4 %collective-permute-start.15 = (bf16[2,64,2048]{2,1,0:T(8,128)(2,1)S(1)}, bf16[2,64,2048]{2,1,0:T(8,128)(2,1)S(1)}, u32[]{:S(2)}, u32[]{:S(2)}) collective-permute-start(bf16[2,64,2048]{2,1,0:T(8,128)(2,1)S(1)} %copy-done.135), channel_id=1, source_target_pairs={{0,4},{4,0},{8,12},{12,8},{16,20},{20,16},{24,28},{28,24},{1,5},{5... | collective-permute-start | bytes 1572872 | tf_op jit(solution)/shard_map/ppermute | solution.py:444
  992.7 93.2 %collective-permute-start.13 = (bf16[2,64,2048]{2,1,0:T(8,128)(2,1)S(1)}, bf16[2,64,2048]{2,1,0:T(8,128)(2,1)S(1)}, u32[]{:S(2)}, u32[]{:S(2)}) collective-permute-start(bf16[2,64,2048]{2,1,0:T(8,128)(2,1)S(1)} %copy-done.132), channel_id=1, source_target_pairs={{0,2},{1,3},{2,0},{3,1},{4,6},{5,7},{6,4},{7,5},{8,10},{9,11},{10,... | collective-permute-start | bytes 1572872 | tf_op jit(solution)/shard_map/ppermute | solution.py:444
  994.9 61.5 %collective-permute-start.82 = (bf16[64,2048]{1,0:T(8,128)(2,1)}, bf16[64,2048]{1,0:T(8,128)(2,1)S(1)}, u32[]{:S(2)}, u32[]{:S(2)}) collective-permute-start(bf16[64,2048]{1,0:T(8,128)(2,1)} %fusion.138), channel_id=1, source_target_pairs={{0,2},{1,3},{2,0},{3,1},{4,6},{5,7},{6,4},{7,5},{8,10},{9,11},{10,... | collective-permute-start | bytes 786440 | tf_op jit(solution)/shard_map/ppermute | solution.py:444
  1004.0 52.5 %collective-permute-start.80 = (bf16[64,2048]{1,0:T(8,128)(2,1)}, bf16[64,2048]{1,0:T(8,128)(2,1)S(1)}, u32[]{:S(2)}, u32[]{:S(2)}) collective-permute-start(bf16[64,2048]{1,0:T(8,128)(2,1)} %fusion.137), channel_id=1, source_target_pairs={{0,4},{4,0},{8,12},{12,8},{16,20},{20,16},{24,28},{28,24},{1,5},{5... | collective-permute-start | bytes 786440 | tf_op jit(solution)/shard_map/ppermute | solution.py:444
  1007.6 33.5 %collective-permute-start.87 = (bf16[64,2048]{1,0:T(8,128)(2,1)S(1)}, bf16[64,2048]{1,0:T(8,128)(2,1)S(1)}, u32[]{:S(2)}, u32[]{:S(2)}) collective-permute-start(bf16[64,2048]{1,0:T(8,128)(2,1)S(1)} %fusion.140), channel_id=1, source_target_pairs={{0,2},{1,3},{2,0},{3,1},{4,6},{5,7},{6,4},{7,5},{8,10},{9,11},{10,... | collective-permute-start | bytes 786440 | tf_op jit(solution)/shard_map/ppermute | solution.py:444
  1056.5 39.5 %collective-permute-start.37 = (bf16[64,2048]{1,0:T(8,128)(2,1)S(1)}, bf16[64,2048]{1,0:T(8,128)(2,1)S(1)}, u32[]{:S(2)}, u32[]{:S(2)}) collective-permute-start(bf16[64,2048]{1,0:T(8,128)(2,1)S(1)} %fusion.130), channel_id=1, source_target_pairs={{0,2},{1,3},{2,0},{3,1},{4,6},{5,7},{6,4},{7,5},{8,10},{9,11},{10,... | collective-permute-start | bytes 786440 | tf_op jit(solution)/shard_map/ppermute | solution.py:444
  1068.9 74.2 %collective-permute-start.35 = (bf16[64,2048]{1,0:T(8,128)(2,1)}, bf16[64,2048]{1,0:T(8,128)(2,1)}, u32[]{:S(2)}, u32[]{:S(2)}) collective-permute-start(bf16[64,2048]{1,0:T(8,128)(2,1)} %fusion.129), channel_id=1, source_target_pairs={{0,4},{4,0},{8,12},{12,8},{16,20},{20,16},{24,28},{28,24},{1,5},{5... | collective-permute-start | bytes 786440 | tf_op jit(solution)/shard_map/ppermute | solution.py:444
  1070.3 74.9 %collective-permute-start.52 = (bf16[64,2048]{1,0:T(8,128)(2,1)}, bf16[64,2048]{1,0:T(8,128)(2,1)}, u32[]{:S(2)}, u32[]{:S(2)}) collective-permute-start(bf16[64,2048]{1,0:T(8,128)(2,1)} %fusion.132), channel_id=1, source_target_pairs={{0,2},{1,3},{2,0},{3,1},{4,6},{5,7},{6,4},{7,5},{8,10},{9,11},{10,... | collective-permute-start | bytes 786440 | tf_op jit(solution)/shard_map/ppermute | solution.py:444
  1085.9 61.1 %collective-permute-start.50 = (bf16[64,2048]{1,0:T(8,128)(2,1)}, bf16[64,2048]{1,0:T(8,128)(2,1)}, u32[]{:S(2)}, u32[]{:S(2)}) collective-permute-start(bf16[64,2048]{1,0:T(8,128)(2,1)} %fusion.131), channel_id=1, source_target_pairs={{0,4},{4,0},{8,12},{12,8},{16,20},{20,16},{24,28},{28,24},{1,5},{5... | collective-permute-start | bytes 786440 | tf_op jit(solution)/shard_map/ppermute | solution.py:444
  1096.0 41.2 %collective-permute-start.67 = (bf16[64,2048]{1,0:T(8,128)(2,1)}, bf16[64,2048]{1,0:T(8,128)(2,1)}, u32[]{:S(2)}, u32[]{:S(2)}) collective-permute-start(bf16[64,2048]{1,0:T(8,128)(2,1)} %fusion.134), channel_id=1, source_target_pairs={{0,2},{1,3},{2,0},{3,1},{4,6},{5,7},{6,4},{7,5},{8,10},{9,11},{10,... | collective-permute-start | bytes 786440 | tf_op jit(solution)/shard_map/ppermute | solution.py:444
  1097.8 41.6 %collective-permute-start.65 = (bf16[64,2048]{1,0:T(8,128)(2,1)}, bf16[64,2048]{1,0:T(8,128)(2,1)}, u32[]{:S(2)}, u32[]{:S(2)}) collective-permute-start(bf16[64,2048]{1,0:T(8,128)(2,1)} %fusion.133), channel_id=1, source_target_pairs={{0,4},{4,0},{8,12},{12,8},{16,20},{20,16},{24,28},{28,24},{1,5},{5... | collective-permute-start | bytes 786440 | tf_op jit(solution)/shard_map/ppermute | solution.py:444
  1115.3 171.1 %reduce-scatter.13.cloned.1.call-start = ((), (), s32[]{:S(2)}) async-start(), calls=%async_computation.16 | async-start | bytes 3041280
  1137.1 221.2 %reduce-scatter.11.cloned.1.call-start = ((), (), s32[]{:S(2)}) async-start(), calls=%async_computation.14 | async-start | bytes 2359296 | tf_op jit(solution)/shard_map/reduce_scatter | solution.py:865
  1139.5 39.0 %collective-permute-start.14 = (bf16[64,2048]{1,0:T(8,128)(2,1)}, bf16[64,2048]{1,0:T(8,128)(2,1)}, u32[]{:S(2)}, u32[]{:S(2)}) collective-permute-start(bf16[64,2048]{1,0:T(8,128)(2,1)} %fusion.127), channel_id=1, source_target_pairs={{0,4},{4,0},{8,12},{12,8},{16,20},{20,16},{24,28},{28,24},{1,5},{5... | collective-permute-start | bytes 786440 | tf_op jit(solution)/shard_map/ppermute | solution.py:444
  1193.4 28.5 %all-to-all-start.3 = ((bf16[2,2048,88]{2,0,1:T(2,128)(2,1)}), bf16[2,2048,88]{2,0,1:T(2,128)(2,1)}, u32[]{:S(2)}, u32[]{:S(2)}) async-start(bf16[2,2048,88]{2,0,1:T(2,128)(2,1)} %copy.366), calls=%async_computation.6 | async-start | bytes 2097152 | tf_op jit(solution)/shard_map/all_to_all | solution.py:918
  1197.7 237.6 %reduce-scatter.7.cloned.1.call-start = ((), (), s32[]{:S(2)}) async-start(), calls=%async_computation.12 | async-start | bytes 3538944 | tf_op jit(solution)/shard_map/reduce_scatter | solution.py:865
  (289 other events, 4169.9 us)
Sparse Core Ops, SparseCore 0:
  11.5 62.0 all-gather.11
  75.7 39.0 all-gather.5
  117.0 58.7 all-gather.7
  177.6 58.5 all-gather.9
  1115.4 64.8 reduce-scatter.8
  1185.5 100.8 reduce-scatter.12
  1290.0 68.2 reduce-scatter.10
  1361.9 73.3 reduce-scatter.6

commit v2 on v1

--- a/solution.py
+++ b/solution.py
@@ -551,6 +551,45 @@
     )
 
 
+def dp_gather(own, dp_index, axis):
+    planes = lax.axis_size("dp") // 2
+    plane = dp_index // 2
+    side = dp_index % 2
+    if axis == 0:
+        whole = jnp.zeros((2 * planes,) + own.shape, own.dtype)
+    else:
+        whole = jnp.zeros(own.shape[:-1] + (2 * planes * own.shape[-1],), own.dtype)
+
+    def place(whole, piece, index):
+        if axis == 0:
+            return lax.dynamic_update_index_in_dim(whole, piece, index, 0)
+        return lax.dynamic_update_slice_in_dim(whole, piece, index * piece.shape[-1], 1)
+
+    piece = own
+    for step in range(planes):
+        base = (plane - step) % planes * 2
+        whole = place(whole, piece, base + side)
+        whole = place(whole, x_hop(piece), base + 1 - side)
+        if step + 1 < planes:
+            piece = z_hop(piece)
+    return whole
+
+
+def dp_scatter(block, dp_index):
+    planes = lax.axis_size("dp") // 2
+    plane = dp_index // 2
+    side = dp_index % 2
+    moving = None
+    for step in list(range(1, planes)) + [0]:
+        base = (plane - step) % planes * 2
+        received = x_hop(low(block(base + 1 - side))).astype(jnp.float32)
+        piece = block(base + side) + received
+        if moving is not None:
+            piece = piece + z_hop(low(moving)).astype(jnp.float32)
+        moving = piece
+    return moving
+
+
 def padded(values, axis, size):
     pads = [(0, 0)] * values.ndim
     pads[axis] = (0, size - values.shape[axis])
@@ -597,28 +636,46 @@
         return lax.dynamic_slice_in_dim(values, own_start, own_count, 0)
 
     lat_width = w_latent.shape[1]
-    lat_rows = w_latent.shape[0] // tensor_size
-    lat_piece = lax.dynamic_slice_in_dim(w_latent, tensor_index * lat_rows, lat_rows, 0)
-    gains = jnp.concatenate([gain_attn, gain_ffn, gain_latent])[None]
-    gain_rows = gain_attn.shape[0]
-    router_piece = lax.dynamic_slice_in_dim(
-        w_router, tensor_index * lat_rows, lat_rows, 0
-    ).reshape(2, lat_rows * experts // 2)
-    pack = jnp.concatenate([lat_piece, gains, padded(router_piece, 1, lat_width)])
-    pack_rows = -(-pack.shape[0] // 8) * 8
-    packed = lax.all_gather(padded(pack, 0, pack_rows), ("dp", "tensor"), axis=0, tiled=False)
-    latent_weight = packed[:, :lat_rows].reshape(width, lat_width)
-    gains_all = packed[::tensor_size, lat_rows].astype(jnp.float32)
-    gain_attn_f = gains_all[:, :gain_rows].reshape(width)
-    gain_ffn_f = gains_all[:, gain_rows : 2 * gain_rows].reshape(width)
-    gain_latent_f = gains_all[:, 2 * gain_rows :].reshape(KV_RANK)
-    router_weight = packed[:, lat_rows + 1 : lat_rows + 3, : router_piece.shape[1]].reshape(
-        width, experts
-    )
-
-    query_weight = lax.all_gather(w_query, "dp", axis=0, tiled=True)
-    expand_weight = lax.all_gather(w_expand, "dp", axis=0, tiled=True)
-    output_weight = lax.all_gather(w_output, "dp", axis=1, tiled=True)
+    lat_block = w_latent.shape[0]
+    lat_rows = lat_block // tensor_size
+    side = jnp.concatenate(
+        [
+            w_latent,
+            w_router,
+            gain_attn[:, None],
+            gain_ffn[:, None],
+            padded(gain_latent, 0, lat_block)[:, None],
+        ],
+        axis=1,
+    )
+    side_width = lanes(side.shape[1])
+    side = padded(
+        lax.dynamic_slice_in_dim(side, tensor_index * lat_rows, lat_rows, 0), 1, side_width
+    )
+    side_all = dp_gather(side, dp_index, 0)
+    side_pair = jnp.stack([side_all, y_hop(side_all)])
+    side_far = core_hop(side_pair)
+    core = tensor_index % 2
+    level = tensor_index // 2
+    side_even = jnp.where(core == 0, side_pair, side_far)
+    side_odd = jnp.where(core == 0, side_far, side_pair)
+    side_near = jnp.stack([side_even, side_odd], axis=1)
+    side_all = jnp.where(level == 0, side_near, side_near[::-1]).reshape(
+        tensor_size, dp_size, lat_rows, side_width
+    )
+    side_all = side_all.transpose(1, 0, 2, 3).reshape(width, side_width)
+    latent_weight = side_all[:, :lat_width]
+    router_weight = side_all[:, lat_width : lat_width + experts]
+    gains_all = side_all[:, lat_width + experts : lat_width + experts + 3].astype(jnp.float32).T
+    gain_attn_f = gains_all[0]
+    gain_ffn_f = gains_all[1]
+    gain_latent_f = gains_all[2].reshape(dp_size, lat_block)[:, : gain_latent.shape[0]].reshape(
+        KV_RANK
+    )
+
+    query_weight = dp_gather(w_query, dp_index, 0).reshape(width, w_query.shape[1])
+    expand_weight = dp_gather(w_expand, dp_index, 0).reshape(KV_RANK, w_expand.shape[1])
+    output_weight = dp_gather(w_output, dp_index, 1).reshape(w_output.shape[0], width)
 
     routed = jnp.sum(
         (routes[:, :, None] == jnp.arange(experts, dtype=jnp.int32)[None, None, :]).astype(
@@ -630,10 +687,28 @@
     earlier = (order[None, :] < order[:, None]).astype(jnp.bfloat16)
     rank = jnp.dot(earlier, low(routed), preferred_element_type=jnp.float32)
     standing = routed * (1.0 + (rank < capacity).astype(jnp.float32))
+    standing_own = own_rows(standing)
+    marks_all = lax.all_gather(low(standing), "dp", axis=0, tiled=True)
     cot_own = own_rows(cotangent)
-    standing_own = own_rows(standing)
-    cot_sent = jnp.concatenate([cot_own, padded(low(standing_own), 1, 128)], axis=1)
+    cot_sent, _ = lax.optimization_barrier((cot_own, query_weight))
     cot_chunks = slice_gather(cot_sent)
+    planes = dp_size // 2
+    marks_all = marks_all.reshape(planes, 8, own_count, experts)
+    near = jnp.arange(8, dtype=jnp.int32)
+    near_x = near % 2 ^ dp_index % 2
+    near_y = near // 2 % 2 ^ level
+    near_core = near // 4 ^ core
+    near_block = near_x * 4 + near_y * 2 + near_core
+    mark_chunks = [
+        jnp.take(
+            lax.dynamic_index_in_dim(
+                marks_all, (dp_index // 2 - step) % planes, 0, keepdims=False
+            ),
+            near_block,
+            axis=0,
+        ).reshape(8 * own_count, experts)
+        for step in range(planes)
+    ]
 
     shared_here = w_shared_gate.shape[1] // dp_size
     shared_in = lax.all_to_all(
@@ -702,7 +777,8 @@
     resid_own = own_rows(tokens).astype(jnp.float32) + tensor_scatter(attn_part, tensor_index)
     normed_own, inverse_own = norm_forward(resid_own, gain_ffn_f)
     normed_own_low = low(normed_own)
-    row_chunks = slice_gather(normed_own_low)
+    rows_sent, cot_chunks = lax.optimization_barrier((normed_own_low, cot_chunks))
+    row_chunks = slice_gather(rows_sent)
 
     def gating(rows, standing_rows):
         probs = jax.nn.softmax(
@@ -714,14 +790,15 @@
 
     expert_index = jnp.arange(experts, dtype=jnp.int32)[None, :]
     column = jnp.arange(hidden, dtype=jnp.int32)[None, :]
-    out_parts, in_parts, gate_parts = [], [], []
-    gate_weight_grad = up_weight_grad = down_weight_grad = 0.0
-    for (near_rows, far_rows), (near_cot, far_cot) in zip(row_chunks, cot_chunks):
-        rows = jnp.concatenate([near_rows, far_rows])
-        cots = jnp.concatenate([near_cot[:, :width], far_cot[:, :width]])
-        marks = jnp.concatenate(
-            [near_cot[:, width : width + experts], far_cot[:, width : width + experts]]
-        ).astype(jnp.float32)
+    out_parts, in_parts, gate_parts, kept_parts = [], [], [], []
+    for step in range(planes):
+        rows = jnp.concatenate(row_chunks[step])
+        cots = jnp.concatenate(cot_chunks[step])
+        if step > 0:
+            rows, cots, in_parts[-1], out_parts[-1] = lax.optimization_barrier(
+                (rows, cots, in_parts[-1], out_parts[-1])
+            )
+        marks = mark_chunks[step].astype(jnp.float32)
         _, chunk_gates, _ = gating(rows, marks)
         chunk_gates = jnp.where(marks > 1.5, chunk_gates, 0.0)
         scale = jnp.ones((rows.shape[0], hidden), jnp.float32)
@@ -757,6 +834,9 @@
                 + jnp.einsum("tf,df->td", up_grad, up_weight, preferred_element_type=jnp.float32)
             )
         )
+        kept_parts.append((rows, cots, gate_grad, up_grad, act_scaled))
+    gate_weight_grad = up_weight_grad = down_weight_grad = 0.0
+    for rows, cots, gate_grad, up_grad, act_scaled in kept_parts:
         gate_weight_grad += jnp.einsum(
             "td,tf->df", rows, gate_grad, preferred_element_type=jnp.float32
         )
@@ -769,7 +849,6 @@
     gate_sums = jnp.stack(gate_parts).reshape(-1, exp_here, 2, 2, 2, own_count)
     gate_sums = gate_sums[:, :, 0] + core_hop(gate_sums[:, :, 1])
     gate_sums = gate_sums[:, :, 0] + y_hop(gate_sums[:, :, 1])
-    planes = dp_size // 2
     block = jnp.arange(dp_size, dtype=jnp.int32)
     place = ((dp_index // 2 - block // 2) % planes) * 2 + (block + dp_index) % 2
     gate_sums = gate_sums.transpose(0, 2, 1, 3).reshape(dp_size, exp_here, own_count)[place]
@@ -861,47 +940,49 @@
     out_sum = slice_scatter(out_parts)
     result = tensor_gather(low(resid_own + out_sum), tensor_index)
 
-    def scattered(values, dimension):
-        return lax.psum_scatter(
-            low(values), "dp", scatter_dimension=dimension, tiled=True
-        ).astype(jnp.float32)
-
-    output_share = scattered(output_weight_grad, 1)
-    query_share = scattered(query_weight_grad, 0)
-    expand_share = scattered(expand_weight_grad, 0)
-
-    gain_shares = jnp.concatenate(
+    output_share = dp_scatter(
+        lambda i: lax.dynamic_slice_in_dim(
+            output_weight_grad, i * w_output.shape[1], w_output.shape[1], 1
+        ),
+        dp_index,
+    )
+    query_share = dp_scatter(
+        lambda i: lax.dynamic_slice_in_dim(query_weight_grad, i * lat_block, lat_block, 0),
+        dp_index,
+    )
+    expand_rows = w_expand.shape[0]
+    expand_share = dp_scatter(
+        lambda i: lax.dynamic_slice_in_dim(expand_weight_grad, i * expand_rows, expand_rows, 0),
+        dp_index,
+    )
+
+    gain_latent_rows = padded(gain_latent_grad.reshape(dp_size, -1), 1, lat_block).reshape(width)
+    side_grad = jnp.concatenate(
         [
-            gain_attn_grad.reshape(dp_size, -1),
-            gain_ffn_grad.reshape(dp_size, -1),
-            gain_latent_grad.reshape(dp_size, -1),
+            latent_weight_grad,
+            router_grad,
+            jnp.stack([gain_attn_grad, gain_ffn_grad, gain_latent_rows]).T,
         ],
         axis=1,
-    )[:, None]
-    router_lanes = 512
-    router_rows = router_grad.reshape(dp_size, -1, router_lanes)
-    lat_block = w_latent.shape[0]
-    grad_pack = jnp.concatenate(
-        [
-            low(latent_weight_grad).reshape(dp_size, lat_block, lat_width),
-            low(gain_shares),
-            padded(low(router_rows), 2, lat_width),
-        ],
-        axis=1,
-    )
-    unit = 8 * tensor_size
-    grad_rows = -(-grad_pack.shape[1] // unit) * unit
-    grad_pack = padded(grad_pack, 1, grad_rows).reshape(dp_size * grad_rows, lat_width)
-    grad_piece = lax.psum_scatter(grad_pack, ("dp", "tensor"), scatter_dimension=0, tiled=True)
-    grad_full = tensor_gather(grad_piece, tensor_index).astype(jnp.float32)
-    latent_share = grad_full[:lat_block]
-    gain_row = grad_full[lat_block]
-    gain_attn_share = gain_row[:gain_rows]
-    gain_ffn_share = gain_row[gain_rows : 2 * gain_rows]
-    gain_latent_share = gain_row[2 * gain_rows :]
-    router_share = grad_full[
-        lat_block + 1 : lat_block + 1 + router_rows.shape[1], :router_lanes
-    ].reshape(lat_block, experts)
+    )
+    side_grad = padded(side_grad, 1, side_width)
+    side_grad = side_grad.reshape(dp_size, 2, 2, lat_rows, side_width)
+    kept_side = lax.dynamic_index_in_dim(side_grad, core, 2, keepdims=False)
+    sent_side = lax.dynamic_index_in_dim(side_grad, 1 - core, 2, keepdims=False)
+    side_grad = kept_side + core_hop(low(sent_side)).astype(jnp.float32)
+    kept_side = lax.dynamic_index_in_dim(side_grad, level, 1, keepdims=False)
+    sent_side = lax.dynamic_index_in_dim(side_grad, 1 - level, 1, keepdims=False)
+    side_grad = kept_side + y_hop(low(sent_side)).astype(jnp.float32)
+    side_piece = dp_scatter(
+        lambda i: lax.dynamic_index_in_dim(side_grad, i, 0, keepdims=False), dp_index
+    )
+    grad_full = tensor_gather(low(side_piece), tensor_index).astype(jnp.float32)
+    latent_share = grad_full[:, :lat_width]
+    router_share = grad_full[:, lat_width : lat_width + experts]
+    gain_rows = grad_full[:, lat_width + experts : lat_width + experts + 3].T
+    gain_attn_share = gain_rows[0]
+    gain_ffn_share = gain_rows[1]
+    gain_latent_share = gain_rows[2, : gain_latent.shape[0]]
 
     def routed_grad(grad, axis):
         return jnp.stack(

time: 1460 us -> 1270 us (0.87)
  waiting for transfers between devices: 592 us -> 384 us
  starting transfers between devices: 112 us -> 158 us
  blocking collectives: 0 us -> 30.6 us
  local copies, waits for them, and re-layouts: 253 us -> 230 us
    all_gather x4 -> x0, waiting for transfers between devices: 169 us -> none  [the longest x1 52.8 us: body_dense(): query_weight = lax.all_gather(w_query, 'dp', axis=0, tiled=True)]
    reduce_scatter x3 -> x0, waiting for transfers between devices: 137 us -> none  [scattered(): lax.psum_scatter(low(values), 'dp', scatter_dimension=dimension, tiled=True)]
    ppermute x94 -> x130, waiting for transfers between devices: 164 us -> 239 us  [hop(): lax.ppermute(values, axis, [(i, i ^ bit) for i in range(lax.axis_size(axi...]
    ppermute x12 -> x36, waiting for transfers between devices: 66.3 us -> 124 us  [z_hop(): lax.ppermute(values, 'dp', [(i, (i + 2) % count) for i in range(count)])]
    unnamed x9 -> x0, waiting for transfers between devices: 50.9 us -> none
    ppermute x94 -> x130, starting transfers between devices: 76.3 us -> 110 us  [hop(): lax.ppermute(values, axis, [(i, i ^ bit) for i in range(lax.axis_size(axi...]
    dynamic_update_slice x0 -> x32, local copies, waits for them, and re-layouts: none -> 31.8 us  [the longest x24 20.4 us: place(): return lax.dynamic_update_index_in_dim(whole, piece, index, 0)]
    all_gather x0 -> x1, blocking collectives: none -> 30.6 us  [body_dense(): marks_all = lax.all_gather(low(standing), 'dp', axis=0, tiled=True)]
  transfers between devices with their start and end apart: 119 -> 171, of which waited for: 50 -> 68; matrix products, arithmetic and copies ran while one was open for 32% -> 50% of each run, Pallas kernels for 0% -> 0%
where the time goes in v2:
time: 1270 us; the launch traced here: 1260 us
  waiting for transfers between devices  384 us (30%)
  matrix products  343 us (27%)
  local copies, waits for them, and re-layouts  230 us (18%)
  starting transfers between devices  158 us (12%)
  other arithmetic  107 us (8%)
  blocking collectives  30.6 us (2%)
    ppermute x130, waiting for transfers between devices, hop(): lax.ppermute(values, axis, [(i, i ^ bit) for i in range(lax.axis_size(axi...  239 us
    ppermute x36, waiting for transfers between devices, z_hop(): lax.ppermute(values, 'dp', [(i, (i + 2) % count) for i in range(count)])  124 us
    ppermute x130, starting transfers between devices, hop(): lax.ppermute(values, axis, [(i, i ^ bit) for i in range(lax.axis_size(axi...  110 us
    unnamed x425, local copies, waits for them, and re-layouts  67.7 us
    dot_general x4, matrix products, body_dense(): jnp.einsum('tf,td->fd', act_scaled, cots, preferred_element_type=jnp.floa...  39.2 us
    dot_general x4, matrix products, body_dense(): jnp.einsum('tf,df->td', up_grad, up_weight, preferred_element_type=jnp.fl...  37.8 us
    dot_general x4, matrix products, body_dense(): jnp.einsum('td,fd->tf', cots, down_weight, preferred_element_type=jnp.flo...  36.4 us
    dot_general x4, matrix products, body_dense(): jnp.einsum('td,tf->df', rows, up_grad, preferred_element_type=jnp.float32)  34.6 us
  transfers between devices with their start and end apart: 171, of which 68 were waited for; matrix products, arithmetic and copies ran while one was open for 50% of the time, Pallas kernels for 0%

profile of v2, /device:TPU:0, one launch (start us, length us, event | category | flops | bytes accessed | tf_op | source)
XLA Modules:
  0.0 1258.3 jit_solution(15601915157362472291)
XLA Ops:
  24.7 30.6 %all_gather.3 = bf16[4096,16]{0,1:T(8,128)(2,1)S(1)} all-gather(bf16[512,16]{0,1:T(8,128)(2,1)S(1)} %get-tuple-element.347), channel_id=1, replica_groups=mesh['dp'=8,'tensor'=4] {'dp'}, dimensions={0}, use_global_device_ids=true | all-gather | bytes 147456 | tf_op jit(solution)/shard_map/all_gather | solution.py:691
  100.7 8.0 collective-permute-done.4
  264.1 7.4 collective-permute-done.45
  274.4 11.4 collective-permute-start.49
  288.4 11.9 collective-permute-done.49
  310.9 12.3 collective-permute-done.52
  323.2 9.5 collective-permute-done.53
  357.7 15.4 %collective-permute-done.56 = bf16[64,2048]{1,0:T(8,128)(2,1)S(1)} collective-permute-done((bf16[64,2048]{1,0:T(8,128)(2,1)S(1)}, bf16[64,2048]{1,0:T(8,128)(2,1)S(1)}, u32[]{:S(2)}, u32[]{:S(2)}) %collective-permute-start.56) | collective-permute-done | bytes 262176 | tf_op jit(solution)/shard_map/ppermute | solution.py:444
  379.7 13.2 %collective-permute-done.78 = bf16[64,2048]{1,0:T(8,128)(2,1)S(1)} collective-permute-done((bf16[64,2048]{1,0:T(8,128)(2,1)S(1)}, bf16[64,2048]{1,0:T(8,128)(2,1)S(1)}, u32[]{:S(2)}, u32[]{:S(2)}) %collective-permute-start.78) | collective-permute-done | bytes 262176 | tf_op jit(solution)/shard_map/ppermute | solution.py:444
  398.4 8.2 collective-permute-done.72
  449.2 12.6 %multiply_multiply_fusion.3 = (f32[1024,896]{0,1:T(8,128)}, bf16[1024,896]{0,1:T(8,128)(2,1)S(1)}, bf16[1024,896]{0,1:T(8,128)(2,1)}, bf16[1024,896]{0,1:T(8,128)(2,1)}) fusion(f32[1024,896]{0,1:T(8,128)} %fusion.253, f32[1024,896]{0,1:T(8,128)} %fusion.254, f32[1024]{0:T(1024)S(1)} %get-tuple-element.165, pred[896]{0:T(1024)(128)(4,1)S(1)} %copy-done.162, ...), kind=kOutput, calls=%fused_computation.137 | convolution fusion | flops 3776446464 | bytes 24389376 | tf_op jit(solution)/shard_map/td,fd->tf/dot_general | solution.py:818
  461.8 7.7 fusion.265
  480.4 6.9 fusion.255
  494.4 9.6 add_convert_fusion.3
  519.8 9.5 multiply_multiply_fusion.2
  529.2 7.7 fusion.266
  547.9 7.0 fusion.258
  569.9 7.4 add_convert_fusion.2
  584.1 8.0 fusion.260
  592.1 8.1 fusion.259
  600.4 10.2 multiply_multiply_fusion.1
  610.6 7.7 fusion.267
  623.1 8.2 fusion.271
  631.3 7.0 fusion.261
  646.3 8.3 fusion.274
  654.7 7.0 add_convert_fusion.1
  685.8 10.3 multiply_convert_fusion.3
  696.1 14.0 %add_add_fusion.1 = f32[2048,896]{0,1:T(8,128)S(1)} fusion(f32[2048,896]{0,1:T(8,128)} %fusion.274, f32[2048,896]{0,1:T(8,128)} %fusion.272, f32[2048,896]{0,1:T(8,128)} %fusion.273, bf16[1024,2048]{1,0:T(8,128)(2,1)} %constant_dynamic-update-slice_fusion.31, f32[1024,896]{0,1:T(8,128)} %copy-done.57, f32[1024]{0:T(1024)S(1)} %get-tuple-element.159, ...), kind=kOutput, calls=%fused_computation.22 | convolution fusion | flops 3771858944 | bytes 40904448 | tf_op jit(solution)/shard_map/td,tf->df/dot_general | solution.py:843
  712.1 6.9 fusion.264
  719.0 12.6 %add_add_fusion.2 = f32[2048,896]{0,1:T(8,128)} fusion(f32[2048,896]{0,1:T(8,128)} %fusion.271, f32[2048,896]{0,1:T(8,128)} %fusion.269, f32[2048,896]{0,1:T(8,128)} %fusion.270, bf16[1024,896]{0,1:T(8,128)(2,1)S(1)} %get-tuple-element.173, bf16[1024,2048]{1,0:T(8,128)(2,1)} %constant_dynamic-update-slice_fusion.31), kind=kOutput, calls=%fused_computation.23 | convolution fusion | flops 3763601408 | bytes 35389440 | tf_op jit(solution)/shard_map/td,tf->df/dot_general | solution.py:840
  744.5 16.2 %add_add_fusion = f32[896,2048]{1,0:T(8,128)} fusion(f32[896,2048]{1,0:T(8,128)} %fusion.267, f32[896,2048]{1,0:T(8,128)} %fusion.265, f32[896,2048]{1,0:T(8,128)} %fusion.266, bf16[1024,896]{0,1:T(8,128)(2,1)} %get-tuple-element.187, bf16[1024,2048]{1,0:T(8,128)(2,1)} %pad_maximum_fusion.5), kind=kOutput, calls=%fused_computation.21 | convolution fusion | flops 3763601408 | bytes 35389440 | tf_op jit(solution)/shard_map/tf,td->fd/dot_general | solution.py:844
  769.1 13.8 %add_convert_fusion = bf16[1024,2048]{1,0:T(8,128)(2,1)} fusion(f32[1024,2048]{1,0:T(8,128)} %fusion.264, bf16[2048,896]{0,1:T(8,128)(2,1)} %copy-done.65, f32[1024,896]{0,1:T(8,128)} %copy-done.57, f32[1024]{0:T(1024)S(1)} %get-tuple-element.159, f32[1024]{0:T(1024)S(1)} %get-tuple-element.158, pred[896]{0:T(1024)(128)(4,1)S(1)} %copy-done.162, ...), kind=kOutput, calls=%fused_computation.9 | convolution fusion | flops 3770548224 | bytes 23602944 | tf_op jit(solution)/shard_map/tf,df->td/dot_general | solution.py:834
  825.9 8.4 all-to-all-done.4
  851.9 12.2 all-to-all-done.3
  874.8 9.9 collective-permute-done.69
  920.2 10.0 collective-permute-done.94
  931.6 11.3 collective-permute-done.119
  971.3 7.0 collective-permute-done.89
  981.4 8.1 collective-permute-done.114
  991.6 9.2 collective-permute-done.84
  1014.0 8.1 collective-permute-done.115
  1030.8 7.1 collective-permute-done.110
  1038.2 15.6 %collective-permute-done.124 = bf16[128,2048]{1,0:T(8,128)(2,1)S(1)} collective-permute-done((bf16[128,2048]{1,0:T(8,128)(2,1)S(1)}, bf16[128,2048]{1,0:T(8,128)(2,1)S(1)}, u32[]{:S(2)}, u32[]{:S(2)}) %collective-permute-start.124) | collective-permute-done | bytes 524320 | tf_op jit(solution)/shard_map/ppermute | solution.py:461
  1055.2 12.3 collective-permute-done.125
  1071.4 7.6 collective-permute-done.128
  1121.7 6.9 multiply_reduce_fusion
  1165.1 7.6 collective-permute-done.148
  1174.0 8.9 collective-permute-done.164
  (1152 shorter events, 768.1 us)
Async XLA Ops:
  0.7 89.2 %collective-permute-start.10 = (bf16[64,1024]{1,0:T(8,128)(2,1)}, bf16[64,1024]{1,0:T(8,128)(2,1)}, u32[]{:S(2)}, u32[]{:S(2)}) collective-permute-start(bf16[64,1024]{1,0:T(8,128)(2,1)} %param.30), channel_id=1, source_target_pairs={{0,8},{4,12},{8,16},{12,20},{16,24},{20,28},{24,0},{28,4},{1,9},{5... | collective-permute-start | bytes 393224 | tf_op jit(solution)/shard_map/ppermute | solution.py:461
  3.8 84.4 %collective-permute-start.9 = (bf16[64,1024]{1,0:T(8,128)(2,1)}, bf16[64,1024]{1,0:T(8,128)(2,1)}, u32[]{:S(2)}, u32[]{:S(2)}) collective-permute-start(bf16[64,1024]{1,0:T(8,128)(2,1)} %param.30), channel_id=1, source_target_pairs={{0,4},{4,0},{8,12},{12,8},{16,20},{20,16},{24,28},{28,24},{1,5},{5... | collective-permute-start | bytes 393224 | tf_op jit(solution)/shard_map/ppermute | solution.py:444
  5.3 125.8 %collective-permute-start.24 = (bf16[512,256]{1,0:T(8,128)(2,1)}, bf16[512,256]{1,0:T(8,128)(2,1)}, u32[]{:S(2)}, u32[]{:S(2)}) collective-permute-start(bf16[512,256]{1,0:T(8,128)(2,1)} %param.31), channel_id=1, source_target_pairs={{0,8},{4,12},{8,16},{12,20},{16,24},{20,28},{24,0},{28,4},{1,9},{5... | collective-permute-start | bytes 786440 | tf_op jit(solution)/shard_map/ppermute | solution.py:461
  6.8 121.9 %collective-permute-start.23 = (bf16[512,256]{1,0:T(8,128)(2,1)}, bf16[512,256]{1,0:T(8,128)(2,1)}, u32[]{:S(2)}, u32[]{:S(2)}) collective-permute-start(bf16[512,256]{1,0:T(8,128)(2,1)} %param.31), channel_id=1, source_target_pairs={{0,4},{4,0},{8,12},{12,8},{16,20},{20,16},{24,28},{28,24},{1,5},{5... | collective-permute-start | bytes 786440 | tf_op jit(solution)/shard_map/ppermute | solution.py:444
  7.4 145.1 %all-to-all-start = ((bf16[8,88,256]{2,1,0:T(8,128)(2,1)}), bf16[8,88,256]{2,1,0:T(8,128)(2,1)S(1)}, u32[]{:S(2)}, u32[]{:S(2)}) async-start(bf16[8,88,256]{2,1,0:T(8,128)(2,1)} %bitcast.815), calls=%async_computation | async-start | bytes 720896 | tf_op jit(solution)/shard_map/all_to_all | solution.py:717
  17.0 64.0 %collective-permute-start = (bf16[64,640]{1,0:T(8,128)(2,1)}, bf16[64,640]{1,0:T(8,128)(2,1)}, u32[]{:S(2)}, u32[]{:S(2)}) collective-permute-start(bf16[64,640]{1,0:T(8,128)(2,1)} %pad.48), channel_id=1, source_target_pairs={{0,4},{4,0},{8,12},{12,8},{16,20},{20,16},{24,28},{28,24},{1,5},{5... | collective-permute-start | bytes 245768 | tf_op jit(solution)/shard_map/ppermute | solution.py:444
  88.2 53.6 %collective-permute-start.17 = (bf16[256,768]{1,0:T(8,128)(2,1)S(1)}, bf16[256,768]{1,0:T(8,128)(2,1)}, u32[]{:S(2)}, u32[]{:S(2)}) collective-permute-start(bf16[256,768]{1,0:T(8,128)(2,1)S(1)} %copy-done.103), channel_id=1, source_target_pairs={{0,8},{4,12},{8,16},{12,20},{16,24},{20,28},{24,0},{28,4},{1,9},{5... | collective-permute-start | bytes 1179656 | tf_op jit(solution)/shard_map/ppermute | solution.py:461
  98.6 43.7 %collective-permute-start.16 = (bf16[256,768]{1,0:T(8,128)(2,1)S(1)}, bf16[256,768]{1,0:T(8,128)(2,1)S(1)}, u32[]{:S(2)}, u32[]{:S(2)}) collective-permute-start(bf16[256,768]{1,0:T(8,128)(2,1)S(1)} %copy-done.103), channel_id=1, source_target_pairs={{0,4},{4,0},{8,12},{12,8},{16,20},{20,16},{24,28},{28,24},{1,5},{5... | collective-permute-start | bytes 1179656 | tf_op jit(solution)/shard_map/ppermute | solution.py:444
  139.5 35.7 %collective-permute-start.7 = (bf16[8,64,640]{2,1,0:T(8,128)(2,1)S(1)}, bf16[8,64,640]{2,1,0:T(8,128)(2,1)}, u32[]{:S(2)}, u32[]{:S(2)}) collective-permute-start(bf16[8,64,640]{2,1,0:T(8,128)(2,1)S(1)} %bitcast_dynamic-update-slice_fusion.16), channel_id=1, source_target_pairs={{0,2},{1,3},{2,0},{3,1},{4,6},{5,7},{6,4},{7,5},{8,10},{9,11},{10,... | collective-permute-start | bytes 1966088 | tf_op jit(solution)/shard_map/ppermute | solution.py:444
  153.2 29.1 %all-to-all-start.1 = ((bf16[2,256,704]{1,0,2:T(2,128)(2,1)}), bf16[2,256,704]{1,0,2:T(2,128)(2,1)S(1)}, u32[]{:S(2)}, u32[]{:S(2)}) async-start(bf16[2,256,704]{1,0,2:T(2,128)(2,1)} %copy.335), calls=%async_computation.1 | async-start | bytes 1441792 | tf_op jit(solution)/shard_map/all_to_all | solution.py:714
  177.5 42.9 %collective-permute-start.8 = (bf16[2,8,64,640]{3,2,1,0:T(8,128)(2,1)}, bf16[2,8,64,640]{3,2,1,0:T(8,128)(2,1)}, u32[]{:S(2)}, u32[]{:S(2)}) collective-permute-start(bf16[2,8,64,640]{3,2,1,0:T(8,128)(2,1)} %pad_maximum_fusion.13), channel_id=1, source_target_pairs={{0,1},{1,0},{2,3},{3,2},{4,5},{5,4},{6,7},{7,6},{8,9},{9,8},{10,11... | collective-permute-start | bytes 3932168 | tf_op jit(solution)/shard_map/ppermute | solution.py:444
  209.1 47.3 %collective-permute-start.35 = (bf16[128,2048]{1,0:T(8,128)(2,1)}, bf16[128,2048]{1,0:T(8,128)(2,1)}, u32[]{:S(2)}, u32[]{:S(2)}) collective-permute-start(bf16[128,2048]{1,0:T(8,128)(2,1)} %pad_maximum_fusion.33), channel_id=1, source_target_pairs={{0,2},{1,3},{2,0},{3,1},{4,6},{5,7},{6,4},{7,5},{8,10},{9,11},{10,... | collective-permute-start | bytes 1572872 | tf_op jit(solution)/shard_map/ppermute | solution.py:444
  212.0 42.8 %collective-permute-start.34 = (bf16[128,2048]{1,0:T(8,128)(2,1)}, bf16[128,2048]{1,0:T(8,128)(2,1)}, u32[]{:S(2)}, u32[]{:S(2)}) collective-permute-start(bf16[128,2048]{1,0:T(8,128)(2,1)} %pad_maximum_fusion.32), channel_id=1, source_target_pairs={{0,4},{4,0},{8,12},{12,8},{16,20},{20,16},{24,28},{28,24},{1,5},{5... | collective-permute-start | bytes 1572872 | tf_op jit(solution)/shard_map/ppermute | solution.py:444
  216.1 35.6 %collective-permute-start.39 = (bf16[64,2048]{1,0:T(8,128)(2,1)}, bf16[64,2048]{1,0:T(8,128)(2,1)}, u32[]{:S(2)}, u32[]{:S(2)}) collective-permute-start(bf16[64,2048]{1,0:T(8,128)(2,1)} %get-tuple-element.298), channel_id=1, source_target_pairs={{0,2},{1,3},{2,0},{3,1},{4,6},{5,7},{6,4},{7,5},{8,10},{9,11},{10,... | collective-permute-start | bytes 786440 | tf_op jit(solution)/shard_map/ppermute | solution.py:444
  217.1 33.2 %collective-permute-start.38 = (bf16[64,2048]{1,0:T(8,128)(2,1)}, bf16[64,2048]{1,0:T(8,128)(2,1)}, u32[]{:S(2)}, u32[]{:S(2)}) collective-permute-start(bf16[64,2048]{1,0:T(8,128)(2,1)} %get-tuple-element.299), channel_id=1, source_target_pairs={{0,4},{4,0},{8,12},{12,8},{16,20},{20,16},{24,28},{28,24},{1,5},{5... | collective-permute-start | bytes 786440 | tf_op jit(solution)/shard_map/ppermute | solution.py:444
  220.4 38.0 %collective-permute-start.43 = (bf16[128,2048]{1,0:T(8,128)(2,1)}, bf16[128,2048]{1,0:T(8,128)(2,1)}, u32[]{:S(2)}, u32[]{:S(2)}) collective-permute-start(bf16[128,2048]{1,0:T(8,128)(2,1)} %collective-permute-done.37), channel_id=1, source_target_pairs={{0,8},{4,12},{8,16},{12,20},{16,24},{20,28},{24,0},{28,4},{1,9},{5... | collective-permute-start | bytes 1572872 | tf_op jit(solution)/shard_map/ppermute | solution.py:461
  250.3 51.1 %collective-permute-start.30 = (bf16[2,128,2048]{2,1,0:T(8,128)(2,1)S(1)}, bf16[2,128,2048]{2,1,0:T(8,128)(2,1)S(1)}, u32[]{:S(2)}, u32[]{:S(2)}) collective-permute-start(bf16[2,128,2048]{2,1,0:T(8,128)(2,1)S(1)} %fusion.50), channel_id=1, source_target_pairs={{0,1},{1,0},{2,3},{3,2},{4,5},{5,4},{6,7},{7,6},{8,9},{9,8},{10,11... | collective-permute-start | bytes 3145736 | tf_op jit(solution)/shard_map/ppermute | solution.py:444
  251.6 35.3 %collective-permute-start.41 = (bf16[128,2048]{1,0:T(8,128)(2,1)S(1)}, bf16[128,2048]{1,0:T(8,128)(2,1)S(1)}, u32[]{:S(2)}, u32[]{:S(2)}) collective-permute-start(bf16[128,2048]{1,0:T(8,128)(2,1)S(1)} %pad_maximum_fusion.35), channel_id=1, source_target_pairs={{0,2},{1,3},{2,0},{3,1},{4,6},{5,7},{6,4},{7,5},{8,10},{9,11},{10,... | collective-permute-start | bytes 1572872 | tf_op jit(solution)/shard_map/ppermute | solution.py:444
  254.8 31.1 %collective-permute-start.40 = (bf16[128,2048]{1,0:T(8,128)(2,1)S(1)}, bf16[128,2048]{1,0:T(8,128)(2,1)S(1)}, u32[]{:S(2)}, u32[]{:S(2)}) collective-permute-start(bf16[128,2048]{1,0:T(8,128)(2,1)S(1)} %pad_maximum_fusion.34), channel_id=1, source_target_pairs={{0,4},{4,0},{8,12},{12,8},{16,20},{20,16},{24,28},{28,24},{1,5},{5... | collective-permute-start | bytes 1572872 | tf_op jit(solution)/shard_map/ppermute | solution.py:444
  271.5 67.2 %collective-permute-start.36 = (bf16[512,2048]{1,0:T(8,128)(2,1)S(1)}, bf16[512,2048]{1,0:T(8,128)(2,1)S(1)}, u32[]{:S(2)}, u32[]{:S(2)}) collective-permute-start(bf16[512,2048]{1,0:T(8,128)(2,1)S(1)} %slice_dynamic-update-slice_fusion.12), channel_id=1, source_target_pairs={{0,1},{1,0},{2,3},{3,2},{4,5},{5,4},{6,7},{7,6},{8,9},{9,8},{10,11... | collective-permute-start | bytes 6291464 | tf_op jit(solution)/shard_map/ppermute | solution.py:444
  307.0 31.7 %collective-permute-start.42 = (bf16[512,2048]{1,0:T(8,128)(2,1)S(1)}, bf16[512,2048]{1,0:T(8,128)(2,1)S(1)}, u32[]{:S(2)}, u32[]{:S(2)}) collective-permute-start(bf16[512,2048]{1,0:T(8,128)(2,1)S(1)} %slice_dynamic-update-slice_fusion.8), channel_id=1, source_target_pairs={{0,1},{1,0},{2,3},{3,2},{4,5},{5,4},{6,7},{7,6},{8,9},{9,8},{10,11... | collective-permute-start | bytes 6291464 | tf_op jit(solution)/shard_map/ppermute | solution.py:444
  375.1 60.0 %collective-permute-start.65 = (bf16[512,2048]{1,0:T(8,128)(2,1)S(1)}, bf16[512,2048]{1,0:T(8,128)(2,1)S(1)}, u32[]{:S(2)}, u32[]{:S(2)}) collective-permute-start(bf16[512,2048]{1,0:T(8,128)(2,1)S(1)} %get-tuple-element.282), channel_id=1, source_target_pairs={{0,1},{1,0},{2,3},{3,2},{4,5},{5,4},{6,7},{7,6},{8,9},{9,8},{10,11... | collective-permute-start | bytes 6291464 | tf_op jit(solution)/shard_map/ppermute | solution.py:444
  413.1 90.9 %collective-permute-start.60 = (bf16[512,2048]{1,0:T(8,128)(2,1)}, bf16[512,2048]{1,0:T(8,128)(2,1)}, u32[]{:S(2)}, u32[]{:S(2)}) collective-permute-start(bf16[512,2048]{1,0:T(8,128)(2,1)} %get-tuple-element.288), channel_id=1, source_target_pairs={{0,1},{1,0},{2,3},{3,2},{4,5},{5,4},{6,7},{7,6},{8,9},{9,8},{10,11... | collective-permute-start | bytes 6291464 | tf_op jit(solution)/shard_map/ppermute | solution.py:444
  420.9 156.4 %collective-permute-start.82 = (bf16[512,2048]{1,0:T(8,128)(2,1)}, bf16[512,2048]{1,0:T(8,128)(2,1)}, u32[]{:S(2)}, u32[]{:S(2)}) collective-permute-start(bf16[512,2048]{1,0:T(8,128)(2,1)} %get-tuple-element.270), channel_id=1, source_target_pairs={{0,1},{1,0},{2,3},{3,2},{4,5},{5,4},{6,7},{7,6},{8,9},{9,8},{10,11... | collective-permute-start | bytes 6291464 | tf_op jit(solution)/shard_map/ppermute | solution.py:444
  432.2 229.5 %collective-permute-start.77 = (bf16[512,2048]{1,0:T(8,128)(2,1)}, bf16[512,2048]{1,0:T(8,128)(2,1)}, u32[]{:S(2)}, u32[]{:S(2)}) collective-permute-start(bf16[512,2048]{1,0:T(8,128)(2,1)} %get-tuple-element.276), channel_id=1, source_target_pairs={{0,1},{1,0},{2,3},{3,2},{4,5},{5,4},{6,7},{7,6},{8,9},{9,8},{10,11... | collective-permute-start | bytes 6291464 | tf_op jit(solution)/shard_map/ppermute | solution.py:444
  558.2 281.3 %collective-permute-start.66 = (bf16[2,2,2,64,2048]{4,3,0,1,2:T(8,128)(2,1)}, bf16[2,2,2,64,2048]{4,3,0,1,2:T(8,128)(2,1)}, u32[]{:S(2)}, u32[]{:S(2)}) collective-permute-start(bf16[2,2,2,64,2048]{4,3,0,1,2:T(8,128)(2,1)} %copy.338), channel_id=1, source_target_pairs={{0,1},{1,0},{2,3},{3,2},{4,5},{5,4},{6,7},{7,6},{8,9},{9,8},{10,11... | collective-permute-start | bytes 6291464 | tf_op jit(solution)/shard_map/ppermute | solution.py:444
  562.9 280.9 %collective-permute-start.103 = (bf16[2,2,2,64,2048]{4,3,0,1,2:T(8,128)(2,1)}, bf16[2,2,2,64,2048]{4,3,0,1,2:T(8,128)(2,1)}, u32[]{:S(2)}, u32[]{:S(2)}) collective-permute-start(bf16[2,2,2,64,2048]{4,3,0,1,2:T(8,128)(2,1)} %copy.359), channel_id=1, source_target_pairs={{0,1},{1,0},{2,3},{3,2},{4,5},{5,4},{6,7},{7,6},{8,9},{9,8},{10,11... | collective-permute-start | bytes 6291464 | tf_op jit(solution)/shard_map/ppermute | solution.py:444
  641.8 243.1 %collective-permute-start.93 = (bf16[2,2,2,64,2048]{4,3,0,1,2:T(8,128)(2,1)}, bf16[2,2,2,64,2048]{4,3,0,1,2:T(8,128)(2,1)}, u32[]{:S(2)}, u32[]{:S(2)}) collective-permute-start(bf16[2,2,2,64,2048]{4,3,0,1,2:T(8,128)(2,1)} %copy.356), channel_id=1, source_target_pairs={{0,1},{1,0},{2,3},{3,2},{4,5},{5,4},{6,7},{7,6},{8,9},{9,8},{10,11... | collective-permute-start | bytes 6291464 | tf_op jit(solution)/shard_map/ppermute | solution.py:444
  646.3 242.4 %collective-permute-start.118 = (bf16[2,2,2,64,2048]{4,3,0,1,2:T(8,128)(2,1)}, bf16[2,2,2,64,2048]{4,3,0,1,2:T(8,128)(2,1)}, u32[]{:S(2)}, u32[]{:S(2)}) collective-permute-start(bf16[2,2,2,64,2048]{4,3,0,1,2:T(8,128)(2,1)} %copy.368), channel_id=1, source_target_pairs={{0,1},{1,0},{2,3},{3,2},{4,5},{5,4},{6,7},{7,6},{8,9},{9,8},{10,11... | collective-permute-start | bytes 6291464 | tf_op jit(solution)/shard_map/ppermute | solution.py:444
  737.2 58.2 %collective-permute-start.126 = (f32[4,2,2,2,128]{4,3,0,1,2:T(2,128)S(1)}, f32[4,2,2,2,128]{4,3,0,1,2:T(2,128)S(1)}, u32[]{:S(2)}, u32[]{:S(2)}) collective-permute-start(f32[4,2,2,2,128]{4,3,0,1,2:T(2,128)S(1)} %slice_bitcast_fusion.68), channel_id=1, source_target_pairs={{0,1},{1,0},{2,3},{3,2},{4,5},{5,4},{6,7},{7,6},{8,9},{9,8},{10,11... | collective-permute-start | bytes 49160 | tf_op jit(solution)/shard_map/ppermute | solution.py:444
  800.9 142.2 %collective-permute-start.88 = (bf16[2,2,2,64,2048]{4,3,0,1,2:T(8,128)(2,1)}, bf16[2,2,2,64,2048]{4,3,0,1,2:T(8,128)(2,1)}, u32[]{:S(2)}, u32[]{:S(2)}) collective-permute-start(bf16[2,2,2,64,2048]{4,3,0,1,2:T(8,128)(2,1)} %copy.353), channel_id=1, source_target_pairs={{0,1},{1,0},{2,3},{3,2},{4,5},{5,4},{6,7},{7,6},{8,9},{9,8},{10,11... | collective-permute-start | bytes 6291464 | tf_op jit(solution)/shard_map/ppermute | solution.py:444
  834.3 29.8 %all-to-all-start.3 = ((bf16[2,2048,88]{2,0,1:T(2,128)(2,1)}), bf16[2,2048,88]{2,0,1:T(2,128)(2,1)}, u32[]{:S(2)}, u32[]{:S(2)}) async-start(bf16[2,2048,88]{2,0,1:T(2,128)(2,1)} %copy.379), calls=%async_computation.3 | async-start | bytes 2097152 | tf_op jit(solution)/shard_map/all_to_all | solution.py:999
  839.5 108.3 %collective-permute-start.113 = (bf16[2,2,2,64,2048]{4,3,0,1,2:T(8,128)(2,1)}, bf16[2,2,2,64,2048]{4,3,0,1,2:T(8,128)(2,1)}, u32[]{:S(2)}, u32[]{:S(2)}) collective-permute-start(bf16[2,2,2,64,2048]{4,3,0,1,2:T(8,128)(2,1)} %copy.365), channel_id=1, source_target_pairs={{0,1},{1,0},{2,3},{3,2},{4,5},{5,4},{6,7},{7,6},{8,9},{9,8},{10,11... | collective-permute-start | bytes 6291464 | tf_op jit(solution)/shard_map/ppermute | solution.py:444
  843.8 28.2 %collective-permute-start.67 = (bf16[2,64,2048]{2,1,0:T(8,128)(2,1)}, bf16[2,64,2048]{2,1,0:T(8,128)(2,1)}, u32[]{:S(2)}, u32[]{:S(2)}) collective-permute-start(bf16[2,64,2048]{2,1,0:T(8,128)(2,1)} %fusion.81), channel_id=1, source_target_pairs={{0,2},{1,3},{2,0},{3,1},{4,6},{5,7},{6,4},{7,5},{8,10},{9,11},{10,... | collective-permute-start | bytes 1572872 | tf_op jit(solution)/shard_map/ppermute | solution.py:444
  884.7 67.5 %collective-permute-start.83 = (bf16[2,2,2,64,2048]{4,3,0,1,2:T(8,128)(2,1)}, bf16[2,2,2,64,2048]{4,3,0,1,2:T(8,128)(2,1)S(1)}, u32[]{:S(2)}, u32[]{:S(2)}) collective-permute-start(bf16[2,2,2,64,2048]{4,3,0,1,2:T(8,128)(2,1)} %copy.350), channel_id=1, source_target_pairs={{0,1},{1,0},{2,3},{3,2},{4,5},{5,4},{6,7},{7,6},{8,9},{9,8},{10,11... | collective-permute-start | bytes 6291464 | tf_op jit(solution)/shard_map/ppermute | solution.py:444
  970.0 30.7 %collective-permute-start.84 = (bf16[2,64,2048]{2,1,0:T(8,128)(2,1)S(1)}, bf16[2,64,2048]{2,1,0:T(8,128)(2,1)S(1)}, u32[]{:S(2)}, u32[]{:S(2)}) collective-permute-start(bf16[2,64,2048]{2,1,0:T(8,128)(2,1)S(1)} %fusion.83), channel_id=1, source_target_pairs={{0,2},{1,3},{2,0},{3,1},{4,6},{5,7},{6,4},{7,5},{8,10},{9,11},{10,... | collective-permute-start | bytes 1572872 | tf_op jit(solution)/shard_map/ppermute | solution.py:444
  978.3 31.4 %collective-permute-start.86 = (bf16[2,64,2048]{2,1,0:T(8,128)(2,1)S(1)}, bf16[2,64,2048]{2,1,0:T(8,128)(2,1)S(1)}, u32[]{:S(2)}, u32[]{:S(2)}) collective-permute-start(bf16[2,64,2048]{2,1,0:T(8,128)(2,1)S(1)} %fusion.84), channel_id=1, source_target_pairs={{0,4},{4,0},{8,12},{12,8},{16,20},{20,16},{24,28},{28,24},{1,5},{5... | collective-permute-start | bytes 1572872 | tf_op jit(solution)/shard_map/ppermute | solution.py:444
  991.4 79.7 %collective-permute-start.98 = (bf16[128,2048]{1,0:T(8,128)(2,1)S(1)}, bf16[128,2048]{1,0:T(8,128)(2,1)S(1)}, u32[]{:S(2)}, u32[]{:S(2)}) collective-permute-start(bf16[128,2048]{1,0:T(8,128)(2,1)S(1)} %pad_maximum_fusion.48), channel_id=1, source_target_pairs={{0,8},{4,12},{8,16},{12,20},{16,24},{20,28},{24,0},{28,4},{1,9},{5... | collective-permute-start | bytes 1572872 | tf_op jit(solution)/shard_map/ppermute | solution.py:461
  1000.8 28.8 %collective-permute-start.123 = (bf16[128,2048]{1,0:T(8,128)(2,1)S(1)}, bf16[128,2048]{1,0:T(8,128)(2,1)S(1)}, u32[]{:S(2)}, u32[]{:S(2)}) collective-permute-start(bf16[128,2048]{1,0:T(8,128)(2,1)S(1)} %pad_maximum_fusion.49), channel_id=1, source_target_pairs={{0,8},{4,12},{8,16},{12,20},{16,24},{20,28},{24,0},{28,4},{1,9},{5... | collective-permute-start | bytes 1572872 | tf_op jit(solution)/shard_map/ppermute | solution.py:461
  1006.7 47.3 %collective-permute-start.90 = (bf16[64,2048]{1,0:T(8,128)(2,1)S(1)}, bf16[64,2048]{1,0:T(8,128)(2,1)S(1)}, u32[]{:S(2)}, u32[]{:S(2)}) collective-permute-start(bf16[64,2048]{1,0:T(8,128)(2,1)S(1)} %fusion.127), channel_id=1, source_target_pairs={{0,4},{4,0},{8,12},{12,8},{16,20},{20,16},{24,28},{28,24},{1,5},{5... | collective-permute-start | bytes 786440 | tf_op jit(solution)/shard_map/ppermute | solution.py:444
  1009.7 61.3 %collective-permute-start.92 = (bf16[64,2048]{1,0:T(8,128)(2,1)S(1)}, bf16[64,2048]{1,0:T(8,128)(2,1)S(1)}, u32[]{:S(2)}, u32[]{:S(2)}) collective-permute-start(bf16[64,2048]{1,0:T(8,128)(2,1)S(1)} %fusion.128), channel_id=1, source_target_pairs={{0,2},{1,3},{2,0},{3,1},{4,6},{5,7},{6,4},{7,5},{8,10},{9,11},{10,... | collective-permute-start | bytes 786440 | tf_op jit(solution)/shard_map/ppermute | solution.py:444
  1038.0 41.2 %collective-permute-start.85 = (bf16[64,2048]{1,0:T(8,128)(2,1)S(1)}, bf16[64,2048]{1,0:T(8,128)(2,1)S(1)}, u32[]{:S(2)}, u32[]{:S(2)}) collective-permute-start(bf16[64,2048]{1,0:T(8,128)(2,1)S(1)} %fusion.125), channel_id=1, source_target_pairs={{0,4},{4,0},{8,12},{12,8},{16,20},{20,16},{24,28},{28,24},{1,5},{5... | collective-permute-start | bytes 786440 | tf_op jit(solution)/shard_map/ppermute | solution.py:444
  1110.5 37.0 %collective-permute-start.162 = (bf16[512,256]{1,0:T(8,128)(2,1)}, bf16[512,256]{1,0:T(8,128)(2,1)}, u32[]{:S(2)}, u32[]{:S(2)}) collective-permute-start(bf16[512,256]{1,0:T(8,128)(2,1)} %get-tuple-element.199), channel_id=1, source_target_pairs={{0,4},{4,0},{8,12},{12,8},{16,20},{20,16},{24,28},{28,24},{1,5},{5... | collective-permute-start | bytes 786440 | tf_op jit(solution)/shard_map/ppermute | solution.py:444
  1110.5 52.8 %collective-permute-start.161 = (bf16[512,256]{1,0:T(8,128)(2,1)}, bf16[512,256]{1,0:T(8,128)(2,1)}, u32[]{:S(2)}, u32[]{:S(2)}) collective-permute-start(bf16[512,256]{1,0:T(8,128)(2,1)} %get-tuple-element.200), channel_id=1, source_target_pairs={{0,4},{4,0},{8,12},{12,8},{16,20},{20,16},{24,28},{28,24},{1,5},{5... | collective-permute-start | bytes 786440 | tf_op jit(solution)/shard_map/ppermute | solution.py:444
  1112.8 60.0 %collective-permute-start.160 = (bf16[512,256]{1,0:T(8,128)(2,1)}, bf16[512,256]{1,0:T(8,128)(2,1)}, u32[]{:S(2)}, u32[]{:S(2)}) collective-permute-start(bf16[512,256]{1,0:T(8,128)(2,1)} %get-tuple-element.201), channel_id=1, source_target_pairs={{0,4},{4,0},{8,12},{12,8},{16,20},{20,16},{24,28},{28,24},{1,5},{5... | collective-permute-start | bytes 786440 | tf_op jit(solution)/shard_map/ppermute | solution.py:444
  1119.4 29.3 %collective-permute-start.154 = (bf16[64,1024]{1,0:T(8,128)(2,1)}, bf16[64,1024]{1,0:T(8,128)(2,1)}, u32[]{:S(2)}, u32[]{:S(2)}) collective-permute-start(bf16[64,1024]{1,0:T(8,128)(2,1)} %get-tuple-element.230), channel_id=1, source_target_pairs={{0,4},{4,0},{8,12},{12,8},{16,20},{20,16},{24,28},{28,24},{1,5},{5... | collective-permute-start | bytes 393224 | tf_op jit(solution)/shard_map/ppermute | solution.py:444
  1190.5 33.4 %collective-permute-start.100 = (bf16[128,2048]{1,0:T(8,128)(2,1)S(1)}, bf16[128,2048]{1,0:T(8,128)(2,1)S(1)}, u32[]{:S(2)}, u32[]{:S(2)}) collective-permute-start(bf16[128,2048]{1,0:T(8,128)(2,1)S(1)} %copy-done.102), channel_id=1, source_target_pairs={{0,8},{4,12},{8,16},{12,20},{16,24},{20,28},{24,0},{28,4},{1,9},{5... | collective-permute-start | bytes 1572872 | tf_op jit(solution)/shard_map/ppermute | solution.py:461
  1198.6 34.1 %collective-permute-start.145 = (bf16[256,768]{1,0:T(8,128)(2,1)S(1)}, bf16[256,768]{1,0:T(8,128)(2,1)S(1)}, u32[]{:S(2)}, u32[]{:S(2)}) collective-permute-start(bf16[256,768]{1,0:T(8,128)(2,1)S(1)} %get-tuple-element.194), channel_id=1, source_target_pairs={{0,4},{4,0},{8,12},{12,8},{16,20},{20,16},{24,28},{28,24},{1,5},{5... | collective-permute-start | bytes 1179656 | tf_op jit(solution)/shard_map/ppermute | solution.py:444
  (298 other events, 4183.2 us)

commit v3 on v2

--- a/solution.py
+++ b/solution.py
@@ -465,61 +465,89 @@
     return values.astype(jnp.bfloat16)
 
 
-def plane_gather(own):
+class Flow:
+    def __init__(self):
+        self.tasks = []
+
+    def launch(self, steps):
+        task = Task(steps)
+        self.tasks.append(task)
+        return task
+
+    def close(self, values):
+        live = [task for task in self.tasks if not task.done]
+        values, arrived = lax.optimization_barrier((values, [task.sent for task in live]))
+        for task, got in zip(live, arrived):
+            task.advance(got)
+        return values
+
+
+class Task:
+    def __init__(self, steps):
+        self.steps, self.done, self.result = steps, False, None
+        self.advance(None)
+
+    def advance(self, got):
+        try:
+            self.sent = self.steps.send(got)
+        except StopIteration as stop:
+            self.done, self.result = True, stop.value
+
+
+def held(values, count):
+    for _ in range(count):
+        (values,) = yield [values]
+    return values
+
+
+def passing(values):
+    (got,) = yield [z_hop(values)]
+    return got
+
+
+def plane_gather_split(own):
     half = own.shape[0] // 2
     first, second = own[:half], own[half:]
-    first_x = x_hop(first)
-    second_y = y_hop(second)
+    first_x, second_y = yield [x_hop(first), y_hop(second)]
     first_pair = jnp.concatenate([first, first_x])
     second_pair = jnp.concatenate([second, second_y])
-    first_y = y_hop(first_pair)
-    second_x = x_hop(second_pair)
-    parts = [
-        first,
-        second,
-        first_x,
-        second_x[:half],
-        first_y[:half],
-        second_y,
-        first_y[half:],
-        second_x[half:],
-    ]
-    quarter = jnp.concatenate(parts)
-    return quarter, core_hop(quarter)
-
-
-def slice_gather(own):
-    chunks = []
-    piece = own
-    planes = lax.axis_size("dp") // 2
-    for step in range(planes):
-        chunks.append(plane_gather(piece))
-        if step + 1 < planes:
-            piece = z_hop(piece)
-    return chunks
-
-
-def plane_scatter(part):
-    received = core_hop(part[1])
-    total = part[0].astype(jnp.float32) + received.astype(jnp.float32)
-    first, second = total[:, :, 0], total[:, :, 1]
-    first_in = y_hop(low(first[1])).astype(jnp.float32)
-    second_in = x_hop(low(second[:, 1])).astype(jnp.float32)
-    first_near = first[0] + first_in
-    second_near = second[:, 0] + second_in
-    first_in = x_hop(low(first_near[1])).astype(jnp.float32)
-    second_in = y_hop(low(second_near[1])).astype(jnp.float32)
-    return jnp.concatenate([first_near[0] + first_in, second_near[0] + second_in])
-
-
-def slice_scatter(parts):
-    own = parts[0].shape[0] // 8
-    width = parts[0].shape[1]
-    pieces = [plane_scatter(part.reshape(2, 2, 2, 2, own // 2, width)) for part in parts]
-    moving = pieces[1]
-    for piece in pieces[2:] + pieces[:1]:
-        moving = piece + z_hop(low(moving)).astype(jnp.float32)
-    return moving
+    first_y, second_x = yield [y_hop(first_pair), x_hop(second_pair)]
+    quarter = jnp.concatenate(
+        [
+            own,
+            first_x,
+            second_x[:half],
+            first_y[:half],
+            second_y,
+            first_y[half:],
+            second_x[half:],
+        ]
+    )
+    (far,) = yield [core_hop(quarter)]
+    return jnp.concatenate([quarter, far])
+
+
+def plane_gather(own, before=0):
+    (far,) = yield [x_hop(own)]
+    far = yield from held(far, before)
+    pair = jnp.concatenate([own, far])
+    (far,) = yield [y_hop(pair)]
+    quarter = jnp.concatenate([pair, far])
+    (far,) = yield [core_hop(quarter)]
+    return jnp.concatenate([quarter, far])
+
+
+def plane_scatter(part, x_first, before=0, between=0):
+    part = part.reshape(2, 2, 2, part.shape[0] // 8, part.shape[1])
+    (far,) = yield [core_hop(part[1])]
+    far = yield from held(far, before)
+    total = part[0].astype(jnp.float32) + far.astype(jnp.float32)
+    near, away = (total[:, 0], total[:, 1]) if x_first else (total[0], total[1])
+    (far,) = yield [x_hop(low(away)) if x_first else y_hop(low(away))]
+    far = yield from held(far, between)
+    near = near + far.astype(jnp.float32)
+    (far,) = yield [y_hop(low(near[1])) if x_first else x_hop(low(near[1]))]
+    return near[0] + far.astype(jnp.float32)
 
 
 def tensor_scatter(values, tensor_index):
@@ -551,43 +579,85 @@
     )
 
 
-def dp_gather(own, dp_index, axis):
+def laid_out(arrived, axes, dp_index):
+    planes = len(arrived[0]) // 2
+    plane = dp_index // 2
+    side = dp_index % 2
+    wholes = []
+    for pieces, axis in zip(arrived, axes):
+        extent = pieces[0].shape[axis]
+        shape = list(pieces[0].shape)
+        shape[axis] *= 2 * planes
+        whole = jnp.zeros(shape, pieces[0].dtype)
+        for k, piece in enumerate(pieces):
+            home = (plane - k // 2) % planes * 2 + (side if k % 2 == 0 else 1 - side)
+            whole = lax.dynamic_update_slice_in_dim(whole, piece, home * extent, axis)
+        wholes.append(whole)
+    return wholes
+
+
+def dp_ring(pieces, axes, dp_index):
+    planes = lax.axis_size("dp") // 2
+    arrived = [[] for _ in axes]
+    for step in range(planes):
+        sent = [x_hop(piece) for piece in pieces]
+        if step + 1 < planes:
+            sent += [z_hop(piece) for piece in pieces]
+        got = yield sent
+        for i in range(len(axes)):
+            arrived[i] += [pieces[i], got[i]]
+        pieces = got[len(axes) :]
+    return laid_out(arrived, axes, dp_index)
+
+
+def side_ring(own, dp_index, tensor_index):
+    steps = dp_ring([own], [1], dp_index)
+    sent = next(steps)
+    while True:
+        try:
+            sent = steps.send(sent)
+        except StopIteration as stop:
+            (whole,) = stop.value
+            break
+    (far,) = yield [y_hop(whole)]
+    pair = jnp.stack([whole, far])
+    (far,) = yield [core_hop(pair)]
+    core = tensor_index % 2
+    level = tensor_index // 2
+    even = jnp.where(core == 0, pair, far)
+    odd = jnp.where(core == 0, far, pair)
+    near = jnp.stack([even, odd], axis=1)
+    whole = jnp.where(level == 0, near, near[::-1])
+    return whole.reshape((4 * own.shape[0],) + whole.shape[3:])
+
+
+def dp_scatter_steps(block, dp_index):
     planes = lax.axis_size("dp") // 2
     plane = dp_index // 2
     side = dp_index % 2
-    if axis == 0:
-        whole = jnp.zeros((2 * planes,) + own.shape, own.dtype)
-    else:
-        whole = jnp.zeros(own.shape[:-1] + (2 * planes * own.shape[-1],), own.dtype)
-
-    def place(whole, piece, index):
-        if axis == 0:
-            return lax.dynamic_update_index_in_dim(whole, piece, index, 0)
-        return lax.dynamic_update_slice_in_dim(whole, piece, index * piece.shape[-1], 1)
-
-    piece = own
-    for step in range(planes):
-        base = (plane - step) % planes * 2
-        whole = place(whole, piece, base + side)
-        whole = place(whole, x_hop(piece), base + 1 - side)
-        if step + 1 < planes:
-            piece = z_hop(piece)
-    return whole
-
-
-def dp_scatter(block, dp_index):
-    planes = lax.axis_size("dp") // 2
-    plane = dp_index // 2
-    side = dp_index % 2
+    bases = [(plane - step) % planes * 2 for step in list(range(1, planes)) + [0]]
+    half = len(bases) // 2
+    away = [low(block(base + 1 - side)) for base in bases]
+    first, second = yield [x_hop(jnp.stack(away[:half])), x_hop(jnp.stack(away[half:]))]
+    received = [first[i] for i in range(half)] + [second[i] for i in range(len(bases) - half)]
     moving = None
-    for step in list(range(1, planes)) + [0]:
-        base = (plane - step) % planes * 2
-        received = x_hop(low(block(base + 1 - side))).astype(jnp.float32)
-        piece = block(base + side) + received
+    for base, far in zip(bases, received):
+        piece = block(base + side) + far.astype(jnp.float32)
         if moving is not None:
-            piece = piece + z_hop(low(moving)).astype(jnp.float32)
+            (got,) = yield [z_hop(low(moving))]
+            piece = piece + got.astype(jnp.float32)
         moving = piece
     return moving
+
+
+def drained(task):
+    while not task.done:
+        task.advance(task.sent)
+    return task.result
+
+
+def dp_scatter(block, dp_index):
+    return drained(Task(dp_scatter_steps(block, dp_index)))
 
 
 def padded(values, axis, size):
@@ -637,46 +707,6 @@
 
     lat_width = w_latent.shape[1]
     lat_block = w_latent.shape[0]
-    lat_rows = lat_block // tensor_size
-    side = jnp.concatenate(
-        [
-            w_latent,
-            w_router,
-            gain_attn[:, None],
-            gain_ffn[:, None],
-            padded(gain_latent, 0, lat_block)[:, None],
-        ],
-        axis=1,
-    )
-    side_width = lanes(side.shape[1])
-    side = padded(
-        lax.dynamic_slice_in_dim(side, tensor_index * lat_rows, lat_rows, 0), 1, side_width
-    )
-    side_all = dp_gather(side, dp_index, 0)
-    side_pair = jnp.stack([side_all, y_hop(side_all)])
-    side_far = core_hop(side_pair)
-    core = tensor_index % 2
-    level = tensor_index // 2
-    side_even = jnp.where(core == 0, side_pair, side_far)
-    side_odd = jnp.where(core == 0, side_far, side_pair)
-    side_near = jnp.stack([side_even, side_odd], axis=1)
-    side_all = jnp.where(level == 0, side_near, side_near[::-1]).reshape(
-        tensor_size, dp_size, lat_rows, side_width
-    )
-    side_all = side_all.transpose(1, 0, 2, 3).reshape(width, side_width)
-    latent_weight = side_all[:, :lat_width]
-    router_weight = side_all[:, lat_width : lat_width + experts]
-    gains_all = side_all[:, lat_width + experts : lat_width + experts + 3].astype(jnp.float32).T
-    gain_attn_f = gains_all[0]
-    gain_ffn_f = gains_all[1]
-    gain_latent_f = gains_all[2].reshape(dp_size, lat_block)[:, : gain_latent.shape[0]].reshape(
-        KV_RANK
-    )
-
-    query_weight = dp_gather(w_query, dp_index, 0).reshape(width, w_query.shape[1])
-    expand_weight = dp_gather(w_expand, dp_index, 0).reshape(KV_RANK, w_expand.shape[1])
-    output_weight = dp_gather(w_output, dp_index, 1).reshape(w_output.shape[0], width)
-
     routed = jnp.sum(
         (routes[:, :, None] == jnp.arange(experts, dtype=jnp.int32)[None, None, :]).astype(
             jnp.float32
@@ -688,12 +718,53 @@
     rank = jnp.dot(earlier, low(routed), preferred_element_type=jnp.float32)
     standing = routed * (1.0 + (rank < capacity).astype(jnp.float32))
     standing_own = own_rows(standing)
-    marks_all = lax.all_gather(low(standing), "dp", axis=0, tiled=True)
     cot_own = own_rows(cotangent)
-    cot_sent, _ = lax.optimization_barrier((cot_own, query_weight))
-    cot_chunks = slice_gather(cot_sent)
+
+    folds = tok_count // lat_block
+    mark_start = lat_width + experts
+    gain_start = mark_start + folds * experts
+    side_rows = lanes(gain_start + 3)
+    side = jnp.concatenate(
+        [w_latent.T, w_router.T]
+        + [
+            low(standing[fold * lat_block : (fold + 1) * lat_block]).T
+            for fold in range(folds)
+        ]
+        + [jnp.stack([gain_attn, gain_ffn, padded(gain_latent, 0, lat_block)])]
+    )
+    side_rows_here = side_rows // tensor_size
+    side = lax.dynamic_slice_in_dim(
+        padded(side, 0, side_rows), tensor_index * side_rows_here, side_rows_here, 0
+    )
+
+    flow = Flow()
+    side_task = flow.launch(side_ring(side, dp_index, tensor_index))
+    unit = w_output.shape[1]
+    query_rows = w_query.shape[0] * w_query.shape[1] // unit
+    expand_rows = w_expand.shape[0] * w_expand.shape[1] // unit
+
+    def columns(values):
+        return [values[:, i : i + unit] for i in range(0, values.shape[1], unit)]
+
+    pack = jnp.concatenate(columns(w_query) + columns(w_expand) + [w_output])
+    weight_task = flow.launch(dp_ring([pack], [0], dp_index))
+    for _ in range(2):
+        flow.close(())
+
+    core = tensor_index % 2
+    level = tensor_index // 2
     planes = dp_size // 2
-    marks_all = marks_all.reshape(planes, 8, own_count, experts)
+    side_all = side_task.result
+    latent_weight = side_all[:lat_width]
+    router_weight = side_all[lat_width:mark_start]
+    marks_all = side_all[mark_start:gain_start].reshape(folds, experts, dp_size, lat_block)
+    marks_all = marks_all.transpose(2, 0, 3, 1).reshape(planes, 8, own_count, experts)
+    gains_all = side_all[gain_start : gain_start + 3].astype(jnp.float32)
+    gain_attn_f = gains_all[0]
+    gain_ffn_f = gains_all[1]
+    gain_latent_f = gains_all[2].reshape(dp_size, lat_block)[:, : gain_latent.shape[0]].reshape(
+        KV_RANK
+    )
     near = jnp.arange(8, dtype=jnp.int32)
     near_x = near % 2 ^ dp_index % 2
     near_y = near // 2 % 2 ^ level
@@ -709,32 +780,43 @@
         ).reshape(8 * own_count, experts)
         for step in range(planes)
     ]
-
-    shared_here = w_shared_gate.shape[1] // dp_size
-    shared_in = lax.all_to_all(
-        jnp.stack([w_shared_gate, w_shared_up]), "dp", split_axis=2, concat_axis=1, tiled=True
-    )
-    shared_out = lax.all_to_all(w_shared_down, "dp", split_axis=0, concat_axis=1, tiled=True)
-    group = w_gate.shape[2]
-    group_lanes = lanes(group)
-    shared_lanes = lanes(shared_here)
-
-    def joined(routed_weight, shared_weight, axis):
-        pieces = [padded(routed_weight[e], axis, group_lanes) for e in range(exp_here)]
-        return jnp.concatenate(pieces + [padded(shared_weight, axis, shared_lanes)], axis=axis)
-
-    gate_weight = joined(w_gate, shared_in[0], 1)
-    up_weight = joined(w_up, shared_in[1], 1)
-    down_weight = joined(w_down, shared_out, 0)
-    hidden = gate_weight.shape[1]
+    flow.close(())
+    cot_pass = flow.launch(passing(cot_own))
 
     head_width = QK_NOPE + QK_ROPE
-    heads_here = query_weight.shape[1] // head_width
+    heads_here = w_query.shape[1] // head_width
     softmax_scale = head_width ** (-0.5)
     resid_in = tokens.astype(jnp.float32)
     normed_attn, inverse_attn = norm_forward(resid_in, gain_attn_f)
     normed_attn_low = low(normed_attn)
     cosine, sine_part = rope_tables(positions, QK_ROPE)
+    latent_raw = jnp.einsum(
+        "td,cd->tc", normed_attn_low, latent_weight, preferred_element_type=jnp.float32
+    )
+    latent_part = latent_raw[:, :KV_RANK]
+    latent_normed, inverse_latent = norm_forward(latent_part, gain_latent_f)
+    latent_low = low(latent_normed)
+    key_rope_low = low(rotate(latent_raw[:, KV_RANK:], cosine, sine_part))
+    normed_attn_low, latent_low, key_rope_low, w_shared_gate, w_shared_up, w_shared_down = (
+        flow.close(
+            (normed_attn_low, latent_low, key_rope_low, w_shared_gate, w_shared_up, w_shared_down)
+        )
+    )
+
+    (packed,) = weight_task.result
+    packed = packed.reshape(dp_size, pack.shape[0], unit)
+
+    def rejoined(values, rows):
+        values = values.reshape(dp_size, -1, rows, unit).transpose(0, 2, 1, 3)
+        return values.reshape(dp_size * rows, -1)
+
+    query_weight = rejoined(packed[:, :query_rows], w_query.shape[0])
+    expand_weight = rejoined(packed[:, query_rows : query_rows + expand_rows], w_expand.shape[0])
+    output_weight = packed[:, query_rows + expand_rows :].transpose(1, 0, 2)
+    output_weight = output_weight.reshape(w_output.shape[0], width)
+    cot_tasks = [flow.launch(plane_gather(cot_own))]
+    cot_piece = cot_pass.result
+    cot_pass = flow.launch(passing(cot_piece))
     query_raw = jnp.dot(normed_attn_low, query_weight, preferred_element_type=jnp.float32).reshape(
         tok_count, heads_here, head_width
     )
@@ -747,14 +829,13 @@
             axis=-1,
         )
     )
-    latent_raw = jnp.dot(normed_attn_low, latent_weight, preferred_element_type=jnp.float32)
-    latent_part = latent_raw[:, :KV_RANK]
-    latent_normed, inverse_latent = norm_forward(latent_part, gain_latent_f)
-    latent_low = low(latent_normed)
-    key_rope_low = low(rotate(latent_raw[:, KV_RANK:], cosine, sine_part))
-    expanded = low(
-        jnp.dot(latent_low, expand_weight, preferred_element_type=jnp.float32)
-    ).reshape(tok_count, heads_here, QK_NOPE + V_HEAD)
+    expanded = low(jnp.dot(latent_low, expand_weight, preferred_element_type=jnp.float32))
+    query_low, expanded = flow.close((query_low, expanded))
+
+    cot_tasks.append(flow.launch(plane_gather(cot_piece, 4)))
+    cot_piece = cot_pass.result
+    cot_pass = flow.launch(passing(cot_piece))
+    expanded = expanded.reshape(tok_count, heads_here, QK_NOPE + V_HEAD)
     value_low = expanded[..., QK_NOPE:]
     key_full = jnp.concatenate(
         [
@@ -773,16 +854,38 @@
         jnp.einsum("hqk,khc->qhc", probs_low, value_low, preferred_element_type=jnp.float32)
     ).reshape(tok_count, heads_here * V_HEAD)
     attn_part = jnp.dot(heads_low, output_weight, preferred_element_type=jnp.float32)
-
+    attn_part = flow.close(attn_part)
+
+    cot_tasks.append(flow.launch(plane_gather(cot_piece, 6)))
+    cot_piece = cot_pass.result
     resid_own = own_rows(tokens).astype(jnp.float32) + tensor_scatter(attn_part, tensor_index)
     normed_own, inverse_own = norm_forward(resid_own, gain_ffn_f)
-    normed_own_low = low(normed_own)
-    rows_sent, cot_chunks = lax.optimization_barrier((normed_own_low, cot_chunks))
-    row_chunks = slice_gather(rows_sent)
+    normed_own_low = flow.close(low(normed_own))
+
+    row_tasks = [flow.launch(plane_gather_split(normed_own_low))]
+    row_pass = flow.launch(passing(normed_own_low))
+    shared_here = w_shared_gate.shape[1] // dp_size
+    shared = lax.all_to_all(
+        jnp.stack([w_shared_gate.T, w_shared_up.T, w_shared_down]),
+        "dp",
+        split_axis=1,
+        concat_axis=2,
+        tiled=True,
+    )
+    group = w_gate.shape[2]
+    routed_here = exp_here * group
+    hidden = routed_here + shared_here
+    gate_weight = jnp.concatenate([w_gate.swapaxes(1, 2).reshape(routed_here, width), shared[0]])
+    up_weight = jnp.concatenate([w_up.swapaxes(1, 2).reshape(routed_here, width), shared[1]])
+    down_weight = jnp.concatenate([w_down.reshape(routed_here, width), shared[2]])
+    gate_weight, up_weight, down_weight = flow.close((gate_weight, up_weight, down_weight))
+    for _ in range(2):
+        flow.close(())
 
     def gating(rows, standing_rows):
         probs = jax.nn.softmax(
-            jnp.dot(rows, router_weight, preferred_element_type=jnp.float32), axis=-1
+            jnp.einsum("td,ed->te", rows, router_weight, preferred_element_type=jnp.float32),
+            axis=-1,
         )
         gates = jnp.where(standing_rows > 0.5, probs, 0.0)
         picked = jnp.sum(gates, axis=-1, keepdims=True)
@@ -790,14 +893,26 @@
 
     expert_index = jnp.arange(experts, dtype=jnp.int32)[None, :]
     column = jnp.arange(hidden, dtype=jnp.int32)[None, :]
-    out_parts, in_parts, gate_parts, kept_parts = [], [], [], []
+    row_piece = row_pass.result
+    in_tasks, out_tasks, gate_parts, kept_parts = [], [], [], []
+    in_part = None
     for step in range(planes):
-        rows = jnp.concatenate(row_chunks[step])
-        cots = jnp.concatenate(cot_chunks[step])
+        rows = row_tasks[step].result
+        if step + 1 < planes:
+            row_tasks.append(flow.launch(plane_gather(row_piece)))
+            if step + 2 < planes:
+                row_pass = flow.launch(passing(row_piece))
         if step > 0:
-            rows, cots, in_parts[-1], out_parts[-1] = lax.optimization_barrier(
-                (rows, cots, in_parts[-1], out_parts[-1])
-            )
+            in_tasks.append(flow.launch(plane_scatter(in_part, True)))
+        if step == planes - 1:
+            in_moving = flow.launch(passing(low(in_tasks[1].result)))
+        gate_pre = jnp.einsum("td,fd->tf", rows, gate_weight, preferred_element_type=jnp.float32)
+        up_pre = jnp.einsum("td,fd->tf", rows, up_weight, preferred_element_type=jnp.float32)
+        gate_pre, up_pre, rows = flow.close((gate_pre, up_pre, rows))
+        if step + 2 < planes:
+            row_piece = row_pass.result
+
+        cots = cot_tasks[step].result
         marks = mark_chunks[step].astype(jnp.float32)
         _, chunk_gates, _ = gating(rows, marks)
         chunk_gates = jnp.where(marks > 1.5, chunk_gates, 0.0)
@@ -805,22 +920,18 @@
         for e in reversed(range(exp_here)):
             here = expert_index == dp_index * exp_here + e
             gate_column = jnp.sum(jnp.where(here, chunk_gates, 0.0), axis=-1, keepdims=True)
-            scale = jnp.where(column < (e + 1) * group_lanes, gate_column, scale)
-        gate_pre = jnp.dot(rows, gate_weight, preferred_element_type=jnp.float32)
-        up_pre = jnp.dot(rows, up_weight, preferred_element_type=jnp.float32)
+            scale = jnp.where(column < (e + 1) * group, gate_column, scale)
         sigmoid = jax.nn.sigmoid(gate_pre)
         silu = gate_pre * sigmoid
         act = silu * up_pre
         act_scaled = low(act * scale)
-        out_parts.append(
-            low(jnp.dot(act_scaled, down_weight, preferred_element_type=jnp.float32))
-        )
+        out_part = low(jnp.dot(act_scaled, down_weight, preferred_element_type=jnp.float32))
         act_grad = jnp.einsum("td,fd->tf", cots, down_weight, preferred_element_type=jnp.float32)
         meeting = act * act_grad
         gate_parts.append(
             jnp.stack(
                 [
-                    jnp.sum(meeting[:, e * group_lanes : (e + 1) * group_lanes], axis=-1)
+                    jnp.sum(jnp.where(column // group == e, meeting, 0.0), axis=-1)
                     for e in range(exp_here)
                 ]
             )
@@ -828,24 +939,42 @@
         scaled_grad = act_grad * scale
         gate_grad = low(scaled_grad * up_pre * sigmoid * (1.0 + gate_pre * (1.0 - sigmoid)))
         up_grad = low(scaled_grad * silu)
-        in_parts.append(
-            low(
-                jnp.einsum("tf,df->td", gate_grad, gate_weight, preferred_element_type=jnp.float32)
-                + jnp.einsum("tf,df->td", up_grad, up_weight, preferred_element_type=jnp.float32)
-            )
+        gate_grad, up_grad, act_scaled, out_part, rows, cots = flow.close(
+            (gate_grad, up_grad, act_scaled, out_part, rows, cots)
+        )
+
+        after = (planes - 1 - step) * 3
+        places = {0: (after + 6, 0), 1: (after, 1), 2: (after + 3, 0), 3: (after + 5, 0)}[step]
+        out_tasks.append(flow.launch(plane_scatter(out_part, False, *places)))
+        if step == 0:
+            cot_tasks.append(flow.launch(plane_gather(cot_piece, 3)))
+        in_part = low(
+            jnp.dot(gate_grad, gate_weight, preferred_element_type=jnp.float32)
+            + jnp.dot(up_grad, up_weight, preferred_element_type=jnp.float32)
+        )
+        in_part, gate_grad, up_grad, act_scaled, rows, cots = flow.close(
+            (in_part, gate_grad, up_grad, act_scaled, rows, cots)
         )
         kept_parts.append((rows, cots, gate_grad, up_grad, act_scaled))
-    gate_weight_grad = up_weight_grad = down_weight_grad = 0.0
-    for rows, cots, gate_grad, up_grad, act_scaled in kept_parts:
-        gate_weight_grad += jnp.einsum(
-            "td,tf->df", rows, gate_grad, preferred_element_type=jnp.float32
-        )
-        up_weight_grad += jnp.einsum("td,tf->df", rows, up_grad, preferred_element_type=jnp.float32)
-        down_weight_grad += jnp.einsum(
-            "tf,td->fd", act_scaled, cots, preferred_element_type=jnp.float32
-        )
-
-    ffn_sum = slice_scatter(in_parts)
+
+    in_tasks.append(flow.launch(plane_scatter(in_part, True)))
+    in_moving = flow.launch(
+        passing(low(in_tasks[2].result + in_moving.result.astype(jnp.float32)))
+    )
+    kept_parts = flow.close(kept_parts)
+    gate_weight_grad = sum(
+        jnp.einsum("tf,td->fd", gate_grad, rows, preferred_element_type=jnp.float32)
+        for rows, _, gate_grad, _, _ in kept_parts
+    )
+    gate_weight_grad, kept_parts = flow.close((gate_weight_grad, kept_parts))
+    flow.close(())
+    in_moving = flow.launch(
+        passing(low(in_tasks[3].result + in_moving.result.astype(jnp.float32)))
+    )
+    out_moving = flow.launch(passing(low(out_tasks[1].result)))
+
+    kept_parts = flow.close(kept_parts)
+    ffn_sum = in_tasks[0].result + in_moving.result.astype(jnp.float32)
     gate_sums = jnp.stack(gate_parts).reshape(-1, exp_here, 2, 2, 2, own_count)
     gate_sums = gate_sums[:, :, 0] + core_hop(gate_sums[:, :, 1])
     gate_sums = gate_sums[:, :, 0] + y_hop(gate_sums[:, :, 1])
@@ -865,14 +994,21 @@
         probs_own * (probs_grad - jnp.sum(probs_own * probs_grad, axis=-1, keepdims=True))
     )
     router_grad = jnp.einsum(
-        "td,te->de", normed_own_low, logit_grad, preferred_element_type=jnp.float32
-    )
-    ffn_in = ffn_sum + jnp.einsum(
-        "te,de->td", logit_grad, router_weight, preferred_element_type=jnp.float32
-    )
+        "te,td->ed", logit_grad, normed_own_low, preferred_element_type=jnp.float32
+    )
+    ffn_in = ffn_sum + jnp.dot(logit_grad, router_weight, preferred_element_type=jnp.float32)
     ffn_resid_grad, gain_ffn_grad = norm_backward(resid_own, inverse_own, gain_ffn_f, ffn_in)
     mid_grad_own = cot_own.astype(jnp.float32) + ffn_resid_grad
-    mid_low = tensor_gather(low(mid_grad_own), tensor_index)
+    mid_low, kept_parts = flow.close(
+        (tensor_gather(low(mid_grad_own), tensor_index), kept_parts)
+    )
+    up_weight_grad = sum(
+        jnp.einsum("tf,td->fd", up_grad, rows, preferred_element_type=jnp.float32)
+        for rows, _, _, up_grad, _ in kept_parts
+    )
+    out_moving = flow.launch(
+        passing(low(out_tasks[2].result + out_moving.result.astype(jnp.float32)))
+    )
 
     output_weight_grad = jnp.einsum(
         "th,td->hd", heads_low, mid_low, preferred_element_type=jnp.float32
@@ -880,11 +1016,32 @@
     heads_grad = low(
         jnp.einsum("td,hd->th", mid_low, output_weight, preferred_element_type=jnp.float32)
     ).reshape(tok_count, heads_here, V_HEAD)
+    heads_grad, output_weight_grad, up_weight_grad, kept_parts = flow.close(
+        (heads_grad, output_weight_grad, up_weight_grad, kept_parts)
+    )
+    down_weight_grad = sum(
+        jnp.einsum("tf,td->fd", act_scaled, cots, preferred_element_type=jnp.float32)
+        for _, cots, _, _, act_scaled in kept_parts
+    )
+    output_task = flow.launch(
+        dp_scatter_steps(
+            lambda i: lax.dynamic_slice_in_dim(
+                output_weight_grad, i * w_output.shape[1], w_output.shape[1], 1
+            ),
+            dp_index,
+        )
+    )
     masked = block_scores(query_low, key_full, seq_ids, 0)
     attn_probs = jnp.exp(masked - log_total)
     prob_grad = jnp.einsum("qhc,khc->hqk", heads_grad, value_low, preferred_element_type=jnp.float32)
     row_dot = jnp.sum(attn_probs * prob_grad, axis=-1, keepdims=True)
     score_grad = low(attn_probs * (prob_grad - row_dot))
+    score_grad, probs_low, down_weight_grad = flow.close(
+        (score_grad, low(attn_probs), down_weight_grad)
+    )
+    out_moving = flow.launch(
+        passing(low(out_tasks[3].result + out_moving.result.astype(jnp.float32)))
+    )
     query_grad = (
         jnp.einsum("hqk,khc->qhc", score_grad, key_full, preferred_element_type=jnp.float32)
         * softmax_scale
@@ -894,8 +1051,9 @@
         * softmax_scale
     )
     value_grad = jnp.einsum(
-        "hqk,qhc->khc", low(attn_probs), heads_grad, preferred_element_type=jnp.float32
-    )
+        "hqk,qhc->khc", probs_low, heads_grad, preferred_element_type=jnp.float32
+    )
+    query_grad, key_grad, value_grad = flow.close((query_grad, key_grad, value_grad))
     query_pre_grad = low(
         jnp.concatenate(
             [
@@ -917,6 +1075,9 @@
     expand_weight_grad = jnp.einsum(
         "tr,te->re", latent_low, expand_grad, preferred_element_type=jnp.float32
     )
+    latent_grad, query_weight_grad, expand_weight_grad = flow.close(
+        (latent_grad, query_weight_grad, expand_weight_grad)
+    )
     rope_grad = jnp.sum(key_grad[..., QK_NOPE:], axis=1)
     latent_pre_grad, gain_latent_grad = norm_backward(
         latent_part, inverse_latent, gain_latent_f, latent_grad
@@ -926,9 +1087,9 @@
     )
     attn_in = jnp.einsum(
         "tq,dq->td", query_pre_grad, query_weight, preferred_element_type=jnp.float32
-    ) + jnp.einsum("tc,dc->td", latent_all_grad, latent_weight, preferred_element_type=jnp.float32)
+    ) + jnp.dot(latent_all_grad, latent_weight, preferred_element_type=jnp.float32)
     latent_weight_grad = jnp.einsum(
-        "td,tc->dc", normed_attn_low, latent_all_grad, preferred_element_type=jnp.float32
+        "tc,td->cd", latent_all_grad, normed_attn_low, preferred_element_type=jnp.float32
     )
     gain_attn_grad = jnp.sum(attn_in * (resid_in * inverse_attn), axis=0)
     attn_in_own = tensor_scatter(attn_in, tensor_index)
@@ -937,74 +1098,58 @@
     )
     tokens_grad = tensor_gather(low(mid_grad_own + input_grad), tensor_index)
 
-    out_sum = slice_scatter(out_parts)
+    out_sum = out_tasks[0].result + out_moving.result.astype(jnp.float32)
     result = tensor_gather(low(resid_own + out_sum), tensor_index)
 
-    output_share = dp_scatter(
-        lambda i: lax.dynamic_slice_in_dim(
-            output_weight_grad, i * w_output.shape[1], w_output.shape[1], 1
-        ),
-        dp_index,
-    )
+    output_share = drained(output_task)
     query_share = dp_scatter(
         lambda i: lax.dynamic_slice_in_dim(query_weight_grad, i * lat_block, lat_block, 0),
         dp_index,
     )
-    expand_rows = w_expand.shape[0]
+    expand_block = w_expand.shape[0]
     expand_share = dp_scatter(
-        lambda i: lax.dynamic_slice_in_dim(expand_weight_grad, i * expand_rows, expand_rows, 0),
+        lambda i: lax.dynamic_slice_in_dim(expand_weight_grad, i * expand_block, expand_block, 0),
         dp_index,
     )
 
     gain_latent_rows = padded(gain_latent_grad.reshape(dp_size, -1), 1, lat_block).reshape(width)
+    gain_grads = jnp.stack([gain_attn_grad, gain_ffn_grad, gain_latent_rows])
     side_grad = jnp.concatenate(
         [
-            latent_weight_grad,
-            router_grad,
-            jnp.stack([gain_attn_grad, gain_ffn_grad, gain_latent_rows]).T,
-        ],
-        axis=1,
-    )
-    side_grad = padded(side_grad, 1, side_width)
-    side_grad = side_grad.reshape(dp_size, 2, 2, lat_rows, side_width)
-    kept_side = lax.dynamic_index_in_dim(side_grad, core, 2, keepdims=False)
-    sent_side = lax.dynamic_index_in_dim(side_grad, 1 - core, 2, keepdims=False)
-    side_grad = kept_side + core_hop(low(sent_side)).astype(jnp.float32)
-    kept_side = lax.dynamic_index_in_dim(side_grad, level, 1, keepdims=False)
-    sent_side = lax.dynamic_index_in_dim(side_grad, 1 - level, 1, keepdims=False)
+            low(latent_weight_grad),
+            low(router_grad),
+            padded(low(gain_grads), 0, side_rows - mark_start),
+        ]
+    ).reshape(2, 2, side_rows_here, width)
+    kept_side = lax.dynamic_index_in_dim(side_grad, core, 1, keepdims=False)
+    sent_side = lax.dynamic_index_in_dim(side_grad, 1 - core, 1, keepdims=False)
+    side_grad = kept_side.astype(jnp.float32) + core_hop(sent_side).astype(jnp.float32)
+    kept_side = lax.dynamic_index_in_dim(side_grad, level, 0, keepdims=False)
+    sent_side = lax.dynamic_index_in_dim(side_grad, 1 - level, 0, keepdims=False)
     side_grad = kept_side + y_hop(low(sent_side)).astype(jnp.float32)
     side_piece = dp_scatter(
-        lambda i: lax.dynamic_index_in_dim(side_grad, i, 0, keepdims=False), dp_index
+        lambda i: lax.dynamic_slice_in_dim(side_grad, i * lat_block, lat_block, 1), dp_index
     )
     grad_full = tensor_gather(low(side_piece), tensor_index).astype(jnp.float32)
-    latent_share = grad_full[:, :lat_width]
-    router_share = grad_full[:, lat_width : lat_width + experts]
-    gain_rows = grad_full[:, lat_width + experts : lat_width + experts + 3].T
-    gain_attn_share = gain_rows[0]
-    gain_ffn_share = gain_rows[1]
-    gain_latent_share = gain_rows[2, : gain_latent.shape[0]]
-
-    def routed_grad(grad, axis):
-        return jnp.stack(
-            [
-                lax.slice_in_dim(grad, e * group_lanes, e * group_lanes + group, axis=axis)
-                for e in range(exp_here)
-            ]
-        )
-
-    def shared_grad(grad, axis):
-        start = exp_here * group_lanes
-        return low(lax.slice_in_dim(grad, start, start + shared_here, axis=axis))
-
-    shared_in_grad = lax.all_to_all(
-        jnp.stack([shared_grad(gate_weight_grad, 1), shared_grad(up_weight_grad, 1)]),
-        "dp",
-        split_axis=1,
-        concat_axis=2,
-        tiled=True,
-    ).astype(jnp.float32)
-    shared_down_share = lax.all_to_all(
-        shared_grad(down_weight_grad, 0), "dp", split_axis=1, concat_axis=0, tiled=True
+    latent_share = grad_full[:lat_width].T
+    router_share = grad_full[lat_width:mark_start].T
+    gain_attn_share = grad_full[mark_start]
+    gain_ffn_share = grad_full[mark_start + 1]
+    gain_latent_share = grad_full[mark_start + 2, : gain_latent.shape[0]]
+
+    def routed_grad(grad):
+        return grad[:routed_here].reshape(exp_here, group, width)
+
+    routed_grads = (
+        routed_grad(gate_weight_grad).swapaxes(1, 2),
+        routed_grad(up_weight_grad).swapaxes(1, 2),
+        routed_grad(down_weight_grad),
+    )
+    shared_grads = jnp.stack(
+        [low(grad[routed_here:]) for grad in (gate_weight_grad, up_weight_grad, down_weight_grad)]
+    )
+    shared_grads = lax.all_to_all(
+        shared_grads, "dp", split_axis=2, concat_axis=1, tiled=True
     ).astype(jnp.float32)
 
     return (
@@ -1018,12 +1163,10 @@
         output_share,
         gain_ffn_share,
         router_share,
-        shared_in_grad[0],
-        shared_in_grad[1],
-        shared_down_share,
-        routed_grad(gate_weight_grad, 1),
-        routed_grad(up_weight_grad, 1),
-        routed_grad(down_weight_grad, 0),
+        shared_grads[0].T,
+        shared_grads[1].T,
+        shared_grads[2],
+        *routed_grads,
     )
 
 

time: 1270 us -> 1090 us (0.86)
  matrix products: 343 us -> 276 us
  waiting for transfers between devices: 384 us -> 328 us
  other arithmetic: 107 us -> 155 us
  local copies, waits for them, and re-layouts: 230 us -> 193 us
  starting transfers between devices: 158 us -> 127 us
  blocking collectives: 30.6 us -> 0 us
    ppermute x130 -> x84, waiting for transfers between devices: 239 us -> 188 us  [hop(): lax.ppermute(values, axis, [(i, i ^ bit) for i in range(lax.axis_size(axi...]
    dot_general x35, matrix products: 213 us -> 168 us  [the longest x4 30.5 us: body_dense(): jnp.dot(gate_grad, gate_weight, preferred_element_type=jnp.float32)]
    ppermute x130 -> x84, starting transfers between devices: 110 us -> 66 us  [hop(): lax.ppermute(values, axis, [(i, i ^ bit) for i in range(lax.axis_size(axi...]
    convert_element_type x24 -> x32, other arithmetic: 12 us -> 53.1 us  [low(): return values.astype(jnp.bfloat16)]
    all_gather x1 -> x0, blocking collectives: 30.6 us -> none  [body_dense(): marks_all = lax.all_gather(low(standing), 'dp', axis=0, tiled=True)]
    squeeze x19 -> x7, local copies, waits for them, and re-layouts: 23.5 us -> 0.96 us  [the longest x4 0.85 us: plane_scatter(): far, = (yield [core_hop(part[1])])]
    ppermute x36 -> x30, starting transfers between devices: 23.7 us -> 46.2 us  [z_hop(): lax.ppermute(values, 'dp', [(i, (i + 2) % count) for i in range(count)])]
    all_to_all x4 -> x2, waiting for transfers between devices: 20.6 us -> 0.01 us  [the longest x1 0.01 us: body_dense(): lax.all_to_all(jnp.stack([w_shared_gate.T, w_shared_up.T, w_shared_down])...]
  transfers between devices with their start and end apart: 171 -> 117, of which waited for: 68 -> 52; matrix products, arithmetic and copies ran while one was open for 50% -> 50% of each run, Pallas kernels for 0% -> 0%
where the time goes in v3:
time: 1090 us; the launch traced here: 1080 us
  waiting for transfers between devices  328 us (30%)
  matrix products  276 us (25%)
  local copies, waits for them, and re-layouts  193 us (18%)
  other arithmetic  155 us (14%)
  starting transfers between devices  127 us (12%)
    ppermute x84, waiting for transfers between devices, hop(): lax.ppermute(values, axis, [(i, i ^ bit) for i in range(lax.axis_size(axi...  188 us
    ppermute x30, waiting for transfers between devices, z_hop(): lax.ppermute(values, 'dp', [(i, (i + 2) % count) for i in range(count)])  134 us
    ppermute x84, starting transfers between devices, hop(): lax.ppermute(values, axis, [(i, i ^ bit) for i in range(lax.axis_size(axi...  66 us
    unnamed x421, local copies, waits for them, and re-layouts  57.2 us
    convert_element_type x32, other arithmetic, low(): return values.astype(jnp.bfloat16)  53.1 us
    ppermute x30, starting transfers between devices, z_hop(): lax.ppermute(values, 'dp', [(i, (i + 2) % count) for i in range(count)])  46.2 us
    dot_general x4, matrix products, body_dense(): jnp.einsum('tf,td->fd', act_scaled, cots, preferred_element_type=jnp.floa...  32.2 us
    dot_general x4, matrix products, body_dense(): jnp.dot(gate_grad, gate_weight, preferred_element_type=jnp.float32)  30.5 us
  transfers between devices with their start and end apart: 117, of which 52 were waited for; matrix products, arithmetic and copies ran while one was open for 50% of the time, Pallas kernels for 0%

profile of v3, /device:TPU:0, one launch (start us, length us, event | category | flops | bytes accessed | tf_op | source)
XLA Modules:
  0.0 1083.4 jit_solution(8043520536286373641)
XLA Ops:
  32.1 24.5 %collective-permute-done.3 = bf16[160,256]{1,0:T(8,128)(2,1)S(1)} collective-permute-done((bf16[160,256]{1,0:T(8,128)(2,1)S(1)}, bf16[160,256]{1,0:T(8,128)(2,1)S(1)}, u32[]{:S(2)}, u32[]{:S(2)}) %collective-permute-start.3) | collective-permute-done | bytes 81952 | tf_op jit(solution)/shard_map/ppermute | solution.py:461
  64.9 9.1 collective-permute-done.6
  78.0 9.1 collective-permute-done.7
  140.9 10.7 collective-permute-done.15
  211.0 11.8 %collective-permute-done.21 = bf16[128,2048]{1,0:T(8,128)(2,1)} collective-permute-done((bf16[128,2048]{1,0:T(8,128)(2,1)}, bf16[128,2048]{1,0:T(8,128)(2,1)}, u32[]{:S(2)}, u32[]{:S(2)}) %collective-permute-start.21) | collective-permute-done | bytes 524320 | tf_op jit(solution)/shard_map/ppermute | solution.py:461
  244.6 7.2 collective-permute-done.23
  301.6 15.6 %collective-permute-done.32 = bf16[256,2048]{1,0:T(8,128)(2,1)S(1)} collective-permute-done((bf16[256,2048]{1,0:T(8,128)(2,1)S(1)}, bf16[256,2048]{1,0:T(8,128)(2,1)S(1)}, u32[]{:S(2)}, u32[]{:S(2)}) %collective-permute-start.32) | collective-permute-done | bytes 1048608 | tf_op jit(solution)/shard_map/ppermute | solution.py:444
  328.3 8.1 multiply_convert_fusion.11
  341.3 10.9 %collective-permute-done.36 = bf16[256,2048]{1,0:T(8,128)(2,1)S(1)} collective-permute-done((bf16[256,2048]{1,0:T(8,128)(2,1)}, bf16[256,2048]{1,0:T(8,128)(2,1)S(1)}, u32[]{:S(2)}, u32[]{:S(2)}) %collective-permute-start.36) | collective-permute-done | bytes 1048608 | tf_op jit(solution)/shard_map/ppermute | solution.py:444
  352.3 6.9 fusion.238
  366.7 7.0 add_convert_fusion.3
  373.7 6.7 fusion.241
  396.0 11.1 %collective-permute-done.40 = bf16[256,2048]{1,0:T(8,128)(2,1)S(1)} collective-permute-done((bf16[256,2048]{1,0:T(8,128)(2,1)S(1)}, bf16[256,2048]{1,0:T(8,128)(2,1)S(1)}, u32[]{:S(2)}, u32[]{:S(2)}) %collective-permute-start.40) | collective-permute-done | bytes 1048608 | tf_op jit(solution)/shard_map/ppermute | solution.py:444
  424.7 7.1 convolution_convert_fusion.2
  431.9 8.4 collective-permute-done.45
  444.0 8.3 fusion.242
  460.8 7.5 add_convert_fusion.2
  468.3 6.6 fusion.243
  492.3 10.2 collective-permute-done.50
  521.2 7.1 convolution_convert_fusion.1
  528.3 7.7 collective-permute-done.54
  539.3 6.9 fusion.246
  553.7 8.9 add_convert_fusion.1
  562.6 6.5 fusion.247
  595.4 9.7 multiply_convert_fusion.3
  609.5 7.1 convolution_convert_fusion
  623.4 7.3 fusion.250
  630.7 7.1 add_convert_fusion
  645.4 13.5 %collective-permute-done.66 = bf16[128,2048]{1,0:T(8,128)(2,1)S(1)} collective-permute-done((bf16[128,2048]{1,0:T(8,128)(2,1)S(1)}, bf16[128,2048]{1,0:T(8,128)(2,1)S(1)}, u32[]{:S(2)}, u32[]{:S(2)}) %collective-permute-start.66) | collective-permute-done | bytes 524320 | tf_op jit(solution)/shard_map/ppermute | solution.py:461
  659.0 8.4 collective-permute-done.64
  687.2 10.4 add_add_fusion.2
  708.5 6.4 all-to-all-done.1
  723.3 13.1 %collective-permute-done.71 = bf16[128,2048]{1,0:T(8,128)(2,1)S(1)} collective-permute-done((bf16[128,2048]{1,0:T(8,128)(2,1)S(1)}, bf16[128,2048]{1,0:T(8,128)(2,1)S(1)}, u32[]{:S(2)}, u32[]{:S(2)}) %collective-permute-start.71) | collective-permute-done | bytes 524320 | tf_op jit(solution)/shard_map/ppermute | solution.py:461
  736.5 8.1 collective-permute-done.72
  751.5 7.3 collective-permute-done.75
  762.7 11.1 %collective-permute-done.77 = bf16[128,2048]{1,0:T(8,128)(2,1)S(1)} collective-permute-done((bf16[128,2048]{1,0:T(8,128)(2,1)S(1)}, bf16[128,2048]{1,0:T(8,128)(2,1)S(1)}, u32[]{:S(2)}, u32[]{:S(2)}) %collective-permute-start.77) | collective-permute-done | bytes 524320 | tf_op jit(solution)/shard_map/ppermute | solution.py:444
  793.4 10.4 add_add_fusion.1
  818.2 8.0 fusion.260
  832.2 7.8 fusion.259
  840.0 10.4 add_add_fusion
  852.4 6.0 slice.619
  880.2 6.0 all-to-all-start.2
  888.7 8.7 collective-permute-done.86
  913.9 20.1 %collective-permute-done.89 = bf16[512,256]{1,0:T(8,128)(2,1)} collective-permute-done((bf16[512,256]{1,0:T(8,128)(2,1)S(1)}, bf16[512,256]{1,0:T(8,128)(2,1)}, u32[]{:S(2)}, u32[]{:S(2)}) %collective-permute-start.89) | collective-permute-done | bytes 262176 | tf_op jit(solution)/shard_map/ppermute | solution.py:461
  955.6 7.7 collective-permute-start.113
  963.7 14.1 %collective-permute-done.109 = bf16[2,64,1024]{2,1,0:T(8,128)(2,1)S(1)} collective-permute-done((bf16[2,64,1024]{2,1,0:T(8,128)(2,1)S(1)}, bf16[2,64,1024]{2,1,0:T(8,128)(2,1)S(1)}, u32[]{:S(2)}, u32[]{:S(2)}) %collective-permute-start.109) | collective-permute-done | bytes 262176 | tf_op jit(solution)/shard_map/ppermute | solution.py:444
  977.8 7.6 collective-permute-start.110
  1067.7 6.3 collective-permute-done.101
  (969 shorter events, 632.2 us)
Async XLA Ops:
  22.6 55.3 %collective-permute-start.8 = (bf16[1536,256]{1,0:T(8,128)(2,1)}, bf16[1536,256]{1,0:T(8,128)(2,1)}, u32[]{:S(2)}, u32[]{:S(2)}) collective-permute-start(bf16[1536,256]{1,0:T(8,128)(2,1)} %constant_dynamic-update-slice_fusion), channel_id=1, source_target_pairs={{0,4},{4,0},{8,12},{12,8},{16,20},{20,16},{24,28},{28,24},{1,5},{5... | collective-permute-start | bytes 2359304 | tf_op jit(solution)/shard_map/ppermute | solution.py:444
  23.2 54.8 %collective-permute-start.9 = (bf16[1536,256]{1,0:T(8,128)(2,1)}, bf16[1536,256]{1,0:T(8,128)(2,1)}, u32[]{:S(2)}, u32[]{:S(2)}) collective-permute-start(bf16[1536,256]{1,0:T(8,128)(2,1)} %constant_dynamic-update-slice_fusion), channel_id=1, source_target_pairs={{0,8},{4,12},{8,16},{12,20},{16,24},{20,28},{24,0},{28,4},{1,9},{5... | collective-permute-start | bytes 2359304 | tf_op jit(solution)/shard_map/ppermute | solution.py:461
  26.6 114.2 %collective-permute-start.16 = (bf16[128,2048]{1,0:T(8,128)(2,1)}, bf16[128,2048]{1,0:T(8,128)(2,1)}, u32[]{:S(2)}, u32[]{:S(2)}) collective-permute-start(bf16[128,2048]{1,0:T(8,128)(2,1)} %constant_dynamic-slice_fusion.5), channel_id=1, source_target_pairs={{0,8},{4,12},{8,16},{12,20},{16,24},{20,28},{24,0},{28,4},{1,9},{5... | collective-permute-start | bytes 1572872 | tf_op jit(solution)/shard_map/ppermute | solution.py:461
  30.4 27.7 %collective-permute-start.2 = (bf16[160,256]{1,0:T(8,128)(2,1)S(1)}, bf16[160,256]{1,0:T(8,128)(2,1)S(1)}, u32[]{:S(2)}, u32[]{:S(2)}) collective-permute-start(bf16[160,256]{1,0:T(8,128)(2,1)S(1)} %collective-permute-done.1), channel_id=1, source_target_pairs={{0,4},{4,0},{8,12},{12,8},{16,20},{20,16},{24,28},{28,24},{1,5},{5... | collective-permute-start | bytes 245768 | tf_op jit(solution)/shard_map/ppermute | solution.py:444
  61.2 132.5 %collective-permute-start.17 = (bf16[128,2048]{1,0:T(8,128)(2,1)}, bf16[128,2048]{1,0:T(8,128)(2,1)}, u32[]{:S(2)}, u32[]{:S(2)}) collective-permute-start(bf16[128,2048]{1,0:T(8,128)(2,1)} %constant_dynamic-slice_fusion.5), channel_id=1, source_target_pairs={{0,4},{4,0},{8,12},{12,8},{16,20},{20,16},{24,28},{28,24},{1,5},{5... | collective-permute-start | bytes 1572872 | tf_op jit(solution)/shard_map/ppermute | solution.py:444
  160.6 33.1 %collective-permute-start.18 = (bf16[128,2048]{1,0:T(8,128)(2,1)}, bf16[128,2048]{1,0:T(8,128)(2,1)}, u32[]{:S(2)}, u32[]{:S(2)}) collective-permute-start(bf16[128,2048]{1,0:T(8,128)(2,1)} %collective-permute-done.16), channel_id=1, source_target_pairs={{0,8},{4,12},{8,16},{12,20},{16,24},{20,28},{24,0},{28,4},{1,9},{5... | collective-permute-start | bytes 1572872 | tf_op jit(solution)/shard_map/ppermute | solution.py:461
  160.9 50.1 %collective-permute-start.20 = (bf16[128,2048]{1,0:T(8,128)(2,1)}, bf16[128,2048]{1,0:T(8,128)(2,1)}, u32[]{:S(2)}, u32[]{:S(2)}) collective-permute-start(bf16[128,2048]{1,0:T(8,128)(2,1)} %collective-permute-done.16), channel_id=1, source_target_pairs={{0,4},{4,0},{8,12},{12,8},{16,20},{20,16},{24,28},{28,24},{1,5},{5... | collective-permute-start | bytes 1572872 | tf_op jit(solution)/shard_map/ppermute | solution.py:444
  181.8 52.5 %all-to-all-start = ((bf16[3,704,256]{2,0,1:T(4,128)(2,1)}), bf16[3,704,256]{2,0,1:T(4,128)(2,1)S(1)}, u32[]{:S(2)}, u32[]{:S(2)}) async-start(bf16[3,704,256]{2,0,1:T(4,128)(2,1)} %copy.253), calls=%async_computation | async-start | bytes 2883584 | tf_op jit(solution)/shard_map/all_to_all | solution.py:868
  193.7 29.1 %collective-permute-start.21 = (bf16[128,2048]{1,0:T(8,128)(2,1)}, bf16[128,2048]{1,0:T(8,128)(2,1)}, u32[]{:S(2)}, u32[]{:S(2)}) collective-permute-start(bf16[128,2048]{1,0:T(8,128)(2,1)} %collective-permute-done.18), channel_id=1, source_target_pairs={{0,8},{4,12},{8,16},{12,20},{16,24},{20,28},{24,0},{28,4},{1,9},{5... | collective-permute-start | bytes 1572872 | tf_op jit(solution)/shard_map/ppermute | solution.py:461
  196.2 57.1 %collective-permute-start.25 = (bf16[128,2048]{1,0:T(8,128)(2,1)}, bf16[128,2048]{1,0:T(8,128)(2,1)}, u32[]{:S(2)}, u32[]{:S(2)}) collective-permute-start(bf16[128,2048]{1,0:T(8,128)(2,1)} %collective-permute-done.18), channel_id=1, source_target_pairs={{0,4},{4,0},{8,12},{12,8},{16,20},{20,16},{24,28},{28,24},{1,5},{5... | collective-permute-start | bytes 1572872 | tf_op jit(solution)/shard_map/ppermute | solution.py:444
  231.7 148.9 %collective-permute-start.39 = (bf16[128,2048]{1,0:T(8,128)(2,1)}, bf16[128,2048]{1,0:T(8,128)(2,1)}, u32[]{:S(2)}, u32[]{:S(2)}) collective-permute-start(bf16[128,2048]{1,0:T(8,128)(2,1)} %collective-permute-done.21), channel_id=1, source_target_pairs={{0,4},{4,0},{8,12},{12,8},{16,20},{20,16},{24,28},{28,24},{1,5},{5... | collective-permute-start | bytes 1572872 | tf_op jit(solution)/shard_map/ppermute | solution.py:444
  273.9 27.7 %collective-permute-start.33 = (bf16[128,2048]{1,0:T(8,128)(2,1)S(1)}, bf16[128,2048]{1,0:T(8,128)(2,1)S(1)}, u32[]{:S(2)}, u32[]{:S(2)}) collective-permute-start(bf16[128,2048]{1,0:T(8,128)(2,1)S(1)} %collective-permute-done.28), channel_id=1, source_target_pairs={{0,4},{4,0},{8,12},{12,8},{16,20},{20,16},{24,28},{28,24},{1,5},{5... | collective-permute-start | bytes 1572872 | tf_op jit(solution)/shard_map/ppermute | solution.py:444
  275.2 26.4 %collective-permute-start.34 = (bf16[128,2048]{1,0:T(8,128)(2,1)S(1)}, bf16[128,2048]{1,0:T(8,128)(2,1)S(1)}, u32[]{:S(2)}, u32[]{:S(2)}) collective-permute-start(bf16[128,2048]{1,0:T(8,128)(2,1)S(1)} %collective-permute-done.28), channel_id=1, source_target_pairs={{0,8},{4,12},{8,16},{12,20},{16,24},{20,28},{24,0},{28,4},{1,9},{5... | collective-permute-start | bytes 1572872 | tf_op jit(solution)/shard_map/ppermute | solution.py:461
  291.7 25.5 %collective-permute-start.32 = (bf16[256,2048]{1,0:T(8,128)(2,1)S(1)}, bf16[256,2048]{1,0:T(8,128)(2,1)S(1)}, u32[]{:S(2)}, u32[]{:S(2)}) collective-permute-start(bf16[256,2048]{1,0:T(8,128)(2,1)S(1)} %pad_maximum_fusion.20), channel_id=1, source_target_pairs={{0,2},{1,3},{2,0},{3,1},{4,6},{5,7},{6,4},{7,5},{8,10},{9,11},{10,... | collective-permute-start | bytes 3145736 | tf_op jit(solution)/shard_map/ppermute | solution.py:444
  317.2 78.8 %collective-permute-start.41 = (bf16[128,2048]{1,0:T(8,128)(2,1)S(1)}, bf16[128,2048]{1,0:T(8,128)(2,1)S(1)}, u32[]{:S(2)}, u32[]{:S(2)}) collective-permute-start(bf16[128,2048]{1,0:T(8,128)(2,1)S(1)} %collective-permute-done.34), channel_id=1, source_target_pairs={{0,4},{4,0},{8,12},{12,8},{16,20},{20,16},{24,28},{28,24},{1,5},{5... | collective-permute-start | bytes 1572872 | tf_op jit(solution)/shard_map/ppermute | solution.py:444
  318.1 77.9 %collective-permute-start.42 = (bf16[128,2048]{1,0:T(8,128)(2,1)S(1)}, bf16[128,2048]{1,0:T(8,128)(2,1)S(1)}, u32[]{:S(2)}, u32[]{:S(2)}) collective-permute-start(bf16[128,2048]{1,0:T(8,128)(2,1)S(1)} %collective-permute-done.34), channel_id=1, source_target_pairs={{0,8},{4,12},{8,16},{12,20},{16,24},{20,28},{24,0},{28,4},{1,9},{5... | collective-permute-start | bytes 1572872 | tf_op jit(solution)/shard_map/ppermute | solution.py:461
  325.4 26.8 %collective-permute-start.35 = (bf16[512,2048]{1,0:T(8,128)(2,1)}, bf16[512,2048]{1,0:T(8,128)(2,1)}, u32[]{:S(2)}, u32[]{:S(2)}) collective-permute-start(bf16[512,2048]{1,0:T(8,128)(2,1)} %pad_maximum_fusion.7), channel_id=1, source_target_pairs={{0,1},{1,0},{2,3},{3,2},{4,5},{5,4},{6,7},{7,6},{8,9},{9,8},{10,11... | collective-permute-start | bytes 6291464 | tf_op jit(solution)/shard_map/ppermute | solution.py:444
  326.5 25.8 %collective-permute-start.36 = (bf16[256,2048]{1,0:T(8,128)(2,1)}, bf16[256,2048]{1,0:T(8,128)(2,1)S(1)}, u32[]{:S(2)}, u32[]{:S(2)}) collective-permute-start(bf16[256,2048]{1,0:T(8,128)(2,1)} %pad_maximum_fusion.21), channel_id=1, source_target_pairs={{0,2},{1,3},{2,0},{3,1},{4,6},{5,7},{6,4},{7,5},{8,10},{9,11},{10,... | collective-permute-start | bytes 3145736 | tf_op jit(solution)/shard_map/ppermute | solution.py:444
  381.9 25.3 %collective-permute-start.40 = (bf16[256,2048]{1,0:T(8,128)(2,1)S(1)}, bf16[256,2048]{1,0:T(8,128)(2,1)S(1)}, u32[]{:S(2)}, u32[]{:S(2)}) collective-permute-start(bf16[256,2048]{1,0:T(8,128)(2,1)S(1)} %pad_maximum_fusion.22), channel_id=1, source_target_pairs={{0,2},{1,3},{2,0},{3,1},{4,6},{5,7},{6,4},{7,5},{8,10},{9,11},{10,... | collective-permute-start | bytes 3145736 | tf_op jit(solution)/shard_map/ppermute | solution.py:444
  408.5 83.9 %collective-permute-start.51 = (bf16[128,2048]{1,0:T(8,128)(2,1)S(1)}, bf16[128,2048]{1,0:T(8,128)(2,1)S(1)}, u32[]{:S(2)}, u32[]{:S(2)}) collective-permute-start(bf16[128,2048]{1,0:T(8,128)(2,1)S(1)} %collective-permute-done.42), channel_id=1, source_target_pairs={{0,4},{4,0},{8,12},{12,8},{16,20},{20,16},{24,28},{28,24},{1,5},{5... | collective-permute-start | bytes 1572872 | tf_op jit(solution)/shard_map/ppermute | solution.py:444
  413.3 30.7 %collective-permute-start.44 = (bf16[512,2048]{1,0:T(8,128)(2,1)S(1)}, bf16[512,2048]{1,0:T(8,128)(2,1)S(1)}, u32[]{:S(2)}, u32[]{:S(2)}) collective-permute-start(bf16[512,2048]{1,0:T(8,128)(2,1)S(1)} %pad_maximum_fusion.9), channel_id=1, source_target_pairs={{0,1},{1,0},{2,3},{3,2},{4,5},{5,4},{6,7},{7,6},{8,9},{9,8},{10,11... | collective-permute-start | bytes 6291464 | tf_op jit(solution)/shard_map/ppermute | solution.py:444
  414.5 25.8 %collective-permute-start.45 = (bf16[256,2048]{1,0:T(8,128)(2,1)}, bf16[256,2048]{1,0:T(8,128)(2,1)S(1)}, u32[]{:S(2)}, u32[]{:S(2)}) collective-permute-start(bf16[256,2048]{1,0:T(8,128)(2,1)} %pad_maximum_fusion.23), channel_id=1, source_target_pairs={{0,2},{1,3},{2,0},{3,1},{4,6},{5,7},{6,4},{7,5},{8,10},{9,11},{10,... | collective-permute-start | bytes 3145736 | tf_op jit(solution)/shard_map/ppermute | solution.py:444
  416.9 27.1 %collective-permute-start.46 = (bf16[2,128,2048]{2,1,0:T(8,128)(2,1)}, bf16[2,128,2048]{2,1,0:T(8,128)(2,1)S(1)}, u32[]{:S(2)}, u32[]{:S(2)}) collective-permute-start(bf16[2,128,2048]{2,1,0:T(8,128)(2,1)} %fusion.35), channel_id=1, source_target_pairs={{0,4},{4,0},{8,12},{12,8},{16,20},{20,16},{24,28},{28,24},{1,5},{5... | collective-permute-start | bytes 3145736 | tf_op jit(solution)/shard_map/ppermute | solution.py:444
  477.1 25.4 %collective-permute-start.50 = (bf16[256,2048]{1,0:T(8,128)(2,1)S(1)}, bf16[256,2048]{1,0:T(8,128)(2,1)S(1)}, u32[]{:S(2)}, u32[]{:S(2)}) collective-permute-start(bf16[256,2048]{1,0:T(8,128)(2,1)S(1)} %pad_maximum_fusion.24), channel_id=1, source_target_pairs={{0,2},{1,3},{2,0},{3,1},{4,6},{5,7},{6,4},{7,5},{8,10},{9,11},{10,... | collective-permute-start | bytes 3145736 | tf_op jit(solution)/shard_map/ppermute | solution.py:444
  509.1 30.1 %collective-permute-start.53 = (bf16[512,2048]{1,0:T(8,128)(2,1)}, bf16[512,2048]{1,0:T(8,128)(2,1)S(1)}, u32[]{:S(2)}, u32[]{:S(2)}) collective-permute-start(bf16[512,2048]{1,0:T(8,128)(2,1)} %pad_maximum_fusion.11), channel_id=1, source_target_pairs={{0,1},{1,0},{2,3},{3,2},{4,5},{5,4},{6,7},{7,6},{8,9},{9,8},{10,11... | collective-permute-start | bytes 6291464 | tf_op jit(solution)/shard_map/ppermute | solution.py:444
  510.3 25.8 %collective-permute-start.54 = (bf16[256,2048]{1,0:T(8,128)(2,1)}, bf16[256,2048]{1,0:T(8,128)(2,1)S(1)}, u32[]{:S(2)}, u32[]{:S(2)}) collective-permute-start(bf16[256,2048]{1,0:T(8,128)(2,1)} %pad_maximum_fusion.25), channel_id=1, source_target_pairs={{0,2},{1,3},{2,0},{3,1},{4,6},{5,7},{6,4},{7,5},{8,10},{9,11},{10,... | collective-permute-start | bytes 3145736 | tf_op jit(solution)/shard_map/ppermute | solution.py:444
  513.8 25.5 %collective-permute-start.55 = (bf16[2,128,2048]{2,1,0:T(8,128)(2,1)}, bf16[2,128,2048]{2,1,0:T(8,128)(2,1)S(1)}, u32[]{:S(2)}, u32[]{:S(2)}) collective-permute-start(bf16[2,128,2048]{2,1,0:T(8,128)(2,1)} %fusion.36), channel_id=1, source_target_pairs={{0,4},{4,0},{8,12},{12,8},{16,20},{20,16},{24,28},{28,24},{1,5},{5... | collective-permute-start | bytes 3145736 | tf_op jit(solution)/shard_map/ppermute | solution.py:444
  609.4 34.8 %collective-permute-start.73 = (f32[4,2,2,2,128]{4,3,0,1,2:T(2,128)S(1)}, f32[4,2,2,2,128]{4,3,0,1,2:T(2,128)S(1)}, u32[]{:S(2)}, u32[]{:S(2)}) collective-permute-start(f32[4,2,2,2,128]{4,3,0,1,2:T(2,128)S(1)} %slice_bitcast_fusion.46), channel_id=1, source_target_pairs={{0,1},{1,0},{2,3},{3,2},{4,5},{5,4},{6,7},{7,6},{8,9},{9,8},{10,11... | collective-permute-start | bytes 49160 | tf_op jit(solution)/shard_map/ppermute | solution.py:444
  639.4 28.0 %collective-permute-start.65 = (bf16[2,2,128,2048]{3,2,0,1:T(8,128)(2,1)S(1)}, bf16[2,2,128,2048]{3,2,0,1:T(8,128)(2,1)S(1)}, u32[]{:S(2)}, u32[]{:S(2)}) collective-permute-start(bf16[2,2,128,2048]{3,2,0,1:T(8,128)(2,1)S(1)} %copy.274), channel_id=1, source_target_pairs={{0,1},{1,0},{2,3},{3,2},{4,5},{5,4},{6,7},{7,6},{8,9},{9,8},{10,11... | collective-permute-start | bytes 6291464 | tf_op jit(solution)/shard_map/ppermute | solution.py:444
  642.3 25.1 %collective-permute-start.64 = (bf16[2,128,2048]{2,1,0:T(8,128)(2,1)S(1)}, bf16[2,128,2048]{2,1,0:T(8,128)(2,1)S(1)}, u32[]{:S(2)}, u32[]{:S(2)}) collective-permute-start(bf16[2,128,2048]{2,1,0:T(8,128)(2,1)S(1)} %fusion.38), channel_id=1, source_target_pairs={{0,2},{1,3},{2,0},{3,1},{4,6},{5,7},{6,4},{7,5},{8,10},{9,11},{10,... | collective-permute-start | bytes 3145736 | tf_op jit(solution)/shard_map/ppermute | solution.py:444
  644.2 59.6 %collective-permute-start.74 = (f32[4,2,2,128]{3,2,0,1:T(2,128)S(1)}, f32[4,2,2,128]{3,2,0,1:T(2,128)S(1)}, u32[]{:S(2)}, u32[]{:S(2)}) collective-permute-start(f32[4,2,2,128]{3,2,0,1:T(2,128)S(1)} %slice_bitcast_fusion.48), channel_id=1, source_target_pairs={{0,2},{1,3},{2,0},{3,1},{4,6},{5,7},{6,4},{7,5},{8,10},{9,11},{10,... | collective-permute-start | bytes 24584 | tf_op jit(solution)/shard_map/ppermute | solution.py:444
  669.3 28.3 %collective-permute-start.67 = (bf16[2,128,2048]{2,1,0:T(8,128)(2,1)}, bf16[2,128,2048]{2,1,0:T(8,128)(2,1)}, u32[]{:S(2)}, u32[]{:S(2)}) collective-permute-start(bf16[2,128,2048]{2,1,0:T(8,128)(2,1)} %fusion.39), channel_id=1, source_target_pairs={{0,4},{4,0},{8,12},{12,8},{16,20},{20,16},{24,28},{28,24},{1,5},{5... | collective-permute-start | bytes 3145736 | tf_op jit(solution)/shard_map/ppermute | solution.py:444
  718.0 26.6 %collective-permute-start.70 = (bf16[2,128,2048]{2,1,0:T(8,128)(2,1)S(1)}, bf16[2,128,2048]{2,1,0:T(8,128)(2,1)S(1)}, u32[]{:S(2)}, u32[]{:S(2)}) collective-permute-start(bf16[2,128,2048]{2,1,0:T(8,128)(2,1)S(1)} %fusion.40), channel_id=1, source_target_pairs={{0,2},{1,3},{2,0},{3,1},{4,6},{5,7},{6,4},{7,5},{8,10},{9,11},{10,... | collective-permute-start | bytes 3145736 | tf_op jit(solution)/shard_map/ppermute | solution.py:444
  774.7 32.1 %collective-permute-start.78 = (bf16[2,128,2048]{2,1,0:T(8,128)(2,1)S(1)}, bf16[2,128,2048]{2,1,0:T(8,128)(2,1)S(1)}, u32[]{:S(2)}, u32[]{:S(2)}) collective-permute-start(bf16[2,128,2048]{2,1,0:T(8,128)(2,1)S(1)} %fusion.41), channel_id=1, source_target_pairs={{0,2},{1,3},{2,0},{3,1},{4,6},{5,7},{6,4},{7,5},{8,10},{9,11},{10,... | collective-permute-start | bytes 3145736 | tf_op jit(solution)/shard_map/ppermute | solution.py:444
  775.2 31.5 %collective-permute-start.79 = (bf16[128,2048]{1,0:T(8,128)(2,1)S(1)}, bf16[128,2048]{1,0:T(8,128)(2,1)S(1)}, u32[]{:S(2)}, u32[]{:S(2)}) collective-permute-start(bf16[128,2048]{1,0:T(8,128)(2,1)S(1)} %fusion.52), channel_id=1, source_target_pairs={{0,8},{4,12},{8,16},{12,20},{16,24},{20,28},{24,0},{28,4},{1,9},{5... | collective-permute-start | bytes 1572872 | tf_op jit(solution)/shard_map/ppermute | solution.py:461
  812.0 48.3 %collective-permute-start.80 = (bf16[2,128,2048]{2,1,0:T(8,128)(2,1)}, bf16[2,128,2048]{2,1,0:T(8,128)(2,1)S(1)}, u32[]{:S(2)}, u32[]{:S(2)}) collective-permute-start(bf16[2,128,2048]{2,1,0:T(8,128)(2,1)} %fusion.42), channel_id=1, source_target_pairs={{0,2},{1,3},{2,0},{3,1},{4,6},{5,7},{6,4},{7,5},{8,10},{9,11},{10,... | collective-permute-start | bytes 3145736 | tf_op jit(solution)/shard_map/ppermute | solution.py:444
  813.7 46.6 %collective-permute-start.81 = (bf16[128,2048]{1,0:T(8,128)(2,1)}, bf16[128,2048]{1,0:T(8,128)(2,1)}, u32[]{:S(2)}, u32[]{:S(2)}) collective-permute-start(bf16[128,2048]{1,0:T(8,128)(2,1)} %fusion.88), channel_id=1, source_target_pairs={{0,4},{4,0},{8,12},{12,8},{16,20},{20,16},{24,28},{28,24},{1,5},{5... | collective-permute-start | bytes 1572872 | tf_op jit(solution)/shard_map/ppermute | solution.py:444
  815.3 45.0 %collective-permute-start.82 = (bf16[2,512,256]{2,1,0:T(8,128)(2,1)}, bf16[2,512,256]{2,1,0:T(8,128)(2,1)}, u32[]{:S(2)}, u32[]{:S(2)}) collective-permute-start(bf16[2,512,256]{2,1,0:T(8,128)(2,1)} %pad_maximum_fusion.44), channel_id=1, source_target_pairs={{0,4},{4,0},{8,12},{12,8},{16,20},{20,16},{24,28},{28,24},{1,5},{5... | collective-permute-start | bytes 1572872 | tf_op jit(solution)/shard_map/ppermute | solution.py:444
  817.6 42.7 %collective-permute-start.83 = (bf16[2,512,256]{2,1,0:T(8,128)(2,1)}, bf16[2,512,256]{2,1,0:T(8,128)(2,1)S(1)}, u32[]{:S(2)}, u32[]{:S(2)}) collective-permute-start(bf16[2,512,256]{2,1,0:T(8,128)(2,1)} %pad_maximum_fusion.45), channel_id=1, source_target_pairs={{0,4},{4,0},{8,12},{12,8},{16,20},{20,16},{24,28},{28,24},{1,5},{5... | collective-permute-start | bytes 1572872 | tf_op jit(solution)/shard_map/ppermute | solution.py:444
  880.2 127.9 %all-to-all-start.2 = ((bf16[3,88,2048]{1,0,2:T(4,128)(2,1)}), bf16[3,88,2048]{1,0,2:T(4,128)(2,1)}, u32[]{:S(2)}, u32[]{:S(2)}) async-start(bf16[3,88,2048]{1,0,2:T(4,128)(2,1)} %copy.286), calls=%async_computation.2 | async-start | bytes 4194304 | tf_op jit(solution)/shard_map/all_to_all | solution.py:1151
  949.4 56.1 %collective-permute-start.90 = (bf16[2,128,2048]{2,1,0:T(8,128)(2,1)}, bf16[2,128,2048]{2,1,0:T(8,128)(2,1)}, u32[]{:S(2)}, u32[]{:S(2)}) collective-permute-start(bf16[2,128,2048]{2,1,0:T(8,128)(2,1)} %fusion.34), channel_id=1, source_target_pairs={{0,1},{1,0},{2,3},{3,2},{4,5},{5,4},{6,7},{7,6},{8,9},{9,8},{10,11... | collective-permute-start | bytes 3145736 | tf_op jit(solution)/shard_map/ppermute | solution.py:444
  951.7 51.5 %collective-permute-start.104 = (bf16[2,256,768]{2,1,0:T(8,128)(2,1)S(1)}, bf16[2,256,768]{2,1,0:T(8,128)(2,1)S(1)}, u32[]{:S(2)}, u32[]{:S(2)}) collective-permute-start(bf16[2,256,768]{2,1,0:T(8,128)(2,1)S(1)} %pad_maximum_fusion.38), channel_id=1, source_target_pairs={{0,4},{4,0},{8,12},{12,8},{16,20},{20,16},{24,28},{28,24},{1,5},{5... | collective-permute-start | bytes 2359304 | tf_op jit(solution)/shard_map/ppermute | solution.py:444
  952.2 25.6 %collective-permute-start.109 = (bf16[2,64,1024]{2,1,0:T(8,128)(2,1)S(1)}, bf16[2,64,1024]{2,1,0:T(8,128)(2,1)S(1)}, u32[]{:S(2)}, u32[]{:S(2)}) collective-permute-start(bf16[2,64,1024]{2,1,0:T(8,128)(2,1)S(1)} %pad_maximum_fusion.47), channel_id=1, source_target_pairs={{0,4},{4,0},{8,12},{12,8},{16,20},{20,16},{24,28},{28,24},{1,5},{5... | collective-permute-start | bytes 786440 | tf_op jit(solution)/shard_map/ppermute | solution.py:444
  954.0 37.8 %collective-permute-start.108 = (bf16[2,64,1024]{2,1,0:T(8,128)(2,1)S(1)}, bf16[2,64,1024]{2,1,0:T(8,128)(2,1)S(1)}, u32[]{:S(2)}, u32[]{:S(2)}) collective-permute-start(bf16[2,64,1024]{2,1,0:T(8,128)(2,1)S(1)} %pad_maximum_fusion.46), channel_id=1, source_target_pairs={{0,4},{4,0},{8,12},{12,8},{16,20},{20,16},{24,28},{28,24},{1,5},{5... | collective-permute-start | bytes 786440 | tf_op jit(solution)/shard_map/ppermute | solution.py:444
  955.6 40.0 %collective-permute-start.113 = (bf16[512,256]{1,0:T(8,128)(2,1)S(1)}, bf16[512,256]{1,0:T(8,128)(2,1)S(1)}, u32[]{:S(2)}, u32[]{:S(2)}) collective-permute-start(bf16[512,256]{1,0:T(8,128)(2,1)S(1)} %fusion.91), channel_id=1, source_target_pairs={{0,8},{4,12},{8,16},{12,20},{16,24},{20,28},{24,0},{28,4},{1,9},{5... | collective-permute-start | bytes 786440 | tf_op jit(solution)/shard_map/ppermute | solution.py:461
  991.8 25.7 %collective-permute-start.94 = (bf16[2,160,2048]{2,1,0:T(8,128)(2,1)S(1)}, bf16[2,160,2048]{2,1,0:T(8,128)(2,1)}, u32[]{:S(2)}, u32[]{:S(2)}) collective-permute-start(bf16[2,160,2048]{2,1,0:T(8,128)(2,1)S(1)} %dynamic-slice_bitcast_fusion), channel_id=1, source_target_pairs={{0,1},{1,0},{2,3},{3,2},{4,5},{5,4},{6,7},{7,6},{8,9},{9,8},{10,11... | collective-permute-start | bytes 3932168 | tf_op jit(solution)/shard_map/ppermute | solution.py:444
  995.1 39.1 %collective-permute-start.103 = (bf16[2,256,768]{2,1,0:T(8,128)(2,1)}, bf16[2,256,768]{2,1,0:T(8,128)(2,1)}, u32[]{:S(2)}, u32[]{:S(2)}) collective-permute-start(bf16[2,256,768]{2,1,0:T(8,128)(2,1)} %pad_maximum_fusion.37), channel_id=1, source_target_pairs={{0,4},{4,0},{8,12},{12,8},{16,20},{20,16},{24,28},{28,24},{1,5},{5... | collective-permute-start | bytes 2359304 | tf_op jit(solution)/shard_map/ppermute | solution.py:444
  1007.8 28.1 %collective-permute-start.91 = (bf16[128,2048]{1,0:T(8,128)(2,1)}, bf16[128,2048]{1,0:T(8,128)(2,1)}, u32[]{:S(2)}, u32[]{:S(2)}) collective-permute-start(bf16[128,2048]{1,0:T(8,128)(2,1)} %fusion.81), channel_id=1, source_target_pairs={{0,2},{1,3},{2,0},{3,1},{4,6},{5,7},{6,4},{7,5},{8,10},{9,11},{10,... | collective-permute-start | bytes 1572872 | tf_op jit(solution)/shard_map/ppermute | solution.py:444
  (258 other events, 3165.1 us)

commit v4 on v3

--- a/solution.py
+++ b/solution.py
@@ -619,6 +619,7 @@
         except StopIteration as stop:
             (whole,) = stop.value
             break
+    (whole,) = yield [whole]
     (far,) = yield [y_hop(whole)]
     pair = jnp.stack([whole, far])
     (far,) = yield [core_hop(pair)]
@@ -739,15 +740,8 @@
 
     flow = Flow()
     side_task = flow.launch(side_ring(side, dp_index, tensor_index))
-    unit = w_output.shape[1]
-    query_rows = w_query.shape[0] * w_query.shape[1] // unit
-    expand_rows = w_expand.shape[0] * w_expand.shape[1] // unit
-
-    def columns(values):
-        return [values[:, i : i + unit] for i in range(0, values.shape[1], unit)]
-
-    pack = jnp.concatenate(columns(w_query) + columns(w_expand) + [w_output])
-    weight_task = flow.launch(dp_ring([pack], [0], dp_index))
+    weights = flow.close((w_query, w_expand, w_output))
+    weight_task = flow.launch(dp_ring(weights, [0, 0, 1], dp_index))
     for _ in range(2):
         flow.close(())
 
@@ -803,17 +797,7 @@
         )
     )
 
-    (packed,) = weight_task.result
-    packed = packed.reshape(dp_size, pack.shape[0], unit)
-
-    def rejoined(values, rows):
-        values = values.reshape(dp_size, -1, rows, unit).transpose(0, 2, 1, 3)
-        return values.reshape(dp_size * rows, -1)
-
-    query_weight = rejoined(packed[:, :query_rows], w_query.shape[0])
-    expand_weight = rejoined(packed[:, query_rows : query_rows + expand_rows], w_expand.shape[0])
-    output_weight = packed[:, query_rows + expand_rows :].transpose(1, 0, 2)
-    output_weight = output_weight.reshape(w_output.shape[0], width)
+    query_weight, expand_weight, output_weight = weight_task.result
     cot_tasks = [flow.launch(plane_gather(cot_own))]
     cot_piece = cot_pass.result
     cot_pass = flow.launch(passing(cot_piece))
@@ -961,29 +945,34 @@
     in_moving = flow.launch(
         passing(low(in_tasks[2].result + in_moving.result.astype(jnp.float32)))
     )
-    kept_parts = flow.close(kept_parts)
-    gate_weight_grad = sum(
-        jnp.einsum("tf,td->fd", gate_grad, rows, preferred_element_type=jnp.float32)
-        for rows, _, gate_grad, _, _ in kept_parts
-    )
-    gate_weight_grad, kept_parts = flow.close((gate_weight_grad, kept_parts))
-    flow.close(())
-    in_moving = flow.launch(
-        passing(low(in_tasks[3].result + in_moving.result.astype(jnp.float32)))
-    )
-    out_moving = flow.launch(passing(low(out_tasks[1].result)))
-
-    kept_parts = flow.close(kept_parts)
-    ffn_sum = in_tasks[0].result + in_moving.result.astype(jnp.float32)
     gate_sums = jnp.stack(gate_parts).reshape(-1, exp_here, 2, 2, 2, own_count)
     gate_sums = gate_sums[:, :, 0] + core_hop(gate_sums[:, :, 1])
     gate_sums = gate_sums[:, :, 0] + y_hop(gate_sums[:, :, 1])
     block = jnp.arange(dp_size, dtype=jnp.int32)
     place = ((dp_index // 2 - block // 2) % planes) * 2 + (block + dp_index) % 2
     gate_sums = gate_sums.transpose(0, 2, 1, 3).reshape(dp_size, exp_here, own_count)[place]
+    gate_weight_grad = sum(
+        jnp.einsum("tf,td->fd", gate_grad, rows, preferred_element_type=jnp.float32)
+        for rows, _, gate_grad, _, _ in kept_parts
+    )
+    gate_weight_grad, kept_parts, gate_sums = flow.close(
+        (gate_weight_grad, kept_parts, gate_sums)
+    )
     gate_sums = lax.all_to_all(gate_sums, "dp", split_axis=0, concat_axis=0, tiled=True)
     gate_sums = gate_sums.reshape(experts, own_count).T
-
+    up_weight_grad = sum(
+        jnp.einsum("tf,td->fd", up_grad, rows, preferred_element_type=jnp.float32)
+        for rows, _, _, up_grad, _ in kept_parts
+    )
+    gate_sums, up_weight_grad, kept_parts = flow.close((gate_sums, up_weight_grad, kept_parts))
+    flow.close(())
+    in_moving = flow.launch(
+        passing(low(in_tasks[3].result + in_moving.result.astype(jnp.float32)))
+    )
+    out_moving = flow.launch(passing(low(out_tasks[1].result)))
+
+    kept_parts = flow.close(kept_parts)
+    ffn_sum = in_tasks[0].result + in_moving.result.astype(jnp.float32)
     probs_own, gates_own, picked_own = gating(normed_own_low, standing_own)
     gate_sums = jnp.where(standing_own > 1.5, gate_sums, 0.0)
     picked_grad = (
@@ -999,29 +988,37 @@
     ffn_in = ffn_sum + jnp.dot(logit_grad, router_weight, preferred_element_type=jnp.float32)
     ffn_resid_grad, gain_ffn_grad = norm_backward(resid_own, inverse_own, gain_ffn_f, ffn_in)
     mid_grad_own = cot_own.astype(jnp.float32) + ffn_resid_grad
-    mid_low, kept_parts = flow.close(
-        (tensor_gather(low(mid_grad_own), tensor_index), kept_parts)
-    )
-    up_weight_grad = sum(
-        jnp.einsum("tf,td->fd", up_grad, rows, preferred_element_type=jnp.float32)
-        for rows, _, _, up_grad, _ in kept_parts
+    shared_parts = [gate_weight_grad, up_weight_grad]
+    mid_low, kept_parts, shared_parts = flow.close(
+        (tensor_gather(low(mid_grad_own), tensor_index), kept_parts, shared_parts)
     )
     out_moving = flow.launch(
         passing(low(out_tasks[2].result + out_moving.result.astype(jnp.float32)))
     )
-
+    down_weight_grad = sum(
+        jnp.einsum("tf,td->fd", act_scaled, cots, preferred_element_type=jnp.float32)
+        for _, cots, _, _, act_scaled in kept_parts[: planes // 2]
+    )
+
+    def shared_sum(grads):
+        grads = jnp.stack([low(grad[routed_here:]) for grad in grads])
+        return lax.all_to_all(grads, "dp", split_axis=2, concat_axis=1, tiled=True).astype(
+            jnp.float32
+        )
+
+    shared_grads = shared_sum(shared_parts)
     output_weight_grad = jnp.einsum(
         "th,td->hd", heads_low, mid_low, preferred_element_type=jnp.float32
     )
     heads_grad = low(
         jnp.einsum("td,hd->th", mid_low, output_weight, preferred_element_type=jnp.float32)
     ).reshape(tok_count, heads_here, V_HEAD)
-    heads_grad, output_weight_grad, up_weight_grad, kept_parts = flow.close(
-        (heads_grad, output_weight_grad, up_weight_grad, kept_parts)
-    )
-    down_weight_grad = sum(
+    heads_grad, output_weight_grad, down_weight_grad, kept_parts = flow.close(
+        (heads_grad, output_weight_grad, down_weight_grad, kept_parts)
+    )
+    down_weight_grad += sum(
         jnp.einsum("tf,td->fd", act_scaled, cots, preferred_element_type=jnp.float32)
-        for _, cots, _, _, act_scaled in kept_parts
+        for _, cots, _, _, act_scaled in kept_parts[planes // 2 :]
     )
     output_task = flow.launch(
         dp_scatter_steps(
@@ -1145,11 +1142,8 @@
         routed_grad(up_weight_grad).swapaxes(1, 2),
         routed_grad(down_weight_grad),
     )
-    shared_grads = jnp.stack(
-        [low(grad[routed_here:]) for grad in (gate_weight_grad, up_weight_grad, down_weight_grad)]
-    )
-    shared_grads = lax.all_to_all(
-        shared_grads, "dp", split_axis=2, concat_axis=1, tiled=True
+    shared_down_grad = lax.all_to_all(
+        low(down_weight_grad[routed_here:]), "dp", split_axis=1, concat_axis=0, tiled=True
     ).astype(jnp.float32)
 
     return (
@@ -1165,7 +1159,7 @@
         router_share,
         shared_grads[0].T,
         shared_grads[1].T,
-        shared_grads[2],
+        shared_down_grad,
         *routed_grads,
     )
 

time: 1090 us -> 1020 us (0.936)
  waiting for transfers between devices: 328 us -> 284 us
  local copies, waits for them, and re-layouts: 193 us -> 155 us
    ppermute x30 -> x36, waiting for transfers between devices: 134 us -> 103 us  [z_hop(): lax.ppermute(values, 'dp', [(i, (i + 2) % count) for i in range(count)])]
    unnamed x421 -> x404, local copies, waits for them, and re-layouts: 57.2 us -> 37.3 us
    dynamic_update_slice x16 -> x32, local copies, waits for them, and re-layouts: 15.8 us -> 31.6 us  [laid_out(): whole = lax.dynamic_update_slice_in_dim(whole, piece, home * extent, axis)]
    add x0 -> x1, other arithmetic: none -> 12.6 us  [body_dense(): down_weight_grad += sum((jnp.einsum('tf,td->fd', act_scaled, cots, prefer...]
    transpose x3 -> x0, local copies, waits for them, and re-layouts: 11.8 us -> none  [the longest x2 6.99 us: body_dense(): output_weight = packed[:, query_rows + expand_rows:].transpose(1, 0, 2)]
    ppermute x30 -> x36, starting transfers between devices: 46.2 us -> 37 us  [z_hop(): lax.ppermute(values, 'dp', [(i, (i + 2) % count) for i in range(count)])]
    ppermute x84 -> x92, starting transfers between devices: 66 us -> 74.8 us  [hop(): lax.ppermute(values, axis, [(i, i ^ bit) for i in range(lax.axis_size(axi...]
    convert_element_type x32 -> x30, other arithmetic: 53.1 us -> 47 us  [low(): return values.astype(jnp.bfloat16)]
  transfers between devices with their start and end apart: 117 -> 132, of which waited for: 52 -> 53; matrix products, arithmetic and copies ran while one was open for 50% -> 50% of each run, Pallas kernels for 0% -> 0%
where the time goes in v4:
time: 1020 us; the launch traced here: 1010 us
  waiting for transfers between devices  284 us (28%)
  matrix products  276 us (27%)
  other arithmetic  161 us (16%)
  local copies, waits for them, and re-layouts  155 us (15%)
  starting transfers between devices  130 us (13%)
    ppermute x92, waiting for transfers between devices, hop(): lax.ppermute(values, axis, [(i, i ^ bit) for i in range(lax.axis_size(axi...  182 us
    ppermute x36, waiting for transfers between devices, z_hop(): lax.ppermute(values, 'dp', [(i, (i + 2) % count) for i in range(count)])  103 us
    ppermute x92, starting transfers between devices, hop(): lax.ppermute(values, axis, [(i, i ^ bit) for i in range(lax.axis_size(axi...  74.8 us
    convert_element_type x30, other arithmetic, low(): return values.astype(jnp.bfloat16)  47 us
    unnamed x404, local copies, waits for them, and re-layouts  37.3 us
    ppermute x36, starting transfers between devices, z_hop(): lax.ppermute(values, 'dp', [(i, (i + 2) % count) for i in range(count)])  37 us
    dot_general x4, matrix products, body_dense(): jnp.einsum('td,fd->tf', cots, down_weight, preferred_element_type=jnp.flo...  33.5 us
    dynamic_update_slice x32, local copies, waits for them, and re-layouts, laid_out(): whole = lax.dynamic_update_slice_in_dim(whole, piece, home * extent, axis)  31.6 us
  transfers between devices with their start and end apart: 132, of which 53 were waited for; matrix products, arithmetic and copies ran while one was open for 50% of the time, Pallas kernels for 0%

profile of v4, /device:TPU:0, one launch (start us, length us, event | category | flops | bytes accessed | tf_op | source)
XLA Modules:
  0.0 1011.9 jit_solution(13015279688347856570)
XLA Ops:
  16.7 6.2 collective-permute-done.3
  24.7 6.2 collective-permute-done.5
  73.9 8.3 collective-permute-done.16
  136.5 15.2 %collective-permute-done.28 = bf16[64,1024]{1,0:T(8,128)(2,1)S(1)} collective-permute-done((bf16[64,1024]{1,0:T(8,128)(2,1)S(1)}, bf16[64,1024]{1,0:T(8,128)(2,1)S(1)}, u32[]{:S(2)}, u32[]{:S(2)}) %collective-permute-start.28) | collective-permute-done | bytes 131104 | tf_op jit(solution)/shard_map/ppermute | solution.py:444
  186.4 11.2 %collective-permute-done.35 = bf16[128,2048]{1,0:T(8,128)(2,1)} collective-permute-done((bf16[128,2048]{1,0:T(8,128)(2,1)}, bf16[128,2048]{1,0:T(8,128)(2,1)}, u32[]{:S(2)}, u32[]{:S(2)}) %collective-permute-start.35) | collective-permute-done | bytes 524320 | tf_op jit(solution)/shard_map/ppermute | solution.py:461
  216.2 11.3 %collective-permute-done.37 = bf16[128,2048]{1,0:T(8,128)(2,1)S(1)} collective-permute-done((bf16[128,2048]{1,0:T(8,128)(2,1)S(1)}, bf16[128,2048]{1,0:T(8,128)(2,1)S(1)}, u32[]{:S(2)}, u32[]{:S(2)}) %collective-permute-start.37) | collective-permute-done | bytes 524320 | tf_op jit(solution)/shard_map/ppermute | solution.py:444
  251.2 7.7 collective-permute-done.44
  274.9 15.7 %collective-permute-done.46 = bf16[256,2048]{1,0:T(8,128)(2,1)S(1)} collective-permute-done((bf16[256,2048]{1,0:T(8,128)(2,1)S(1)}, bf16[256,2048]{1,0:T(8,128)(2,1)S(1)}, u32[]{:S(2)}, u32[]{:S(2)}) %collective-permute-start.46) | collective-permute-done | bytes 1048608 | tf_op jit(solution)/shard_map/ppermute | solution.py:444
  302.3 8.1 multiply_convert_fusion.11
  321.1 6.9 fusion.237
  332.7 7.0 add_convert_fusion.3
  339.7 6.7 fusion.240
  361.6 5.6 fusion.242
  367.2 6.2 collective-permute-done.54
  386.8 8.8 multiply_convert_fusion.8
  400.5 8.7 collective-permute-done.60
  415.0 7.1 fusion.241
  425.9 9.4 add_convert_fusion.2
  435.3 8.5 fusion.244
  463.8 7.0 collective-permute-done.64
  483.8 8.4 multiply_convert_fusion.5
  492.3 7.0 convolution_convert_fusion.1
  508.7 6.9 fusion.247
  515.5 7.5 add_convert_fusion.1
  543.1 5.9 fusion.248
  555.6 14.7 %select_reduce_fusion.1 = (f32[1024]{0:T(1024)S(1)}, f32[1024]{0:T(1024)S(1)}, f32[1024]{0:T(1024)S(1)}, f32[1024]{0:T(1024)S(1)}, f32[1024]{0:T(1024)S(1)}, /*i...) fusion(pred[792]{0:T(1024)(128)(4,1)S(1)} %copy-done.172, ...), kind=kOutput, calls=%fused_computation.43 | convolution fusion | flops 3351887872 | bytes 39922784 | tf_op jit(solution)/shard_map/td,fd->tf/dot_general | solution.py:913
  575.3 6.1 convolution_convert_fusion
  589.0 7.0 fusion.251
  596.1 7.1 add_convert_fusion
  612.4 8.9 add_add_fusion.2
  621.3 15.1 %collective-permute-done.80 = bf16[2,128,2048]{2,1,0:T(8,128)(2,1)S(1)} collective-permute-done((bf16[2,128,2048]{2,1,0:T(8,128)(2,1)S(1)}, bf16[2,128,2048]{2,1,0:T(8,128)(2,1)S(1)}, u32[]{:S(2)}, u32[]{:S(2)}) %collective-permute-start.80) | collective-permute-done | bytes 1048608 | tf_op jit(solution)/shard_map/ppermute | solution.py:444
  660.6 7.8 add_add_fusion.1
  675.8 6.9 collective-permute-done.85
  692.3 9.2 collective-permute-done.88
  701.5 7.7 collective-permute-done.87
  728.6 11.1 %collective-permute-done.91 = bf16[128,2048]{1,0:T(8,128)(2,1)S(1)} collective-permute-done((bf16[128,2048]{1,0:T(8,128)(2,1)S(1)}, bf16[128,2048]{1,0:T(8,128)(2,1)S(1)}, u32[]{:S(2)}, u32[]{:S(2)}) %collective-permute-start.91) | collective-permute-done | bytes 524320 | tf_op jit(solution)/shard_map/ppermute | solution.py:444
  761.0 5.6 convolution_add_fusion
  772.3 6.8 collective-permute-done.93
  804.5 12.6 %add_add_fusion = f32[792,2048]{1,0:T(8,128)} fusion(f32[792,2048]{1,0:T(8,128)} %convolution_add_fusion, f32[792,2048]{1,0:T(8,128)} %fusion.257, f32[792,2048]{1,0:T(8,128)} %fusion.258), kind=kLoop, calls=%fused_computation.10 | loop fusion | flops 3244032 | bytes 25952256 | tf_op jit(solution)/shard_map/add | solution.py:1019
  817.0 6.4 multiply_convert_fusion
  831.1 6.0 slice.577
  862.2 5.9 collective-permute-done.98
  892.1 6.5 multiply_reduce_fusion
  913.0 6.5 collective-permute-done.124
  922.2 12.1 %collective-permute-done.122 = bf16[2,64,1024]{2,1,0:T(8,128)(2,1)S(1)} collective-permute-done((bf16[2,64,1024]{2,1,0:T(8,128)(2,1)S(1)}, bf16[2,64,1024]{2,1,0:T(8,128)(2,1)S(1)}, u32[]{:S(2)}, u32[]{:S(2)}) %collective-permute-start.122) | collective-permute-done | bytes 262176 | tf_op jit(solution)/shard_map/ppermute | solution.py:444
  939.8 9.9 collective-permute-done.119
  953.5 7.3 collective-permute-done.120
  996.1 6.3 collective-permute-done.115
  (996 shorter events, 605.8 us)
Async XLA Ops:
  56.9 38.1 %collective-permute-start.14 = (bf16[2,160,2048]{2,1,0:T(8,128)(2,1)}, bf16[2,160,2048]{2,1,0:T(8,128)(2,1)}, u32[]{:S(2)}, u32[]{:S(2)}) collective-permute-start(bf16[2,160,2048]{2,1,0:T(8,128)(2,1)} %pad_maximum_fusion.16), channel_id=1, source_target_pairs={{0,1},{1,0},{2,3},{3,2},{4,5},{5,4},{6,7},{7,6},{8,9},{9,8},{10,11... | collective-permute-start | bytes 3932168 | tf_op jit(solution)/shard_map/ppermute | solution.py:444
  67.6 27.3 %collective-permute-start.15 = (bf16[256,768]{1,0:T(8,128)(2,1)}, bf16[256,768]{1,0:T(8,128)(2,1)S(1)}, u32[]{:S(2)}, u32[]{:S(2)}) collective-permute-start(bf16[256,768]{1,0:T(8,128)(2,1)} %collective-permute-done.11), channel_id=1, source_target_pairs={{0,4},{4,0},{8,12},{12,8},{16,20},{20,16},{24,28},{28,24},{1,5},{5... | collective-permute-start | bytes 1179656 | tf_op jit(solution)/shard_map/ppermute | solution.py:444
  69.0 25.9 %collective-permute-start.18 = (bf16[256,768]{1,0:T(8,128)(2,1)}, bf16[256,768]{1,0:T(8,128)(2,1)}, u32[]{:S(2)}, u32[]{:S(2)}) collective-permute-start(bf16[256,768]{1,0:T(8,128)(2,1)} %collective-permute-done.11), channel_id=1, source_target_pairs={{0,8},{4,12},{8,16},{12,20},{16,24},{20,28},{24,0},{28,4},{1,9},{5... | collective-permute-start | bytes 1179656 | tf_op jit(solution)/shard_map/ppermute | solution.py:461
  94.9 29.7 %collective-permute-start.21 = (bf16[256,768]{1,0:T(8,128)(2,1)}, bf16[256,768]{1,0:T(8,128)(2,1)}, u32[]{:S(2)}, u32[]{:S(2)}) collective-permute-start(bf16[256,768]{1,0:T(8,128)(2,1)} %collective-permute-done.18), channel_id=1, source_target_pairs={{0,4},{4,0},{8,12},{12,8},{16,20},{20,16},{24,28},{28,24},{1,5},{5... | collective-permute-start | bytes 1179656 | tf_op jit(solution)/shard_map/ppermute | solution.py:444
  95.6 29.1 %collective-permute-start.24 = (bf16[256,768]{1,0:T(8,128)(2,1)}, bf16[256,768]{1,0:T(8,128)(2,1)}, u32[]{:S(2)}, u32[]{:S(2)}) collective-permute-start(bf16[256,768]{1,0:T(8,128)(2,1)} %collective-permute-done.18), channel_id=1, source_target_pairs={{0,8},{4,12},{8,16},{12,20},{16,24},{20,28},{24,0},{28,4},{1,9},{5... | collective-permute-start | bytes 1179656 | tf_op jit(solution)/shard_map/ppermute | solution.py:461
  95.6 27.6 %collective-permute-start.23 = (bf16[512,256]{1,0:T(8,128)(2,1)}, bf16[512,256]{1,0:T(8,128)(2,1)}, u32[]{:S(2)}, u32[]{:S(2)}) collective-permute-start(bf16[512,256]{1,0:T(8,128)(2,1)} %collective-permute-done.20), channel_id=1, source_target_pairs={{0,4},{4,0},{8,12},{12,8},{16,20},{20,16},{24,28},{28,24},{1,5},{5... | collective-permute-start | bytes 786440 | tf_op jit(solution)/shard_map/ppermute | solution.py:444
  97.0 27.6 %collective-permute-start.26 = (bf16[512,256]{1,0:T(8,128)(2,1)}, bf16[512,256]{1,0:T(8,128)(2,1)}, u32[]{:S(2)}, u32[]{:S(2)}) collective-permute-start(bf16[512,256]{1,0:T(8,128)(2,1)} %collective-permute-done.20), channel_id=1, source_target_pairs={{0,8},{4,12},{8,16},{12,20},{16,24},{20,28},{24,0},{28,4},{1,9},{5... | collective-permute-start | bytes 786440 | tf_op jit(solution)/shard_map/ppermute | solution.py:461
  123.2 48.9 %collective-permute-start.31 = (bf16[128,2048]{1,0:T(8,128)(2,1)}, bf16[128,2048]{1,0:T(8,128)(2,1)S(1)}, u32[]{:S(2)}, u32[]{:S(2)}) collective-permute-start(bf16[128,2048]{1,0:T(8,128)(2,1)} %constant_dynamic-slice_fusion.5), channel_id=1, source_target_pairs={{0,4},{4,0},{8,12},{12,8},{16,20},{20,16},{24,28},{28,24},{1,5},{5... | collective-permute-start | bytes 1572872 | tf_op jit(solution)/shard_map/ppermute | solution.py:444
  124.7 27.1 %collective-permute-start.27 = (bf16[256,768]{1,0:T(8,128)(2,1)}, bf16[256,768]{1,0:T(8,128)(2,1)S(1)}, u32[]{:S(2)}, u32[]{:S(2)}) collective-permute-start(bf16[256,768]{1,0:T(8,128)(2,1)} %collective-permute-done.24), channel_id=1, source_target_pairs={{0,4},{4,0},{8,12},{12,8},{16,20},{20,16},{24,28},{28,24},{1,5},{5... | collective-permute-start | bytes 1179656 | tf_op jit(solution)/shard_map/ppermute | solution.py:444
  125.3 26.4 %collective-permute-start.29 = (bf16[512,256]{1,0:T(8,128)(2,1)}, bf16[512,256]{1,0:T(8,128)(2,1)S(1)}, u32[]{:S(2)}, u32[]{:S(2)}) collective-permute-start(bf16[512,256]{1,0:T(8,128)(2,1)} %collective-permute-done.26), channel_id=1, source_target_pairs={{0,4},{4,0},{8,12},{12,8},{16,20},{20,16},{24,28},{28,24},{1,5},{5... | collective-permute-start | bytes 786440 | tf_op jit(solution)/shard_map/ppermute | solution.py:444
  126.8 25.0 %collective-permute-start.28 = (bf16[64,1024]{1,0:T(8,128)(2,1)S(1)}, bf16[64,1024]{1,0:T(8,128)(2,1)S(1)}, u32[]{:S(2)}, u32[]{:S(2)}) collective-permute-start(bf16[64,1024]{1,0:T(8,128)(2,1)S(1)} %collective-permute-done.25), channel_id=1, source_target_pairs={{0,4},{4,0},{8,12},{12,8},{16,20},{20,16},{24,28},{28,24},{1,5},{5... | collective-permute-start | bytes 393224 | tf_op jit(solution)/shard_map/ppermute | solution.py:444
  151.8 34.5 %collective-permute-start.34 = (bf16[128,2048]{1,0:T(8,128)(2,1)}, bf16[128,2048]{1,0:T(8,128)(2,1)}, u32[]{:S(2)}, u32[]{:S(2)}) collective-permute-start(bf16[128,2048]{1,0:T(8,128)(2,1)} %collective-permute-done.30), channel_id=1, source_target_pairs={{0,4},{4,0},{8,12},{12,8},{16,20},{20,16},{24,28},{28,24},{1,5},{5... | collective-permute-start | bytes 1572872 | tf_op jit(solution)/shard_map/ppermute | solution.py:444
  156.7 52.4 %all-to-all-start = ((bf16[3,704,256]{2,0,1:T(4,128)(2,1)}), bf16[3,704,256]{2,0,1:T(4,128)(2,1)}, u32[]{:S(2)}, u32[]{:S(2)}) async-start(bf16[3,704,256]{2,0,1:T(4,128)(2,1)} %copy.247), calls=%async_computation | async-start | bytes 2883584 | tf_op jit(solution)/shard_map/all_to_all | solution.py:852
  201.5 27.6 %collective-permute-start.39 = (bf16[128,2048]{1,0:T(8,128)(2,1)}, bf16[128,2048]{1,0:T(8,128)(2,1)}, u32[]{:S(2)}, u32[]{:S(2)}) collective-permute-start(bf16[128,2048]{1,0:T(8,128)(2,1)} %collective-permute-done.32), channel_id=1, source_target_pairs={{0,4},{4,0},{8,12},{12,8},{16,20},{20,16},{24,28},{28,24},{1,5},{5... | collective-permute-start | bytes 1572872 | tf_op jit(solution)/shard_map/ppermute | solution.py:444
  206.7 139.9 %collective-permute-start.53 = (bf16[128,2048]{1,0:T(8,128)(2,1)}, bf16[128,2048]{1,0:T(8,128)(2,1)}, u32[]{:S(2)}, u32[]{:S(2)}) collective-permute-start(bf16[128,2048]{1,0:T(8,128)(2,1)} %collective-permute-done.35), channel_id=1, source_target_pairs={{0,4},{4,0},{8,12},{12,8},{16,20},{20,16},{24,28},{28,24},{1,5},{5... | collective-permute-start | bytes 1572872 | tf_op jit(solution)/shard_map/ppermute | solution.py:444
  248.3 26.6 %collective-permute-start.47 = (bf16[128,2048]{1,0:T(8,128)(2,1)S(1)}, bf16[128,2048]{1,0:T(8,128)(2,1)S(1)}, u32[]{:S(2)}, u32[]{:S(2)}) collective-permute-start(bf16[128,2048]{1,0:T(8,128)(2,1)S(1)} %collective-permute-done.42), channel_id=1, source_target_pairs={{0,4},{4,0},{8,12},{12,8},{16,20},{20,16},{24,28},{28,24},{1,5},{5... | collective-permute-start | bytes 1572872 | tf_op jit(solution)/shard_map/ppermute | solution.py:444
  248.7 26.2 %collective-permute-start.48 = (bf16[128,2048]{1,0:T(8,128)(2,1)S(1)}, bf16[128,2048]{1,0:T(8,128)(2,1)S(1)}, u32[]{:S(2)}, u32[]{:S(2)}) collective-permute-start(bf16[128,2048]{1,0:T(8,128)(2,1)S(1)} %collective-permute-done.42), channel_id=1, source_target_pairs={{0,8},{4,12},{8,16},{12,20},{16,24},{20,28},{24,0},{28,4},{1,9},{5... | collective-permute-start | bytes 1572872 | tf_op jit(solution)/shard_map/ppermute | solution.py:461
  265.2 25.5 %collective-permute-start.46 = (bf16[256,2048]{1,0:T(8,128)(2,1)S(1)}, bf16[256,2048]{1,0:T(8,128)(2,1)S(1)}, u32[]{:S(2)}, u32[]{:S(2)}) collective-permute-start(bf16[256,2048]{1,0:T(8,128)(2,1)S(1)} %pad_maximum_fusion.19), channel_id=1, source_target_pairs={{0,2},{1,3},{2,0},{3,1},{4,6},{5,7},{6,4},{7,5},{8,10},{9,11},{10,... | collective-permute-start | bytes 3145736 | tf_op jit(solution)/shard_map/ppermute | solution.py:444
  290.7 76.5 %collective-permute-start.55 = (bf16[128,2048]{1,0:T(8,128)(2,1)S(1)}, bf16[128,2048]{1,0:T(8,128)(2,1)S(1)}, u32[]{:S(2)}, u32[]{:S(2)}) collective-permute-start(bf16[128,2048]{1,0:T(8,128)(2,1)S(1)} %collective-permute-done.48), channel_id=1, source_target_pairs={{0,4},{4,0},{8,12},{12,8},{16,20},{20,16},{24,28},{28,24},{1,5},{5... | collective-permute-start | bytes 1572872 | tf_op jit(solution)/shard_map/ppermute | solution.py:444
  292.3 74.9 %collective-permute-start.56 = (bf16[128,2048]{1,0:T(8,128)(2,1)S(1)}, bf16[128,2048]{1,0:T(8,128)(2,1)S(1)}, u32[]{:S(2)}, u32[]{:S(2)}) collective-permute-start(bf16[128,2048]{1,0:T(8,128)(2,1)S(1)} %collective-permute-done.48), channel_id=1, source_target_pairs={{0,8},{4,12},{8,16},{12,20},{16,24},{20,28},{24,0},{28,4},{1,9},{5... | collective-permute-start | bytes 1572872 | tf_op jit(solution)/shard_map/ppermute | solution.py:461
  321.1 25.5 %collective-permute-start.51 = (bf16[512,2048]{1,0:T(8,128)(2,1)}, bf16[512,2048]{1,0:T(8,128)(2,1)}, u32[]{:S(2)}, u32[]{:S(2)}) collective-permute-start(bf16[512,2048]{1,0:T(8,128)(2,1)} %pad_maximum_fusion.8), channel_id=1, source_target_pairs={{0,1},{1,0},{2,3},{3,2},{4,5},{5,4},{6,7},{7,6},{8,9},{9,8},{10,11... | collective-permute-start | bytes 6291464 | tf_op jit(solution)/shard_map/ppermute | solution.py:444
  347.9 25.5 %collective-permute-start.54 = (bf16[256,2048]{1,0:T(8,128)(2,1)S(1)}, bf16[256,2048]{1,0:T(8,128)(2,1)S(1)}, u32[]{:S(2)}, u32[]{:S(2)}) collective-permute-start(bf16[256,2048]{1,0:T(8,128)(2,1)S(1)} %pad_maximum_fusion.21), channel_id=1, source_target_pairs={{0,2},{1,3},{2,0},{3,1},{4,6},{5,7},{6,4},{7,5},{8,10},{9,11},{10,... | collective-permute-start | bytes 3145736 | tf_op jit(solution)/shard_map/ppermute | solution.py:444
  349.0 24.4 %collective-permute-start.57 = (bf16[2,2,128,2048]{3,2,0,1:T(8,128)(2,1)S(1)}, bf16[2,2,128,2048]{3,2,0,1:T(8,128)(2,1)S(1)}, u32[]{:S(2)}, u32[]{:S(2)}) collective-permute-start(bf16[2,2,128,2048]{3,2,0,1:T(8,128)(2,1)S(1)} %copy.253), channel_id=1, source_target_pairs={{0,1},{1,0},{2,3},{3,2},{4,5},{5,4},{6,7},{7,6},{8,9},{9,8},{10,11... | collective-permute-start | bytes 6291464 | tf_op jit(solution)/shard_map/ppermute | solution.py:444
  373.4 90.4 %collective-permute-start.65 = (bf16[128,2048]{1,0:T(8,128)(2,1)S(1)}, bf16[128,2048]{1,0:T(8,128)(2,1)S(1)}, u32[]{:S(2)}, u32[]{:S(2)}) collective-permute-start(bf16[128,2048]{1,0:T(8,128)(2,1)S(1)} %collective-permute-done.56), channel_id=1, source_target_pairs={{0,4},{4,0},{8,12},{12,8},{16,20},{20,16},{24,28},{28,24},{1,5},{5... | collective-permute-start | bytes 1572872 | tf_op jit(solution)/shard_map/ppermute | solution.py:444
  378.2 31.1 %collective-permute-start.60 = (bf16[2,128,2048]{2,1,0:T(8,128)(2,1)}, bf16[2,128,2048]{2,1,0:T(8,128)(2,1)}, u32[]{:S(2)}, u32[]{:S(2)}) collective-permute-start(bf16[2,128,2048]{2,1,0:T(8,128)(2,1)} %fusion.34), channel_id=1, source_target_pairs={{0,4},{4,0},{8,12},{12,8},{16,20},{20,16},{24,28},{28,24},{1,5},{5... | collective-permute-start | bytes 3145736 | tf_op jit(solution)/shard_map/ppermute | solution.py:444
  380.0 29.2 %collective-permute-start.59 = (bf16[256,2048]{1,0:T(8,128)(2,1)}, bf16[256,2048]{1,0:T(8,128)(2,1)S(1)}, u32[]{:S(2)}, u32[]{:S(2)}) collective-permute-start(bf16[256,2048]{1,0:T(8,128)(2,1)} %pad_maximum_fusion.22), channel_id=1, source_target_pairs={{0,2},{1,3},{2,0},{3,1},{4,6},{5,7},{6,4},{7,5},{8,10},{9,11},{10,... | collective-permute-start | bytes 3145736 | tf_op jit(solution)/shard_map/ppermute | solution.py:444
  383.4 25.9 %collective-permute-start.58 = (bf16[512,2048]{1,0:T(8,128)(2,1)}, bf16[512,2048]{1,0:T(8,128)(2,1)S(1)}, u32[]{:S(2)}, u32[]{:S(2)}) collective-permute-start(bf16[512,2048]{1,0:T(8,128)(2,1)} %pad_maximum_fusion.9), channel_id=1, source_target_pairs={{0,1},{1,0},{2,3},{3,2},{4,5},{5,4},{6,7},{7,6},{8,9},{9,8},{10,11... | collective-permute-start | bytes 6291464 | tf_op jit(solution)/shard_map/ppermute | solution.py:444
  411.7 32.1 %collective-permute-start.62 = (bf16[128,2048]{1,0:T(8,128)(2,1)}, bf16[128,2048]{1,0:T(8,128)(2,1)}, u32[]{:S(2)}, u32[]{:S(2)}) collective-permute-start(bf16[128,2048]{1,0:T(8,128)(2,1)} %fusion.81), channel_id=1, source_target_pairs={{0,2},{1,3},{2,0},{3,1},{4,6},{5,7},{6,4},{7,5},{8,10},{9,11},{10,... | collective-permute-start | bytes 1572872 | tf_op jit(solution)/shard_map/ppermute | solution.py:444
  413.8 30.1 %collective-permute-start.61 = (bf16[512,2048]{1,0:T(8,128)(2,1)}, bf16[512,2048]{1,0:T(8,128)(2,1)}, u32[]{:S(2)}, u32[]{:S(2)}) collective-permute-start(bf16[512,2048]{1,0:T(8,128)(2,1)} %pad_maximum_fusion.10), channel_id=1, source_target_pairs={{0,1},{1,0},{2,3},{3,2},{4,5},{5,4},{6,7},{7,6},{8,9},{9,8},{10,11... | collective-permute-start | bytes 6291464 | tf_op jit(solution)/shard_map/ppermute | solution.py:444
  445.2 25.6 %collective-permute-start.64 = (bf16[256,2048]{1,0:T(8,128)(2,1)S(1)}, bf16[256,2048]{1,0:T(8,128)(2,1)S(1)}, u32[]{:S(2)}, u32[]{:S(2)}) collective-permute-start(bf16[256,2048]{1,0:T(8,128)(2,1)S(1)} %pad_maximum_fusion.23), channel_id=1, source_target_pairs={{0,2},{1,3},{2,0},{3,1},{4,6},{5,7},{6,4},{7,5},{8,10},{9,11},{10,... | collective-permute-start | bytes 3145736 | tf_op jit(solution)/shard_map/ppermute | solution.py:444
  475.6 24.9 %collective-permute-start.69 = (bf16[2,128,2048]{2,1,0:T(8,128)(2,1)}, bf16[2,128,2048]{2,1,0:T(8,128)(2,1)S(1)}, u32[]{:S(2)}, u32[]{:S(2)}) collective-permute-start(bf16[2,128,2048]{2,1,0:T(8,128)(2,1)} %fusion.35), channel_id=1, source_target_pairs={{0,4},{4,0},{8,12},{12,8},{16,20},{20,16},{24,28},{28,24},{1,5},{5... | collective-permute-start | bytes 3145736 | tf_op jit(solution)/shard_map/ppermute | solution.py:444
  477.2 24.6 %collective-permute-start.68 = (bf16[256,2048]{1,0:T(8,128)(2,1)}, bf16[256,2048]{1,0:T(8,128)(2,1)S(1)}, u32[]{:S(2)}, u32[]{:S(2)}) collective-permute-start(bf16[256,2048]{1,0:T(8,128)(2,1)} %pad_maximum_fusion.24), channel_id=1, source_target_pairs={{0,2},{1,3},{2,0},{3,1},{4,6},{5,7},{6,4},{7,5},{8,10},{9,11},{10,... | collective-permute-start | bytes 3145736 | tf_op jit(solution)/shard_map/ppermute | solution.py:444
  550.9 31.8 %collective-permute-start.75 = (bf16[2,128,2048]{2,1,0:T(8,128)(2,1)}, bf16[2,128,2048]{2,1,0:T(8,128)(2,1)}, u32[]{:S(2)}, u32[]{:S(2)}) collective-permute-start(bf16[2,128,2048]{2,1,0:T(8,128)(2,1)} %fusion.36), channel_id=1, source_target_pairs={{0,4},{4,0},{8,12},{12,8},{16,20},{20,16},{24,28},{28,24},{1,5},{5... | collective-permute-start | bytes 3145736 | tf_op jit(solution)/shard_map/ppermute | solution.py:444
  604.9 31.5 %collective-permute-start.81 = (bf16[2,2,128,2048]{3,2,0,1:T(8,128)(2,1)S(1)}, bf16[2,2,128,2048]{3,2,0,1:T(8,128)(2,1)S(1)}, u32[]{:S(2)}, u32[]{:S(2)}) collective-permute-start(bf16[2,2,128,2048]{3,2,0,1:T(8,128)(2,1)S(1)} %copy.269), channel_id=1, source_target_pairs={{0,1},{1,0},{2,3},{3,2},{4,5},{5,4},{6,7},{7,6},{8,9},{9,8},{10,11... | collective-permute-start | bytes 6291464 | tf_op jit(solution)/shard_map/ppermute | solution.py:444
  611.5 24.9 %collective-permute-start.80 = (bf16[2,128,2048]{2,1,0:T(8,128)(2,1)S(1)}, bf16[2,128,2048]{2,1,0:T(8,128)(2,1)S(1)}, u32[]{:S(2)}, u32[]{:S(2)}) collective-permute-start(bf16[2,128,2048]{2,1,0:T(8,128)(2,1)S(1)} %fusion.37), channel_id=1, source_target_pairs={{0,2},{1,3},{2,0},{3,1},{4,6},{5,7},{6,4},{7,5},{8,10},{9,11},{10,... | collective-permute-start | bytes 3145736 | tf_op jit(solution)/shard_map/ppermute | solution.py:444
  640.4 28.0 %collective-permute-start.83 = (bf16[2,128,2048]{2,1,0:T(8,128)(2,1)}, bf16[2,128,2048]{2,1,0:T(8,128)(2,1)}, u32[]{:S(2)}, u32[]{:S(2)}) collective-permute-start(bf16[2,128,2048]{2,1,0:T(8,128)(2,1)} %fusion.38), channel_id=1, source_target_pairs={{0,4},{4,0},{8,12},{12,8},{16,20},{20,16},{24,28},{28,24},{1,5},{5... | collective-permute-start | bytes 3145736 | tf_op jit(solution)/shard_map/ppermute | solution.py:444
  641.5 26.8 %all-to-all-start.1 = ((f32[8,2,128]{2,1,0:T(2,128)}), f32[8,2,128]{2,1,0:T(2,128)S(1)}, u32[]{:S(2)}, u32[]{:S(2)}) async-start(f32[8,2,128]{2,1,0:T(2,128)} %gather_fusion), calls=%async_computation.1 | async-start | bytes 16384 | tf_op jit(solution)/shard_map/all_to_all | solution.py:961
  742.5 80.9 %all-to-all-start.2 = ((bf16[2,88,2048]{1,0,2:T(2,128)(2,1)}), bf16[2,88,2048]{1,0,2:T(2,128)(2,1)}, u32[]{:S(2)}, u32[]{:S(2)}) async-start(bf16[2,88,2048]{1,0,2:T(2,128)(2,1)} %copy.280), calls=%async_computation.2 | async-start | bytes 2097152 | tf_op jit(solution)/shard_map/all_to_all | solution.py:1005
  748.8 30.4 %collective-permute-start.93 = (bf16[128,2048]{1,0:T(8,128)(2,1)S(1)}, bf16[128,2048]{1,0:T(8,128)(2,1)S(1)}, u32[]{:S(2)}, u32[]{:S(2)}) collective-permute-start(bf16[128,2048]{1,0:T(8,128)(2,1)S(1)} %fusion.51), channel_id=1, source_target_pairs={{0,8},{4,12},{8,16},{12,20},{16,24},{20,28},{24,0},{28,4},{1,9},{5... | collective-permute-start | bytes 1572872 | tf_op jit(solution)/shard_map/ppermute | solution.py:461
  753.9 25.3 %collective-permute-start.92 = (bf16[2,128,2048]{2,1,0:T(8,128)(2,1)S(1)}, bf16[2,128,2048]{2,1,0:T(8,128)(2,1)S(1)}, u32[]{:S(2)}, u32[]{:S(2)}) collective-permute-start(bf16[2,128,2048]{2,1,0:T(8,128)(2,1)S(1)} %fusion.40), channel_id=1, source_target_pairs={{0,2},{1,3},{2,0},{3,1},{4,6},{5,7},{6,4},{7,5},{8,10},{9,11},{10,... | collective-permute-start | bytes 3145736 | tf_op jit(solution)/shard_map/ppermute | solution.py:444
  780.2 50.9 %collective-permute-start.97 = (bf16[2,512,256]{2,1,0:T(8,128)(2,1)}, bf16[2,512,256]{2,1,0:T(8,128)(2,1)}, u32[]{:S(2)}, u32[]{:S(2)}) collective-permute-start(bf16[2,512,256]{2,1,0:T(8,128)(2,1)} %pad_maximum_fusion.47), channel_id=1, source_target_pairs={{0,4},{4,0},{8,12},{12,8},{16,20},{20,16},{24,28},{28,24},{1,5},{5... | collective-permute-start | bytes 1572872 | tf_op jit(solution)/shard_map/ppermute | solution.py:444
  782.5 48.6 %collective-permute-start.96 = (bf16[2,512,256]{2,1,0:T(8,128)(2,1)}, bf16[2,512,256]{2,1,0:T(8,128)(2,1)}, u32[]{:S(2)}, u32[]{:S(2)}) collective-permute-start(bf16[2,512,256]{2,1,0:T(8,128)(2,1)} %pad_maximum_fusion.46), channel_id=1, source_target_pairs={{0,4},{4,0},{8,12},{12,8},{16,20},{20,16},{24,28},{28,24},{1,5},{5... | collective-permute-start | bytes 1572872 | tf_op jit(solution)/shard_map/ppermute | solution.py:444
  784.3 46.8 %collective-permute-start.95 = (bf16[128,2048]{1,0:T(8,128)(2,1)}, bf16[128,2048]{1,0:T(8,128)(2,1)}, u32[]{:S(2)}, u32[]{:S(2)}) collective-permute-start(bf16[128,2048]{1,0:T(8,128)(2,1)} %fusion.87), channel_id=1, source_target_pairs={{0,4},{4,0},{8,12},{12,8},{16,20},{20,16},{24,28},{28,24},{1,5},{5... | collective-permute-start | bytes 1572872 | tf_op jit(solution)/shard_map/ppermute | solution.py:444
  789.3 41.8 %collective-permute-start.94 = (bf16[2,128,2048]{2,1,0:T(8,128)(2,1)}, bf16[2,128,2048]{2,1,0:T(8,128)(2,1)}, u32[]{:S(2)}, u32[]{:S(2)}) collective-permute-start(bf16[2,128,2048]{2,1,0:T(8,128)(2,1)} %fusion.41), channel_id=1, source_target_pairs={{0,2},{1,3},{2,0},{3,1},{4,6},{5,7},{6,4},{7,5},{8,10},{9,11},{10,... | collective-permute-start | bytes 3145736 | tf_op jit(solution)/shard_map/ppermute | solution.py:444
  855.4 24.4 %all-to-all-start.3 = ((bf16[88,8,256]{2,0,1:T(8,128)(2,1)}), bf16[88,8,256]{2,0,1:T(8,128)(2,1)}, u32[]{:S(2)}, u32[]{:S(2)}) async-start(bf16[88,8,256]{2,0,1:T(8,128)(2,1)} %bitcast.661), calls=%async_computation.3 | async-start | bytes 720896 | tf_op jit(solution)/shard_map/all_to_all | solution.py:1145
  899.1 50.8 %collective-permute-start.108 = (bf16[2,160,2048]{2,1,0:T(8,128)(2,1)S(1)}, bf16[2,160,2048]{2,1,0:T(8,128)(2,1)S(1)}, u32[]{:S(2)}, u32[]{:S(2)}) collective-permute-start(bf16[2,160,2048]{2,1,0:T(8,128)(2,1)S(1)} %dynamic-slice_bitcast_fusion), channel_id=1, source_target_pairs={{0,1},{1,0},{2,3},{3,2},{4,5},{5,4},{6,7},{7,6},{8,9},{9,8},{10,11... | collective-permute-start | bytes 3932168 | tf_op jit(solution)/shard_map/ppermute | solution.py:444
  906.3 29.2 %collective-permute-start.118 = (bf16[2,256,768]{2,1,0:T(8,128)(2,1)S(1)}, bf16[2,256,768]{2,1,0:T(8,128)(2,1)S(1)}, u32[]{:S(2)}, u32[]{:S(2)}) collective-permute-start(bf16[2,256,768]{2,1,0:T(8,128)(2,1)S(1)} %pad_maximum_fusion.39), channel_id=1, source_target_pairs={{0,4},{4,0},{8,12},{12,8},{16,20},{20,16},{24,28},{28,24},{1,5},{5... | collective-permute-start | bytes 2359304 | tf_op jit(solution)/shard_map/ppermute | solution.py:444
  908.0 29.7 %collective-permute-start.104 = (bf16[2,128,2048]{2,1,0:T(8,128)(2,1)S(1)}, bf16[2,128,2048]{2,1,0:T(8,128)(2,1)S(1)}, u32[]{:S(2)}, u32[]{:S(2)}) collective-permute-start(bf16[2,128,2048]{2,1,0:T(8,128)(2,1)S(1)} %fusion.33), channel_id=1, source_target_pairs={{0,1},{1,0},{2,3},{3,2},{4,5},{5,4},{6,7},{7,6},{8,9},{9,8},{10,11... | collective-permute-start | bytes 3145736 | tf_op jit(solution)/shard_map/ppermute | solution.py:444
  (269 other events, 3266.3 us)

commit v5 on v4

--- a/solution.py
+++ b/solution.py
@@ -527,11 +527,14 @@
     return jnp.concatenate([quarter, far])
 
 
-def plane_gather(own, before=0):
+def plane_gather(own, before=0, windows=1):
     (far,) = yield [x_hop(own)]
     far = yield from held(far, before)
     pair = jnp.concatenate([own, far])
-    (far,) = yield [y_hop(pair)]
+    far = y_hop(pair)
+    for _ in range(windows - 1):
+        yield []
+    (far,) = yield [far]
     quarter = jnp.concatenate([pair, far])
     (far,) = yield [core_hop(quarter)]
     return jnp.concatenate([quarter, far])
@@ -816,7 +819,7 @@
     expanded = low(jnp.dot(latent_low, expand_weight, preferred_element_type=jnp.float32))
     query_low, expanded = flow.close((query_low, expanded))
 
-    cot_tasks.append(flow.launch(plane_gather(cot_piece, 4)))
+    cot_tasks.append(flow.launch(plane_gather(cot_piece, 4, 2)))
     cot_piece = cot_pass.result
     cot_pass = flow.launch(passing(cot_piece))
     expanded = expanded.reshape(tok_count, heads_here, QK_NOPE + V_HEAD)
@@ -840,7 +843,7 @@
     attn_part = jnp.dot(heads_low, output_weight, preferred_element_type=jnp.float32)
     attn_part = flow.close(attn_part)
 
-    cot_tasks.append(flow.launch(plane_gather(cot_piece, 6)))
+    cot_tasks.append(flow.launch(plane_gather(cot_piece, 6, 2)))
     cot_piece = cot_pass.result
     resid_own = own_rows(tokens).astype(jnp.float32) + tensor_scatter(attn_part, tensor_index)
     normed_own, inverse_own = norm_forward(resid_own, gain_ffn_f)
@@ -928,10 +931,10 @@
         )
 
         after = (planes - 1 - step) * 3
-        places = {0: (after + 6, 0), 1: (after, 1), 2: (after + 3, 0), 3: (after + 5, 0)}[step]
+        places = {0: (after + 6, 0), 1: (after, 1), 2: (after + 1, 1), 3: (after + 5, 0)}[step]
         out_tasks.append(flow.launch(plane_scatter(out_part, False, *places)))
         if step == 0:
-            cot_tasks.append(flow.launch(plane_gather(cot_piece, 3)))
+            cot_tasks.append(flow.launch(plane_gather(cot_piece, 3, 2)))
         in_part = low(
             jnp.dot(gate_grad, gate_weight, preferred_element_type=jnp.float32)
             + jnp.dot(up_grad, up_weight, preferred_element_type=jnp.float32)
@@ -969,9 +972,8 @@
     in_moving = flow.launch(
         passing(low(in_tasks[3].result + in_moving.result.astype(jnp.float32)))
     )
+    kept_parts = flow.close(kept_parts)
     out_moving = flow.launch(passing(low(out_tasks[1].result)))
-
-    kept_parts = flow.close(kept_parts)
     ffn_sum = in_tasks[0].result + in_moving.result.astype(jnp.float32)
     probs_own, gates_own, picked_own = gating(normed_own_low, standing_own)
     gate_sums = jnp.where(standing_own > 1.5, gate_sums, 0.0)

time: 1020 us -> 1040 us (1.020)
    unnamed x404 -> x418, local copies, waits for them, and re-layouts: 37.3 us -> 34.9 us
  transfers between devices with their start and end apart: 132 -> 132, of which waited for: 53 -> 49; matrix products, arithmetic and copies ran while one was open for 50% -> 51% of each run, Pallas kernels for 0% -> 0%
where the time goes in v5:
time: 1040 us; the launch traced here: 1030 us
  waiting for transfers between devices  291 us (28%)
  matrix products  275 us (26%)
  other arithmetic  171 us (16%)
  local copies, waits for them, and re-layouts  160 us (15%)
  starting transfers between devices  129 us (12%)
    ppermute x92, waiting for transfers between devices, hop(): lax.ppermute(values, axis, [(i, i ^ bit) for i in range(lax.axis_size(axi...  179 us
    ppermute x36, waiting for transfers between devices, z_hop(): lax.ppermute(values, 'dp', [(i, (i + 2) % count) for i in range(count)])  112 us
    ppermute x92, starting transfers between devices, hop(): lax.ppermute(values, axis, [(i, i ^ bit) for i in range(lax.axis_size(axi...  75.8 us
    convert_element_type x30, other arithmetic, low(): return values.astype(jnp.bfloat16)  48.7 us
    ppermute x36, starting transfers between devices, z_hop(): lax.ppermute(values, 'dp', [(i, (i + 2) % count) for i in range(count)])  35.9 us
    unnamed x418, local copies, waits for them, and re-layouts  34.9 us
    dynamic_update_slice x32, local copies, waits for them, and re-layouts, laid_out(): whole = lax.dynamic_update_slice_in_dim(whole, piece, home * extent, axis)  31.6 us
    dot_general x4, matrix products, body_dense(): jnp.einsum('td,fd->tf', cots, down_weight, preferred_element_type=jnp.flo...  30.6 us
  transfers between devices with their start and end apart: 132, of which 49 were waited for; matrix products, arithmetic and copies ran while one was open for 51% of the time, Pallas kernels for 0%

profile of v5, /device:TPU:0, one launch (start us, length us, event | category | flops | bytes accessed | tf_op | source)
XLA Modules:
  0.0 1032.2 jit_solution(9030026649109055971)
XLA Ops:
  16.8 6.2 collective-permute-done.3
  24.7 6.2 collective-permute-done.5
  71.4 8.3 collective-permute-done.16
  134.1 15.2 %collective-permute-done.28 = bf16[64,1024]{1,0:T(8,128)(2,1)S(1)} collective-permute-done((bf16[64,1024]{1,0:T(8,128)(2,1)S(1)}, bf16[64,1024]{1,0:T(8,128)(2,1)S(1)}, u32[]{:S(2)}, u32[]{:S(2)}) %collective-permute-start.28) | collective-permute-done | bytes 131104 | tf_op jit(solution)/shard_map/ppermute | solution.py:444
  183.7 11.4 %collective-permute-done.35 = bf16[128,2048]{1,0:T(8,128)(2,1)} collective-permute-done((bf16[128,2048]{1,0:T(8,128)(2,1)}, bf16[128,2048]{1,0:T(8,128)(2,1)}, u32[]{:S(2)}, u32[]{:S(2)}) %collective-permute-start.35) | collective-permute-done | bytes 524320 | tf_op jit(solution)/shard_map/ppermute | solution.py:461
  213.8 11.3 %collective-permute-done.37 = bf16[128,2048]{1,0:T(8,128)(2,1)S(1)} collective-permute-done((bf16[128,2048]{1,0:T(8,128)(2,1)S(1)}, bf16[128,2048]{1,0:T(8,128)(2,1)S(1)}, u32[]{:S(2)}, u32[]{:S(2)}) %collective-permute-start.37) | collective-permute-done | bytes 524320 | tf_op jit(solution)/shard_map/ppermute | solution.py:444
  248.8 7.7 collective-permute-done.44
  276.8 8.3 multiply_convert_fusion.11
  296.2 21.4 %collective-permute-done.48 = bf16[256,2048]{1,0:T(8,128)(2,1)S(1)} collective-permute-done((bf16[256,2048]{1,0:T(8,128)(2,1)}, bf16[256,2048]{1,0:T(8,128)(2,1)S(1)}, u32[]{:S(2)}, u32[]{:S(2)}) %collective-permute-start.48) | collective-permute-done | bytes 1048608 | tf_op jit(solution)/shard_map/ppermute | solution.py:444
  325.2 6.9 fusion.237
  332.1 7.5 add_convert_fusion.3
  361.4 5.8 fusion.240
  383.1 8.0 multiply_convert_fusion.8
  396.0 12.8 %collective-permute-done.59 = bf16[2,128,2048]{2,1,0:T(8,128)(2,1)S(1)} collective-permute-done((bf16[2,128,2048]{2,1,0:T(8,128)(2,1)}, bf16[2,128,2048]{2,1,0:T(8,128)(2,1)S(1)}, u32[]{:S(2)}, u32[]{:S(2)}) %collective-permute-start.59) | collective-permute-done | bytes 1048608 | tf_op jit(solution)/shard_map/ppermute | solution.py:444
  418.8 7.3 fusion.241
  426.0 7.5 add_convert_fusion.2
  453.3 5.7 fusion.244
  471.0 8.0 multiply_convert_fusion.5
  483.9 6.3 collective-permute-done.68
  503.7 7.1 fusion.247
  510.7 7.5 add_convert_fusion.1
  533.8 5.9 fusion.248
  549.8 15.5 %select_reduce_fusion.1 = (f32[1024]{0:T(1024)S(1)}, f32[1024]{0:T(1024)S(1)}, f32[1024]{0:T(1024)S(1)}, f32[1024]{0:T(1024)S(1)}, f32[1024]{0:T(1024)S(1)}, /*i...) fusion(pred[792]{0:T(1024)(128)(4,1)S(1)} %copy-done.181, ...), kind=kOutput, calls=%fused_computation.43 | convolution fusion | flops 3351887872 | bytes 39922784 | tf_op jit(solution)/shard_map/td,fd->tf/dot_general | solution.py:916
  569.8 6.1 convolution_convert_fusion
  583.2 7.1 fusion.251
  590.2 7.1 add_convert_fusion
  606.7 9.4 add_add_fusion.2
  616.1 14.7 %collective-permute-done.80 = bf16[2,128,2048]{2,1,0:T(8,128)(2,1)S(1)} collective-permute-done((bf16[2,128,2048]{2,1,0:T(8,128)(2,1)S(1)}, bf16[2,128,2048]{2,1,0:T(8,128)(2,1)S(1)}, u32[]{:S(2)}, u32[]{:S(2)}) %collective-permute-start.80) | collective-permute-done | bytes 1048608 | tf_op jit(solution)/shard_map/ppermute | solution.py:444
  644.3 5.9 fusion.253
  659.4 7.9 add_add_fusion.1
  674.4 7.6 collective-permute-done.86
  687.4 9.0 collective-permute-done.88
  705.0 6.9 collective-permute-done.89
  717.6 6.0 slice.575
  733.4 11.7 %collective-permute-done.91 = bf16[128,2048]{1,0:T(8,128)(2,1)S(1)} collective-permute-done((bf16[128,2048]{1,0:T(8,128)(2,1)S(1)}, bf16[128,2048]{1,0:T(8,128)(2,1)S(1)}, u32[]{:S(2)}, u32[]{:S(2)}) %collective-permute-start.91) | collective-permute-done | bytes 524320 | tf_op jit(solution)/shard_map/ppermute | solution.py:461
  762.8 5.8 fusion.256
  768.7 5.6 convolution_add_fusion
  780.1 7.5 collective-permute-done.93
  808.2 7.8 fusion.257
  816.0 12.2 %add_add_fusion = f32[792,2048]{1,0:T(8,128)} fusion(f32[792,2048]{1,0:T(8,128)} %convolution_add_fusion, f32[792,2048]{1,0:T(8,128)} %fusion.257, f32[792,2048]{1,0:T(8,128)} %fusion.258), kind=kLoop, calls=%fused_computation.10 | loop fusion | flops 3244032 | bytes 25952256 | tf_op jit(solution)/shard_map/add | solution.py:1021
  828.2 9.5 multiply_convert_fusion
  850.0 6.0 slice.577
  910.9 6.4 multiply_reduce_fusion
  933.9 6.5 collective-permute-done.124
  943.0 12.0 %collective-permute-done.122 = bf16[2,64,1024]{2,1,0:T(8,128)(2,1)S(1)} collective-permute-done((bf16[2,64,1024]{2,1,0:T(8,128)(2,1)S(1)}, bf16[2,64,1024]{2,1,0:T(8,128)(2,1)S(1)}, u32[]{:S(2)}, u32[]{:S(2)}) %collective-permute-start.122) | collective-permute-done | bytes 262176 | tf_op jit(solution)/shard_map/ppermute | solution.py:444
  958.3 12.2 %collective-permute-done.119 = bf16[256,768]{1,0:T(8,128)(2,1)S(1)} collective-permute-done((bf16[256,768]{1,0:T(8,128)(2,1)S(1)}, bf16[256,768]{1,0:T(8,128)(2,1)S(1)}, u32[]{:S(2)}, u32[]{:S(2)}) %collective-permute-start.119) | collective-permute-done | bytes 393248 | tf_op jit(solution)/shard_map/ppermute | solution.py:461
  973.7 8.0 collective-permute-done.120
  1016.2 6.3 collective-permute-done.115
  (1009 shorter events, 614.0 us)
Async XLA Ops:
  56.9 35.6 %collective-permute-start.14 = (bf16[2,160,2048]{2,1,0:T(8,128)(2,1)}, bf16[2,160,2048]{2,1,0:T(8,128)(2,1)}, u32[]{:S(2)}, u32[]{:S(2)}) collective-permute-start(bf16[2,160,2048]{2,1,0:T(8,128)(2,1)} %pad_maximum_fusion.16), channel_id=1, source_target_pairs={{0,1},{1,0},{2,3},{3,2},{4,5},{5,4},{6,7},{7,6},{8,9},{9,8},{10,11... | collective-permute-start | bytes 3932168 | tf_op jit(solution)/shard_map/ppermute | solution.py:444
  65.1 27.3 %collective-permute-start.15 = (bf16[256,768]{1,0:T(8,128)(2,1)}, bf16[256,768]{1,0:T(8,128)(2,1)S(1)}, u32[]{:S(2)}, u32[]{:S(2)}) collective-permute-start(bf16[256,768]{1,0:T(8,128)(2,1)} %collective-permute-done.11), channel_id=1, source_target_pairs={{0,4},{4,0},{8,12},{12,8},{16,20},{20,16},{24,28},{28,24},{1,5},{5... | collective-permute-start | bytes 1179656 | tf_op jit(solution)/shard_map/ppermute | solution.py:444
  66.6 25.9 %collective-permute-start.18 = (bf16[256,768]{1,0:T(8,128)(2,1)}, bf16[256,768]{1,0:T(8,128)(2,1)}, u32[]{:S(2)}, u32[]{:S(2)}) collective-permute-start(bf16[256,768]{1,0:T(8,128)(2,1)} %collective-permute-done.11), channel_id=1, source_target_pairs={{0,8},{4,12},{8,16},{12,20},{16,24},{20,28},{24,0},{28,4},{1,9},{5... | collective-permute-start | bytes 1179656 | tf_op jit(solution)/shard_map/ppermute | solution.py:461
  92.5 29.8 %collective-permute-start.21 = (bf16[256,768]{1,0:T(8,128)(2,1)}, bf16[256,768]{1,0:T(8,128)(2,1)}, u32[]{:S(2)}, u32[]{:S(2)}) collective-permute-start(bf16[256,768]{1,0:T(8,128)(2,1)} %collective-permute-done.18), channel_id=1, source_target_pairs={{0,4},{4,0},{8,12},{12,8},{16,20},{20,16},{24,28},{28,24},{1,5},{5... | collective-permute-start | bytes 1179656 | tf_op jit(solution)/shard_map/ppermute | solution.py:444
  93.1 29.2 %collective-permute-start.24 = (bf16[256,768]{1,0:T(8,128)(2,1)}, bf16[256,768]{1,0:T(8,128)(2,1)}, u32[]{:S(2)}, u32[]{:S(2)}) collective-permute-start(bf16[256,768]{1,0:T(8,128)(2,1)} %collective-permute-done.18), channel_id=1, source_target_pairs={{0,8},{4,12},{8,16},{12,20},{16,24},{20,28},{24,0},{28,4},{1,9},{5... | collective-permute-start | bytes 1179656 | tf_op jit(solution)/shard_map/ppermute | solution.py:461
  93.1 27.7 %collective-permute-start.23 = (bf16[512,256]{1,0:T(8,128)(2,1)}, bf16[512,256]{1,0:T(8,128)(2,1)}, u32[]{:S(2)}, u32[]{:S(2)}) collective-permute-start(bf16[512,256]{1,0:T(8,128)(2,1)} %collective-permute-done.20), channel_id=1, source_target_pairs={{0,4},{4,0},{8,12},{12,8},{16,20},{20,16},{24,28},{28,24},{1,5},{5... | collective-permute-start | bytes 786440 | tf_op jit(solution)/shard_map/ppermute | solution.py:444
  94.6 27.7 %collective-permute-start.26 = (bf16[512,256]{1,0:T(8,128)(2,1)}, bf16[512,256]{1,0:T(8,128)(2,1)}, u32[]{:S(2)}, u32[]{:S(2)}) collective-permute-start(bf16[512,256]{1,0:T(8,128)(2,1)} %collective-permute-done.20), channel_id=1, source_target_pairs={{0,8},{4,12},{8,16},{12,20},{16,24},{20,28},{24,0},{28,4},{1,9},{5... | collective-permute-start | bytes 786440 | tf_op jit(solution)/shard_map/ppermute | solution.py:461
  120.8 48.6 %collective-permute-start.31 = (bf16[128,2048]{1,0:T(8,128)(2,1)}, bf16[128,2048]{1,0:T(8,128)(2,1)S(1)}, u32[]{:S(2)}, u32[]{:S(2)}) collective-permute-start(bf16[128,2048]{1,0:T(8,128)(2,1)} %constant_dynamic-slice_fusion.5), channel_id=1, source_target_pairs={{0,4},{4,0},{8,12},{12,8},{16,20},{20,16},{24,28},{28,24},{1,5},{5... | collective-permute-start | bytes 1572872 | tf_op jit(solution)/shard_map/ppermute | solution.py:444
  122.3 27.1 %collective-permute-start.27 = (bf16[256,768]{1,0:T(8,128)(2,1)}, bf16[256,768]{1,0:T(8,128)(2,1)S(1)}, u32[]{:S(2)}, u32[]{:S(2)}) collective-permute-start(bf16[256,768]{1,0:T(8,128)(2,1)} %collective-permute-done.24), channel_id=1, source_target_pairs={{0,4},{4,0},{8,12},{12,8},{16,20},{20,16},{24,28},{28,24},{1,5},{5... | collective-permute-start | bytes 1179656 | tf_op jit(solution)/shard_map/ppermute | solution.py:444
  122.9 26.4 %collective-permute-start.29 = (bf16[512,256]{1,0:T(8,128)(2,1)}, bf16[512,256]{1,0:T(8,128)(2,1)S(1)}, u32[]{:S(2)}, u32[]{:S(2)}) collective-permute-start(bf16[512,256]{1,0:T(8,128)(2,1)} %collective-permute-done.26), channel_id=1, source_target_pairs={{0,4},{4,0},{8,12},{12,8},{16,20},{20,16},{24,28},{28,24},{1,5},{5... | collective-permute-start | bytes 786440 | tf_op jit(solution)/shard_map/ppermute | solution.py:444
  124.4 25.0 %collective-permute-start.28 = (bf16[64,1024]{1,0:T(8,128)(2,1)S(1)}, bf16[64,1024]{1,0:T(8,128)(2,1)S(1)}, u32[]{:S(2)}, u32[]{:S(2)}) collective-permute-start(bf16[64,1024]{1,0:T(8,128)(2,1)S(1)} %collective-permute-done.25), channel_id=1, source_target_pairs={{0,4},{4,0},{8,12},{12,8},{16,20},{20,16},{24,28},{28,24},{1,5},{5... | collective-permute-start | bytes 393224 | tf_op jit(solution)/shard_map/ppermute | solution.py:444
  149.4 34.2 %collective-permute-start.34 = (bf16[128,2048]{1,0:T(8,128)(2,1)}, bf16[128,2048]{1,0:T(8,128)(2,1)}, u32[]{:S(2)}, u32[]{:S(2)}) collective-permute-start(bf16[128,2048]{1,0:T(8,128)(2,1)} %collective-permute-done.30), channel_id=1, source_target_pairs={{0,4},{4,0},{8,12},{12,8},{16,20},{20,16},{24,28},{28,24},{1,5},{5... | collective-permute-start | bytes 1572872 | tf_op jit(solution)/shard_map/ppermute | solution.py:444
  154.4 52.2 %all-to-all-start = ((bf16[3,704,256]{2,0,1:T(4,128)(2,1)}), bf16[3,704,256]{2,0,1:T(4,128)(2,1)}, u32[]{:S(2)}, u32[]{:S(2)}) async-start(bf16[3,704,256]{2,0,1:T(4,128)(2,1)} %copy.247), calls=%async_computation | async-start | bytes 2883584 | tf_op jit(solution)/shard_map/all_to_all | solution.py:855
  199.1 27.5 %collective-permute-start.39 = (bf16[128,2048]{1,0:T(8,128)(2,1)}, bf16[128,2048]{1,0:T(8,128)(2,1)}, u32[]{:S(2)}, u32[]{:S(2)}) collective-permute-start(bf16[128,2048]{1,0:T(8,128)(2,1)} %collective-permute-done.32), channel_id=1, source_target_pairs={{0,4},{4,0},{8,12},{12,8},{16,20},{20,16},{24,28},{28,24},{1,5},{5... | collective-permute-start | bytes 1572872 | tf_op jit(solution)/shard_map/ppermute | solution.py:444
  204.3 136.6 %collective-permute-start.53 = (bf16[128,2048]{1,0:T(8,128)(2,1)}, bf16[128,2048]{1,0:T(8,128)(2,1)}, u32[]{:S(2)}, u32[]{:S(2)}) collective-permute-start(bf16[128,2048]{1,0:T(8,128)(2,1)} %collective-permute-done.35), channel_id=1, source_target_pairs={{0,4},{4,0},{8,12},{12,8},{16,20},{20,16},{24,28},{28,24},{1,5},{5... | collective-permute-start | bytes 1572872 | tf_op jit(solution)/shard_map/ppermute | solution.py:444
  268.3 104.4 %collective-permute-start.54 = (bf16[128,2048]{1,0:T(8,128)(2,1)S(1)}, bf16[128,2048]{1,0:T(8,128)(2,1)S(1)}, u32[]{:S(2)}, u32[]{:S(2)}) collective-permute-start(bf16[128,2048]{1,0:T(8,128)(2,1)S(1)} %collective-permute-done.47), channel_id=1, source_target_pairs={{0,4},{4,0},{8,12},{12,8},{16,20},{20,16},{24,28},{28,24},{1,5},{5... | collective-permute-start | bytes 1572872 | tf_op jit(solution)/shard_map/ppermute | solution.py:444
  270.1 26.1 %collective-permute-start.49 = (bf16[256,2048]{1,0:T(8,128)(2,1)S(1)}, bf16[256,2048]{1,0:T(8,128)(2,1)S(1)}, u32[]{:S(2)}, u32[]{:S(2)}) collective-permute-start(bf16[256,2048]{1,0:T(8,128)(2,1)S(1)} %pad_maximum_fusion.20), channel_id=1, source_target_pairs={{0,2},{1,3},{2,0},{3,1},{4,6},{5,7},{6,4},{7,5},{8,10},{9,11},{10,... | collective-permute-start | bytes 3145736 | tf_op jit(solution)/shard_map/ppermute | solution.py:444
  275.1 42.5 %collective-permute-start.48 = (bf16[256,2048]{1,0:T(8,128)(2,1)}, bf16[256,2048]{1,0:T(8,128)(2,1)S(1)}, u32[]{:S(2)}, u32[]{:S(2)}) collective-permute-start(bf16[256,2048]{1,0:T(8,128)(2,1)} %pad_maximum_fusion.19), channel_id=1, source_target_pairs={{0,2},{1,3},{2,0},{3,1},{4,6},{5,7},{6,4},{7,5},{8,10},{9,11},{10,... | collective-permute-start | bytes 3145736 | tf_op jit(solution)/shard_map/ppermute | solution.py:444
  319.1 23.9 %collective-permute-start.51 = (bf16[512,2048]{1,0:T(8,128)(2,1)}, bf16[512,2048]{1,0:T(8,128)(2,1)}, u32[]{:S(2)}, u32[]{:S(2)}) collective-permute-start(bf16[512,2048]{1,0:T(8,128)(2,1)} %pad_maximum_fusion.8), channel_id=1, source_target_pairs={{0,1},{1,0},{2,3},{3,2},{4,5},{5,4},{6,7},{7,6},{8,9},{9,8},{10,11... | collective-permute-start | bytes 6291464 | tf_op jit(solution)/shard_map/ppermute | solution.py:444
  340.9 31.9 %collective-permute-start.55 = (bf16[128,2048]{1,0:T(8,128)(2,1)S(1)}, bf16[128,2048]{1,0:T(8,128)(2,1)S(1)}, u32[]{:S(2)}, u32[]{:S(2)}) collective-permute-start(bf16[128,2048]{1,0:T(8,128)(2,1)S(1)} %collective-permute-done.47), channel_id=1, source_target_pairs={{0,8},{4,12},{8,16},{12,20},{16,24},{20,28},{24,0},{28,4},{1,9},{5... | collective-permute-start | bytes 1572872 | tf_op jit(solution)/shard_map/ppermute | solution.py:461
  355.7 40.3 %collective-permute-start.57 = (bf16[256,2048]{1,0:T(8,128)(2,1)}, bf16[256,2048]{1,0:T(8,128)(2,1)S(1)}, u32[]{:S(2)}, u32[]{:S(2)}) collective-permute-start(bf16[256,2048]{1,0:T(8,128)(2,1)} %pad_maximum_fusion.21), channel_id=1, source_target_pairs={{0,2},{1,3},{2,0},{3,1},{4,6},{5,7},{6,4},{7,5},{8,10},{9,11},{10,... | collective-permute-start | bytes 3145736 | tf_op jit(solution)/shard_map/ppermute | solution.py:444
  372.7 91.9 %collective-permute-start.64 = (bf16[128,2048]{1,0:T(8,128)(2,1)S(1)}, bf16[128,2048]{1,0:T(8,128)(2,1)S(1)}, u32[]{:S(2)}, u32[]{:S(2)}) collective-permute-start(bf16[128,2048]{1,0:T(8,128)(2,1)S(1)} %collective-permute-done.55), channel_id=1, source_target_pairs={{0,4},{4,0},{8,12},{12,8},{16,20},{20,16},{24,28},{28,24},{1,5},{5... | collective-permute-start | bytes 1572872 | tf_op jit(solution)/shard_map/ppermute | solution.py:444
  377.5 31.3 %collective-permute-start.59 = (bf16[2,128,2048]{2,1,0:T(8,128)(2,1)}, bf16[2,128,2048]{2,1,0:T(8,128)(2,1)S(1)}, u32[]{:S(2)}, u32[]{:S(2)}) collective-permute-start(bf16[2,128,2048]{2,1,0:T(8,128)(2,1)} %fusion.34), channel_id=1, source_target_pairs={{0,4},{4,0},{8,12},{12,8},{16,20},{20,16},{24,28},{28,24},{1,5},{5... | collective-permute-start | bytes 3145736 | tf_op jit(solution)/shard_map/ppermute | solution.py:444
  379.4 29.4 %collective-permute-start.58 = (bf16[256,2048]{1,0:T(8,128)(2,1)}, bf16[256,2048]{1,0:T(8,128)(2,1)S(1)}, u32[]{:S(2)}, u32[]{:S(2)}) collective-permute-start(bf16[256,2048]{1,0:T(8,128)(2,1)} %pad_maximum_fusion.22), channel_id=1, source_target_pairs={{0,2},{1,3},{2,0},{3,1},{4,6},{5,7},{6,4},{7,5},{8,10},{9,11},{10,... | collective-permute-start | bytes 3145736 | tf_op jit(solution)/shard_map/ppermute | solution.py:444
  409.3 25.5 %collective-permute-start.62 = (bf16[128,2048]{1,0:T(8,128)(2,1)S(1)}, bf16[128,2048]{1,0:T(8,128)(2,1)S(1)}, u32[]{:S(2)}, u32[]{:S(2)}) collective-permute-start(bf16[128,2048]{1,0:T(8,128)(2,1)S(1)} %fusion.81), channel_id=1, source_target_pairs={{0,2},{1,3},{2,0},{3,1},{4,6},{5,7},{6,4},{7,5},{8,10},{9,11},{10,... | collective-permute-start | bytes 1572872 | tf_op jit(solution)/shard_map/ppermute | solution.py:444
  447.7 36.3 %collective-permute-start.66 = (bf16[256,2048]{1,0:T(8,128)(2,1)}, bf16[256,2048]{1,0:T(8,128)(2,1)S(1)}, u32[]{:S(2)}, u32[]{:S(2)}) collective-permute-start(bf16[256,2048]{1,0:T(8,128)(2,1)} %pad_maximum_fusion.23), channel_id=1, source_target_pairs={{0,2},{1,3},{2,0},{3,1},{4,6},{5,7},{6,4},{7,5},{8,10},{9,11},{10,... | collective-permute-start | bytes 3145736 | tf_op jit(solution)/shard_map/ppermute | solution.py:444
  465.6 24.7 %collective-permute-start.68 = (bf16[2,128,2048]{2,1,0:T(8,128)(2,1)S(1)}, bf16[2,128,2048]{2,1,0:T(8,128)(2,1)S(1)}, u32[]{:S(2)}, u32[]{:S(2)}) collective-permute-start(bf16[2,128,2048]{2,1,0:T(8,128)(2,1)S(1)} %fusion.35), channel_id=1, source_target_pairs={{0,4},{4,0},{8,12},{12,8},{16,20},{20,16},{24,28},{28,24},{1,5},{5... | collective-permute-start | bytes 3145736 | tf_op jit(solution)/shard_map/ppermute | solution.py:444
  467.3 28.0 %collective-permute-start.67 = (bf16[256,2048]{1,0:T(8,128)(2,1)}, bf16[256,2048]{1,0:T(8,128)(2,1)S(1)}, u32[]{:S(2)}, u32[]{:S(2)}) collective-permute-start(bf16[256,2048]{1,0:T(8,128)(2,1)} %pad_maximum_fusion.24), channel_id=1, source_target_pairs={{0,2},{1,3},{2,0},{3,1},{4,6},{5,7},{6,4},{7,5},{8,10},{9,11},{10,... | collective-permute-start | bytes 3145736 | tf_op jit(solution)/shard_map/ppermute | solution.py:444
  495.6 23.8 %collective-permute-start.71 = (bf16[128,2048]{1,0:T(8,128)(2,1)S(1)}, bf16[128,2048]{1,0:T(8,128)(2,1)S(1)}, u32[]{:S(2)}, u32[]{:S(2)}) collective-permute-start(bf16[128,2048]{1,0:T(8,128)(2,1)S(1)} %fusion.82), channel_id=1, source_target_pairs={{0,2},{1,3},{2,0},{3,1},{4,6},{5,7},{6,4},{7,5},{8,10},{9,11},{10,... | collective-permute-start | bytes 1572872 | tf_op jit(solution)/shard_map/ppermute | solution.py:444
  545.5 31.7 %collective-permute-start.75 = (bf16[2,128,2048]{2,1,0:T(8,128)(2,1)}, bf16[2,128,2048]{2,1,0:T(8,128)(2,1)S(1)}, u32[]{:S(2)}, u32[]{:S(2)}) collective-permute-start(bf16[2,128,2048]{2,1,0:T(8,128)(2,1)} %fusion.36), channel_id=1, source_target_pairs={{0,4},{4,0},{8,12},{12,8},{16,20},{20,16},{24,28},{28,24},{1,5},{5... | collective-permute-start | bytes 3145736 | tf_op jit(solution)/shard_map/ppermute | solution.py:444
  599.2 31.7 %collective-permute-start.81 = (bf16[2,2,128,2048]{3,2,0,1:T(8,128)(2,1)S(1)}, bf16[2,2,128,2048]{3,2,0,1:T(8,128)(2,1)S(1)}, u32[]{:S(2)}, u32[]{:S(2)}) collective-permute-start(bf16[2,2,128,2048]{3,2,0,1:T(8,128)(2,1)S(1)} %copy.269), channel_id=1, source_target_pairs={{0,1},{1,0},{2,3},{3,2},{4,5},{5,4},{6,7},{7,6},{8,9},{9,8},{10,11... | collective-permute-start | bytes 6291464 | tf_op jit(solution)/shard_map/ppermute | solution.py:444
  605.6 25.2 %collective-permute-start.80 = (bf16[2,128,2048]{2,1,0:T(8,128)(2,1)S(1)}, bf16[2,128,2048]{2,1,0:T(8,128)(2,1)S(1)}, u32[]{:S(2)}, u32[]{:S(2)}) collective-permute-start(bf16[2,128,2048]{2,1,0:T(8,128)(2,1)S(1)} %fusion.37), channel_id=1, source_target_pairs={{0,2},{1,3},{2,0},{3,1},{4,6},{5,7},{6,4},{7,5},{8,10},{9,11},{10,... | collective-permute-start | bytes 3145736 | tf_op jit(solution)/shard_map/ppermute | solution.py:444
  632.9 34.4 %collective-permute-start.84 = (bf16[2,128,2048]{2,1,0:T(8,128)(2,1)}, bf16[2,128,2048]{2,1,0:T(8,128)(2,1)}, u32[]{:S(2)}, u32[]{:S(2)}) collective-permute-start(bf16[2,128,2048]{2,1,0:T(8,128)(2,1)} %fusion.39), channel_id=1, source_target_pairs={{0,4},{4,0},{8,12},{12,8},{16,20},{20,16},{24,28},{28,24},{1,5},{5... | collective-permute-start | bytes 3145736 | tf_op jit(solution)/shard_map/ppermute | solution.py:444
  638.5 28.8 %collective-permute-start.83 = (bf16[2,128,2048]{2,1,0:T(8,128)(2,1)S(1)}, bf16[2,128,2048]{2,1,0:T(8,128)(2,1)S(1)}, u32[]{:S(2)}, u32[]{:S(2)}) collective-permute-start(bf16[2,128,2048]{2,1,0:T(8,128)(2,1)S(1)} %fusion.38), channel_id=1, source_target_pairs={{0,2},{1,3},{2,0},{3,1},{4,6},{5,7},{6,4},{7,5},{8,10},{9,11},{10,... | collective-permute-start | bytes 3145736 | tf_op jit(solution)/shard_map/ppermute | solution.py:444
  639.7 27.6 %all-to-all-start.1 = ((f32[8,2,128]{2,1,0:T(2,128)}), f32[8,2,128]{2,1,0:T(2,128)S(1)}, u32[]{:S(2)}, u32[]{:S(2)}) async-start(f32[8,2,128]{2,1,0:T(2,128)} %gather_fusion), calls=%async_computation.1 | async-start | bytes 16384 | tf_op jit(solution)/shard_map/all_to_all | solution.py:964
  751.1 86.6 %all-to-all-start.2 = ((bf16[2,88,2048]{1,0,2:T(2,128)(2,1)}), bf16[2,88,2048]{1,0,2:T(2,128)(2,1)}, u32[]{:S(2)}, u32[]{:S(2)}) async-start(bf16[2,88,2048]{1,0,2:T(2,128)(2,1)} %copy.280), calls=%async_computation.2 | async-start | bytes 2097152 | tf_op jit(solution)/shard_map/all_to_all | solution.py:1007
  757.2 30.4 %collective-permute-start.93 = (bf16[128,2048]{1,0:T(8,128)(2,1)S(1)}, bf16[128,2048]{1,0:T(8,128)(2,1)S(1)}, u32[]{:S(2)}, u32[]{:S(2)}) collective-permute-start(bf16[128,2048]{1,0:T(8,128)(2,1)S(1)} %fusion.51), channel_id=1, source_target_pairs={{0,8},{4,12},{8,16},{12,20},{16,24},{20,28},{24,0},{28,4},{1,9},{5... | collective-permute-start | bytes 1572872 | tf_op jit(solution)/shard_map/ppermute | solution.py:461
  761.8 25.8 %collective-permute-start.92 = (bf16[2,128,2048]{2,1,0:T(8,128)(2,1)S(1)}, bf16[2,128,2048]{2,1,0:T(8,128)(2,1)S(1)}, u32[]{:S(2)}, u32[]{:S(2)}) collective-permute-start(bf16[2,128,2048]{2,1,0:T(8,128)(2,1)S(1)} %fusion.40), channel_id=1, source_target_pairs={{0,2},{1,3},{2,0},{3,1},{4,6},{5,7},{6,4},{7,5},{8,10},{9,11},{10,... | collective-permute-start | bytes 3145736 | tf_op jit(solution)/shard_map/ppermute | solution.py:444
  788.6 61.4 %collective-permute-start.97 = (bf16[2,512,256]{2,1,0:T(8,128)(2,1)}, bf16[2,512,256]{2,1,0:T(8,128)(2,1)}, u32[]{:S(2)}, u32[]{:S(2)}) collective-permute-start(bf16[2,512,256]{2,1,0:T(8,128)(2,1)} %pad_maximum_fusion.47), channel_id=1, source_target_pairs={{0,4},{4,0},{8,12},{12,8},{16,20},{20,16},{24,28},{28,24},{1,5},{5... | collective-permute-start | bytes 1572872 | tf_op jit(solution)/shard_map/ppermute | solution.py:444
  790.9 59.0 %collective-permute-start.96 = (bf16[2,512,256]{2,1,0:T(8,128)(2,1)}, bf16[2,512,256]{2,1,0:T(8,128)(2,1)}, u32[]{:S(2)}, u32[]{:S(2)}) collective-permute-start(bf16[2,512,256]{2,1,0:T(8,128)(2,1)} %pad_maximum_fusion.46), channel_id=1, source_target_pairs={{0,4},{4,0},{8,12},{12,8},{16,20},{20,16},{24,28},{28,24},{1,5},{5... | collective-permute-start | bytes 1572872 | tf_op jit(solution)/shard_map/ppermute | solution.py:444
  792.7 57.3 %collective-permute-start.95 = (bf16[128,2048]{1,0:T(8,128)(2,1)}, bf16[128,2048]{1,0:T(8,128)(2,1)}, u32[]{:S(2)}, u32[]{:S(2)}) collective-permute-start(bf16[128,2048]{1,0:T(8,128)(2,1)} %fusion.87), channel_id=1, source_target_pairs={{0,4},{4,0},{8,12},{12,8},{16,20},{20,16},{24,28},{28,24},{1,5},{5... | collective-permute-start | bytes 1572872 | tf_op jit(solution)/shard_map/ppermute | solution.py:444
  797.8 52.2 %collective-permute-start.94 = (bf16[2,128,2048]{2,1,0:T(8,128)(2,1)}, bf16[2,128,2048]{2,1,0:T(8,128)(2,1)}, u32[]{:S(2)}, u32[]{:S(2)}) collective-permute-start(bf16[2,128,2048]{2,1,0:T(8,128)(2,1)} %fusion.41), channel_id=1, source_target_pairs={{0,2},{1,3},{2,0},{3,1},{4,6},{5,7},{6,4},{7,5},{8,10},{9,11},{10,... | collective-permute-start | bytes 3145736 | tf_op jit(solution)/shard_map/ppermute | solution.py:444
  873.2 25.8 %all-to-all-start.3 = ((bf16[88,8,256]{2,0,1:T(8,128)(2,1)}), bf16[88,8,256]{2,0,1:T(8,128)(2,1)S(1)}, u32[]{:S(2)}, u32[]{:S(2)}) async-start(bf16[88,8,256]{2,0,1:T(8,128)(2,1)} %bitcast.728), calls=%async_computation.3 | async-start | bytes 720896 | tf_op jit(solution)/shard_map/all_to_all | solution.py:1147
  919.6 51.2 %collective-permute-start.108 = (bf16[2,160,2048]{2,1,0:T(8,128)(2,1)S(1)}, bf16[2,160,2048]{2,1,0:T(8,128)(2,1)S(1)}, u32[]{:S(2)}, u32[]{:S(2)}) collective-permute-start(bf16[2,160,2048]{2,1,0:T(8,128)(2,1)S(1)} %dynamic-slice_bitcast_fusion), channel_id=1, source_target_pairs={{0,1},{1,0},{2,3},{3,2},{4,5},{5,4},{6,7},{7,6},{8,9},{9,8},{10,11... | collective-permute-start | bytes 3932168 | tf_op jit(solution)/shard_map/ppermute | solution.py:444
  927.1 29.2 %collective-permute-start.118 = (bf16[2,256,768]{2,1,0:T(8,128)(2,1)S(1)}, bf16[2,256,768]{2,1,0:T(8,128)(2,1)S(1)}, u32[]{:S(2)}, u32[]{:S(2)}) collective-permute-start(bf16[2,256,768]{2,1,0:T(8,128)(2,1)S(1)} %pad_maximum_fusion.39), channel_id=1, source_target_pairs={{0,4},{4,0},{8,12},{12,8},{16,20},{20,16},{24,28},{28,24},{1,5},{5... | collective-permute-start | bytes 2359304 | tf_op jit(solution)/shard_map/ppermute | solution.py:444
  928.8 28.1 %collective-permute-start.104 = (bf16[2,128,2048]{2,1,0:T(8,128)(2,1)S(1)}, bf16[2,128,2048]{2,1,0:T(8,128)(2,1)S(1)}, u32[]{:S(2)}, u32[]{:S(2)}) collective-permute-start(bf16[2,128,2048]{2,1,0:T(8,128)(2,1)S(1)} %fusion.33), channel_id=1, source_target_pairs={{0,1},{1,0},{2,3},{3,2},{4,5},{5,4},{6,7},{7,6},{8,9},{9,8},{10,11... | collective-permute-start | bytes 3145736 | tf_op jit(solution)/shard_map/ppermute | solution.py:444
  957.3 24.6 %collective-permute-start.105 = (bf16[128,2048]{1,0:T(8,128)(2,1)S(1)}, bf16[128,2048]{1,0:T(8,128)(2,1)S(1)}, u32[]{:S(2)}, u32[]{:S(2)}) collective-permute-start(bf16[128,2048]{1,0:T(8,128)(2,1)S(1)} %fusion.80), channel_id=1, source_target_pairs={{0,2},{1,3},{2,0},{3,1},{4,6},{5,7},{6,4},{7,5},{8,10},{9,11},{10,... | collective-permute-start | bytes 1572872 | tf_op jit(solution)/shard_map/ppermute | solution.py:444
  981.8 24.2 %collective-permute-start.121 = (bf16[256,768]{1,0:T(8,128)(2,1)S(1)}, bf16[256,768]{1,0:T(8,128)(2,1)S(1)}, u32[]{:S(2)}, u32[]{:S(2)}) collective-permute-start(bf16[256,768]{1,0:T(8,128)(2,1)S(1)} %fusion.72), channel_id=1, source_target_pairs={{0,8},{4,12},{8,16},{12,20},{16,24},{20,28},{24,0},{28,4},{1,9},{5... | collective-permute-start | bytes 1179656 | tf_op jit(solution)/shard_map/ppermute | solution.py:461
  (276 other events, 3289.4 us)

commit v6 on v5

--- a/solution.py
+++ b/solution.py
@@ -1004,9 +1004,7 @@
 
     def shared_sum(grads):
         grads = jnp.stack([low(grad[routed_here:]) for grad in grads])
-        return lax.all_to_all(grads, "dp", split_axis=2, concat_axis=1, tiled=True).astype(
-            jnp.float32
-        )
+        return lax.all_to_all(grads, "dp", split_axis=2, concat_axis=1, tiled=True)
 
     shared_grads = shared_sum(shared_parts)
     output_weight_grad = jnp.einsum(
@@ -1074,8 +1072,10 @@
     expand_weight_grad = jnp.einsum(
         "tr,te->re", latent_low, expand_grad, preferred_element_type=jnp.float32
     )
-    latent_grad, query_weight_grad, expand_weight_grad = flow.close(
-        (latent_grad, query_weight_grad, expand_weight_grad)
+    shared_down_sent = low(down_weight_grad[routed_here:])
+    weight_grads = [gate_weight_grad, up_weight_grad, down_weight_grad]
+    latent_grad, query_weight_grad, expand_weight_grad, shared_grads, weight_grads = flow.close(
+        (latent_grad, query_weight_grad, expand_weight_grad, shared_grads, weight_grads)
     )
     rope_grad = jnp.sum(key_grad[..., QK_NOPE:], axis=1)
     latent_pre_grad, gain_latent_grad = norm_backward(
@@ -1140,12 +1140,12 @@
         return grad[:routed_here].reshape(exp_here, group, width)
 
     routed_grads = (
-        routed_grad(gate_weight_grad).swapaxes(1, 2),
-        routed_grad(up_weight_grad).swapaxes(1, 2),
-        routed_grad(down_weight_grad),
+        routed_grad(weight_grads[0]).swapaxes(1, 2),
+        routed_grad(weight_grads[1]).swapaxes(1, 2),
+        routed_grad(weight_grads[2]),
     )
     shared_down_grad = lax.all_to_all(
-        low(down_weight_grad[routed_here:]), "dp", split_axis=1, concat_axis=0, tiled=True
+        shared_down_sent, "dp", split_axis=1, concat_axis=0, tiled=True
     ).astype(jnp.float32)
 
     return (
@@ -1159,8 +1159,8 @@
         output_share,
         gain_ffn_share,
         router_share,
-        shared_grads[0].T,
-        shared_grads[1].T,
+        shared_grads[0].astype(jnp.float32).T,
+        shared_grads[1].astype(jnp.float32).T,
         shared_down_grad,
         *routed_grads,
     )

time: 1040 us -> 999 us (0.961)
  waiting for transfers between devices: 291 us -> 251 us
    ppermute x36, waiting for transfers between devices: 112 us -> 89.6 us  [z_hop(): lax.ppermute(values, 'dp', [(i, (i + 2) % count) for i in range(count)])]
    ppermute x92, waiting for transfers between devices: 179 us -> 161 us  [hop(): lax.ppermute(values, axis, [(i, i ^ bit) for i in range(lax.axis_size(axi...]
    slice x4 -> x1, local copies, waits for them, and re-layouts: 11.6 us -> 1.15 us  [body_dense(): shared_down_sent = low(down_weight_grad[routed_here:])]
    unnamed x418 -> x430, local copies, waits for them, and re-layouts: 34.9 us -> 36.9 us
  transfers between devices with their start and end apart: 132 -> 132, of which waited for: 49 -> 45; matrix products, arithmetic and copies ran while one was open for 51% -> 53% of each run, Pallas kernels for 0% -> 0%
where the time goes in v6:
time: 999 us; the launch traced here: 988 us
  matrix products  273 us (27%)
  waiting for transfers between devices  251 us (25%)
  other arithmetic  172 us (17%)
  local copies, waits for them, and re-layouts  155 us (16%)
  starting transfers between devices  132 us (13%)
    ppermute x92, waiting for transfers between devices, hop(): lax.ppermute(values, axis, [(i, i ^ bit) for i in range(lax.axis_size(axi...  161 us
    ppermute x36, waiting for transfers between devices, z_hop(): lax.ppermute(values, 'dp', [(i, (i + 2) % count) for i in range(count)])  89.6 us
    ppermute x92, starting transfers between devices, hop(): lax.ppermute(values, axis, [(i, i ^ bit) for i in range(lax.axis_size(axi...  79 us
    convert_element_type x30, other arithmetic, low(): return values.astype(jnp.bfloat16)  51.7 us
    unnamed x430, local copies, waits for them, and re-layouts  36.9 us
    ppermute x36, starting transfers between devices, z_hop(): lax.ppermute(values, 'dp', [(i, (i + 2) % count) for i in range(count)])  32.8 us
    dynamic_update_slice x32, local copies, waits for them, and re-layouts, laid_out(): whole = lax.dynamic_update_slice_in_dim(whole, piece, home * extent, axis)  31.5 us
    dot_general x4, matrix products, body_dense(): jnp.einsum('td,fd->tf', cots, down_weight, preferred_element_type=jnp.flo...  30.7 us
  transfers between devices with their start and end apart: 132, of which 45 were waited for; matrix products, arithmetic and copies ran while one was open for 53% of the time, Pallas kernels for 0%

profile of v6, /device:TPU:0, one launch (start us, length us, event | category | flops | bytes accessed | tf_op | source)
XLA Modules:
  0.0 987.9 jit_solution(7978316911009708246)
XLA Ops:
  16.7 6.2 collective-permute-done.3
  24.7 6.2 collective-permute-done.5
  71.3 8.3 collective-permute-done.16
  133.9 15.3 %collective-permute-done.28 = bf16[64,1024]{1,0:T(8,128)(2,1)S(1)} collective-permute-done((bf16[64,1024]{1,0:T(8,128)(2,1)S(1)}, bf16[64,1024]{1,0:T(8,128)(2,1)S(1)}, u32[]{:S(2)}, u32[]{:S(2)}) %collective-permute-start.28) | collective-permute-done | bytes 131104 | tf_op jit(solution)/shard_map/ppermute | solution.py:444
  183.4 11.6 %collective-permute-done.35 = bf16[128,2048]{1,0:T(8,128)(2,1)} collective-permute-done((bf16[128,2048]{1,0:T(8,128)(2,1)}, bf16[128,2048]{1,0:T(8,128)(2,1)}, u32[]{:S(2)}, u32[]{:S(2)}) %collective-permute-start.35) | collective-permute-done | bytes 524320 | tf_op jit(solution)/shard_map/ppermute | solution.py:461
  213.7 11.3 %collective-permute-done.37 = bf16[128,2048]{1,0:T(8,128)(2,1)S(1)} collective-permute-done((bf16[128,2048]{1,0:T(8,128)(2,1)S(1)}, bf16[128,2048]{1,0:T(8,128)(2,1)S(1)}, u32[]{:S(2)}, u32[]{:S(2)}) %collective-permute-start.37) | collective-permute-done | bytes 524320 | tf_op jit(solution)/shard_map/ppermute | solution.py:444
  248.6 7.7 collective-permute-done.44
  276.7 8.3 multiply_convert_fusion.11
  296.1 21.4 %collective-permute-done.48 = bf16[256,2048]{1,0:T(8,128)(2,1)S(1)} collective-permute-done((bf16[256,2048]{1,0:T(8,128)(2,1)}, bf16[256,2048]{1,0:T(8,128)(2,1)S(1)}, u32[]{:S(2)}, u32[]{:S(2)}) %collective-permute-start.48) | collective-permute-done | bytes 1048608 | tf_op jit(solution)/shard_map/ppermute | solution.py:444
  325.1 6.9 fusion.236
  332.0 7.5 add_convert_fusion.3
  361.1 5.8 fusion.239
  367.0 5.5 fusion.241
  382.9 7.9 multiply_convert_fusion.8
  395.7 12.8 %collective-permute-done.59 = bf16[2,128,2048]{2,1,0:T(8,128)(2,1)S(1)} collective-permute-done((bf16[2,128,2048]{2,1,0:T(8,128)(2,1)}, bf16[2,128,2048]{2,1,0:T(8,128)(2,1)S(1)}, u32[]{:S(2)}, u32[]{:S(2)}) %collective-permute-start.59) | collective-permute-done | bytes 1048608 | tf_op jit(solution)/shard_map/ppermute | solution.py:444
  418.5 7.3 fusion.240
  425.8 7.5 add_convert_fusion.2
  453.0 5.7 fusion.243
  458.8 5.6 fusion.242
  470.8 8.0 multiply_convert_fusion.5
  483.7 6.3 collective-permute-done.68
  503.3 7.1 fusion.246
  510.4 7.5 add_convert_fusion.1
  533.6 5.9 fusion.247
  549.5 15.6 %select_reduce_fusion.1 = (f32[1024]{0:T(1024)S(1)}, f32[1024]{0:T(1024)S(1)}, f32[1024]{0:T(1024)S(1)}, f32[1024]{0:T(1024)S(1)}, f32[1024]{0:T(1024)S(1)}, /*i...) fusion(pred[792]{0:T(1024)(128)(4,1)S(1)} %copy-done.185, ...), kind=kOutput, calls=%fused_computation.43 | convolution fusion | flops 3351887872 | bytes 39922784 | tf_op jit(solution)/shard_map/td,fd->tf/dot_general | solution.py:916
  569.6 6.2 convolution_convert_fusion
  583.0 7.1 fusion.250
  590.1 7.1 add_convert_fusion
  606.6 9.4 add_add_fusion.2
  616.0 14.7 %collective-permute-done.80 = bf16[2,128,2048]{2,1,0:T(8,128)(2,1)S(1)} collective-permute-done((bf16[2,128,2048]{2,1,0:T(8,128)(2,1)S(1)}, bf16[2,128,2048]{2,1,0:T(8,128)(2,1)S(1)}, u32[]{:S(2)}, u32[]{:S(2)}) %collective-permute-start.80) | collective-permute-done | bytes 1048608 | tf_op jit(solution)/shard_map/ppermute | solution.py:444
  644.1 5.9 fusion.252
  653.7 5.6 fusion.253
  659.3 7.9 add_add_fusion.1
  674.3 7.5 collective-permute-done.86
  687.3 9.0 collective-permute-done.88
  704.8 6.8 collective-permute-done.89
  723.8 11.5 %collective-permute-done.91 = bf16[128,2048]{1,0:T(8,128)(2,1)S(1)} collective-permute-done((bf16[128,2048]{1,0:T(8,128)(2,1)S(1)}, bf16[128,2048]{1,0:T(8,128)(2,1)S(1)}, u32[]{:S(2)}, u32[]{:S(2)}) %collective-permute-start.91) | collective-permute-done | bytes 524320 | tf_op jit(solution)/shard_map/ppermute | solution.py:461
  748.6 5.7 all-to-all-start.2
  754.3 5.9 fusion.255
  760.3 5.6 convolution_add_fusion
  785.0 5.5 fusion.257
  790.5 7.8 fusion.256
  798.2 12.3 %add_add_fusion = f32[792,2048]{1,0:T(8,128)} fusion(f32[792,2048]{1,0:T(8,128)} %convolution_add_fusion, f32[792,2048]{1,0:T(8,128)} %fusion.256, f32[792,2048]{1,0:T(8,128)} %fusion.257), kind=kLoop, calls=%fused_computation.10 | loop fusion | flops 3244032 | bytes 25952256 | tf_op jit(solution)/shard_map/add | solution.py:1019
  868.1 6.3 multiply_reduce_fusion
  892.3 6.5 slice.573
  919.1 7.7 collective-permute-done.119
  932.0 6.3 collective-permute-done.120
  972.0 6.3 collective-permute-done.115
  (1020 shorter events, 588.9 us)
Async XLA Ops:
  56.9 35.4 %collective-permute-start.14 = (bf16[2,160,2048]{2,1,0:T(8,128)(2,1)}, bf16[2,160,2048]{2,1,0:T(8,128)(2,1)}, u32[]{:S(2)}, u32[]{:S(2)}) collective-permute-start(bf16[2,160,2048]{2,1,0:T(8,128)(2,1)} %pad_maximum_fusion.16), channel_id=1, source_target_pairs={{0,1},{1,0},{2,3},{3,2},{4,5},{5,4},{6,7},{7,6},{8,9},{9,8},{10,11... | collective-permute-start | bytes 3932168 | tf_op jit(solution)/shard_map/ppermute | solution.py:444
  65.0 27.3 %collective-permute-start.15 = (bf16[256,768]{1,0:T(8,128)(2,1)}, bf16[256,768]{1,0:T(8,128)(2,1)S(1)}, u32[]{:S(2)}, u32[]{:S(2)}) collective-permute-start(bf16[256,768]{1,0:T(8,128)(2,1)} %collective-permute-done.11), channel_id=1, source_target_pairs={{0,4},{4,0},{8,12},{12,8},{16,20},{20,16},{24,28},{28,24},{1,5},{5... | collective-permute-start | bytes 1179656 | tf_op jit(solution)/shard_map/ppermute | solution.py:444
  66.4 25.9 %collective-permute-start.18 = (bf16[256,768]{1,0:T(8,128)(2,1)}, bf16[256,768]{1,0:T(8,128)(2,1)}, u32[]{:S(2)}, u32[]{:S(2)}) collective-permute-start(bf16[256,768]{1,0:T(8,128)(2,1)} %collective-permute-done.11), channel_id=1, source_target_pairs={{0,8},{4,12},{8,16},{12,20},{16,24},{20,28},{24,0},{28,4},{1,9},{5... | collective-permute-start | bytes 1179656 | tf_op jit(solution)/shard_map/ppermute | solution.py:461
  92.3 29.8 %collective-permute-start.21 = (bf16[256,768]{1,0:T(8,128)(2,1)}, bf16[256,768]{1,0:T(8,128)(2,1)}, u32[]{:S(2)}, u32[]{:S(2)}) collective-permute-start(bf16[256,768]{1,0:T(8,128)(2,1)} %collective-permute-done.18), channel_id=1, source_target_pairs={{0,4},{4,0},{8,12},{12,8},{16,20},{20,16},{24,28},{28,24},{1,5},{5... | collective-permute-start | bytes 1179656 | tf_op jit(solution)/shard_map/ppermute | solution.py:444
  93.0 29.1 %collective-permute-start.24 = (bf16[256,768]{1,0:T(8,128)(2,1)}, bf16[256,768]{1,0:T(8,128)(2,1)}, u32[]{:S(2)}, u32[]{:S(2)}) collective-permute-start(bf16[256,768]{1,0:T(8,128)(2,1)} %collective-permute-done.18), channel_id=1, source_target_pairs={{0,8},{4,12},{8,16},{12,20},{16,24},{20,28},{24,0},{28,4},{1,9},{5... | collective-permute-start | bytes 1179656 | tf_op jit(solution)/shard_map/ppermute | solution.py:461
  93.0 27.7 %collective-permute-start.23 = (bf16[512,256]{1,0:T(8,128)(2,1)}, bf16[512,256]{1,0:T(8,128)(2,1)}, u32[]{:S(2)}, u32[]{:S(2)}) collective-permute-start(bf16[512,256]{1,0:T(8,128)(2,1)} %collective-permute-done.20), channel_id=1, source_target_pairs={{0,4},{4,0},{8,12},{12,8},{16,20},{20,16},{24,28},{28,24},{1,5},{5... | collective-permute-start | bytes 786440 | tf_op jit(solution)/shard_map/ppermute | solution.py:444
  94.4 27.7 %collective-permute-start.26 = (bf16[512,256]{1,0:T(8,128)(2,1)}, bf16[512,256]{1,0:T(8,128)(2,1)}, u32[]{:S(2)}, u32[]{:S(2)}) collective-permute-start(bf16[512,256]{1,0:T(8,128)(2,1)} %collective-permute-done.20), channel_id=1, source_target_pairs={{0,8},{4,12},{8,16},{12,20},{16,24},{20,28},{24,0},{28,4},{1,9},{5... | collective-permute-start | bytes 786440 | tf_op jit(solution)/shard_map/ppermute | solution.py:461
  120.7 48.6 %collective-permute-start.31 = (bf16[128,2048]{1,0:T(8,128)(2,1)}, bf16[128,2048]{1,0:T(8,128)(2,1)S(1)}, u32[]{:S(2)}, u32[]{:S(2)}) collective-permute-start(bf16[128,2048]{1,0:T(8,128)(2,1)} %constant_dynamic-slice_fusion.5), channel_id=1, source_target_pairs={{0,4},{4,0},{8,12},{12,8},{16,20},{20,16},{24,28},{28,24},{1,5},{5... | collective-permute-start | bytes 1572872 | tf_op jit(solution)/shard_map/ppermute | solution.py:444
  122.1 27.1 %collective-permute-start.27 = (bf16[256,768]{1,0:T(8,128)(2,1)}, bf16[256,768]{1,0:T(8,128)(2,1)S(1)}, u32[]{:S(2)}, u32[]{:S(2)}) collective-permute-start(bf16[256,768]{1,0:T(8,128)(2,1)} %collective-permute-done.24), channel_id=1, source_target_pairs={{0,4},{4,0},{8,12},{12,8},{16,20},{20,16},{24,28},{28,24},{1,5},{5... | collective-permute-start | bytes 1179656 | tf_op jit(solution)/shard_map/ppermute | solution.py:444
  122.8 26.4 %collective-permute-start.29 = (bf16[512,256]{1,0:T(8,128)(2,1)}, bf16[512,256]{1,0:T(8,128)(2,1)S(1)}, u32[]{:S(2)}, u32[]{:S(2)}) collective-permute-start(bf16[512,256]{1,0:T(8,128)(2,1)} %collective-permute-done.26), channel_id=1, source_target_pairs={{0,4},{4,0},{8,12},{12,8},{16,20},{20,16},{24,28},{28,24},{1,5},{5... | collective-permute-start | bytes 786440 | tf_op jit(solution)/shard_map/ppermute | solution.py:444
  124.2 25.0 %collective-permute-start.28 = (bf16[64,1024]{1,0:T(8,128)(2,1)S(1)}, bf16[64,1024]{1,0:T(8,128)(2,1)S(1)}, u32[]{:S(2)}, u32[]{:S(2)}) collective-permute-start(bf16[64,1024]{1,0:T(8,128)(2,1)S(1)} %collective-permute-done.25), channel_id=1, source_target_pairs={{0,4},{4,0},{8,12},{12,8},{16,20},{20,16},{24,28},{28,24},{1,5},{5... | collective-permute-start | bytes 393224 | tf_op jit(solution)/shard_map/ppermute | solution.py:444
  149.4 34.1 %collective-permute-start.34 = (bf16[128,2048]{1,0:T(8,128)(2,1)}, bf16[128,2048]{1,0:T(8,128)(2,1)}, u32[]{:S(2)}, u32[]{:S(2)}) collective-permute-start(bf16[128,2048]{1,0:T(8,128)(2,1)} %collective-permute-done.30), channel_id=1, source_target_pairs={{0,4},{4,0},{8,12},{12,8},{16,20},{20,16},{24,28},{28,24},{1,5},{5... | collective-permute-start | bytes 1572872 | tf_op jit(solution)/shard_map/ppermute | solution.py:444
  154.2 52.4 %all-to-all-start = ((bf16[3,704,256]{2,0,1:T(4,128)(2,1)}), bf16[3,704,256]{2,0,1:T(4,128)(2,1)}, u32[]{:S(2)}, u32[]{:S(2)}) async-start(bf16[3,704,256]{2,0,1:T(4,128)(2,1)} %copy.242), calls=%async_computation | async-start | bytes 2883584 | tf_op jit(solution)/shard_map/all_to_all | solution.py:855
  198.9 27.6 %collective-permute-start.39 = (bf16[128,2048]{1,0:T(8,128)(2,1)}, bf16[128,2048]{1,0:T(8,128)(2,1)}, u32[]{:S(2)}, u32[]{:S(2)}) collective-permute-start(bf16[128,2048]{1,0:T(8,128)(2,1)} %collective-permute-done.32), channel_id=1, source_target_pairs={{0,4},{4,0},{8,12},{12,8},{16,20},{20,16},{24,28},{28,24},{1,5},{5... | collective-permute-start | bytes 1572872 | tf_op jit(solution)/shard_map/ppermute | solution.py:444
  203.9 22.6 %collective-permute-start.38 = (bf16[512,2048]{1,0:T(8,128)(2,1)}, bf16[512,2048]{1,0:T(8,128)(2,1)}, u32[]{:S(2)}, u32[]{:S(2)}) collective-permute-start(bf16[512,2048]{1,0:T(8,128)(2,1)} %pad_maximum_fusion.6), channel_id=1, source_target_pairs={{0,1},{1,0},{2,3},{3,2},{4,5},{5,4},{6,7},{7,6},{8,9},{9,8},{10,11... | collective-permute-start | bytes 6291464 | tf_op jit(solution)/shard_map/ppermute | solution.py:444
  204.1 136.6 %collective-permute-start.53 = (bf16[128,2048]{1,0:T(8,128)(2,1)}, bf16[128,2048]{1,0:T(8,128)(2,1)}, u32[]{:S(2)}, u32[]{:S(2)}) collective-permute-start(bf16[128,2048]{1,0:T(8,128)(2,1)} %collective-permute-done.35), channel_id=1, source_target_pairs={{0,4},{4,0},{8,12},{12,8},{16,20},{20,16},{24,28},{28,24},{1,5},{5... | collective-permute-start | bytes 1572872 | tf_op jit(solution)/shard_map/ppermute | solution.py:444
  268.2 104.3 %collective-permute-start.54 = (bf16[128,2048]{1,0:T(8,128)(2,1)S(1)}, bf16[128,2048]{1,0:T(8,128)(2,1)S(1)}, u32[]{:S(2)}, u32[]{:S(2)}) collective-permute-start(bf16[128,2048]{1,0:T(8,128)(2,1)S(1)} %collective-permute-done.47), channel_id=1, source_target_pairs={{0,4},{4,0},{8,12},{12,8},{16,20},{20,16},{24,28},{28,24},{1,5},{5... | collective-permute-start | bytes 1572872 | tf_op jit(solution)/shard_map/ppermute | solution.py:444
  270.0 26.1 %collective-permute-start.49 = (bf16[256,2048]{1,0:T(8,128)(2,1)S(1)}, bf16[256,2048]{1,0:T(8,128)(2,1)S(1)}, u32[]{:S(2)}, u32[]{:S(2)}) collective-permute-start(bf16[256,2048]{1,0:T(8,128)(2,1)S(1)} %pad_maximum_fusion.20), channel_id=1, source_target_pairs={{0,2},{1,3},{2,0},{3,1},{4,6},{5,7},{6,4},{7,5},{8,10},{9,11},{10,... | collective-permute-start | bytes 3145736 | tf_op jit(solution)/shard_map/ppermute | solution.py:444
  274.9 42.5 %collective-permute-start.48 = (bf16[256,2048]{1,0:T(8,128)(2,1)}, bf16[256,2048]{1,0:T(8,128)(2,1)S(1)}, u32[]{:S(2)}, u32[]{:S(2)}) collective-permute-start(bf16[256,2048]{1,0:T(8,128)(2,1)} %pad_maximum_fusion.19), channel_id=1, source_target_pairs={{0,2},{1,3},{2,0},{3,1},{4,6},{5,7},{6,4},{7,5},{8,10},{9,11},{10,... | collective-permute-start | bytes 3145736 | tf_op jit(solution)/shard_map/ppermute | solution.py:444
  318.9 23.8 %collective-permute-start.51 = (bf16[512,2048]{1,0:T(8,128)(2,1)}, bf16[512,2048]{1,0:T(8,128)(2,1)}, u32[]{:S(2)}, u32[]{:S(2)}) collective-permute-start(bf16[512,2048]{1,0:T(8,128)(2,1)} %pad_maximum_fusion.8), channel_id=1, source_target_pairs={{0,1},{1,0},{2,3},{3,2},{4,5},{5,4},{6,7},{7,6},{8,9},{9,8},{10,11... | collective-permute-start | bytes 6291464 | tf_op jit(solution)/shard_map/ppermute | solution.py:444
  340.7 31.8 %collective-permute-start.55 = (bf16[128,2048]{1,0:T(8,128)(2,1)S(1)}, bf16[128,2048]{1,0:T(8,128)(2,1)S(1)}, u32[]{:S(2)}, u32[]{:S(2)}) collective-permute-start(bf16[128,2048]{1,0:T(8,128)(2,1)S(1)} %collective-permute-done.47), channel_id=1, source_target_pairs={{0,8},{4,12},{8,16},{12,20},{16,24},{20,28},{24,0},{28,4},{1,9},{5... | collective-permute-start | bytes 1572872 | tf_op jit(solution)/shard_map/ppermute | solution.py:461
  355.5 40.2 %collective-permute-start.57 = (bf16[256,2048]{1,0:T(8,128)(2,1)}, bf16[256,2048]{1,0:T(8,128)(2,1)S(1)}, u32[]{:S(2)}, u32[]{:S(2)}) collective-permute-start(bf16[256,2048]{1,0:T(8,128)(2,1)} %pad_maximum_fusion.21), channel_id=1, source_target_pairs={{0,2},{1,3},{2,0},{3,1},{4,6},{5,7},{6,4},{7,5},{8,10},{9,11},{10,... | collective-permute-start | bytes 3145736 | tf_op jit(solution)/shard_map/ppermute | solution.py:444
  372.5 91.9 %collective-permute-start.64 = (bf16[128,2048]{1,0:T(8,128)(2,1)S(1)}, bf16[128,2048]{1,0:T(8,128)(2,1)S(1)}, u32[]{:S(2)}, u32[]{:S(2)}) collective-permute-start(bf16[128,2048]{1,0:T(8,128)(2,1)S(1)} %collective-permute-done.55), channel_id=1, source_target_pairs={{0,4},{4,0},{8,12},{12,8},{16,20},{20,16},{24,28},{28,24},{1,5},{5... | collective-permute-start | bytes 1572872 | tf_op jit(solution)/shard_map/ppermute | solution.py:444
  377.3 31.3 %collective-permute-start.59 = (bf16[2,128,2048]{2,1,0:T(8,128)(2,1)}, bf16[2,128,2048]{2,1,0:T(8,128)(2,1)S(1)}, u32[]{:S(2)}, u32[]{:S(2)}) collective-permute-start(bf16[2,128,2048]{2,1,0:T(8,128)(2,1)} %fusion.34), channel_id=1, source_target_pairs={{0,4},{4,0},{8,12},{12,8},{16,20},{20,16},{24,28},{28,24},{1,5},{5... | collective-permute-start | bytes 3145736 | tf_op jit(solution)/shard_map/ppermute | solution.py:444
  379.2 29.4 %collective-permute-start.58 = (bf16[256,2048]{1,0:T(8,128)(2,1)}, bf16[256,2048]{1,0:T(8,128)(2,1)S(1)}, u32[]{:S(2)}, u32[]{:S(2)}) collective-permute-start(bf16[256,2048]{1,0:T(8,128)(2,1)} %pad_maximum_fusion.22), channel_id=1, source_target_pairs={{0,2},{1,3},{2,0},{3,1},{4,6},{5,7},{6,4},{7,5},{8,10},{9,11},{10,... | collective-permute-start | bytes 3145736 | tf_op jit(solution)/shard_map/ppermute | solution.py:444
  409.0 25.5 %collective-permute-start.62 = (bf16[128,2048]{1,0:T(8,128)(2,1)S(1)}, bf16[128,2048]{1,0:T(8,128)(2,1)S(1)}, u32[]{:S(2)}, u32[]{:S(2)}) collective-permute-start(bf16[128,2048]{1,0:T(8,128)(2,1)S(1)} %fusion.81), channel_id=1, source_target_pairs={{0,2},{1,3},{2,0},{3,1},{4,6},{5,7},{6,4},{7,5},{8,10},{9,11},{10,... | collective-permute-start | bytes 1572872 | tf_op jit(solution)/shard_map/ppermute | solution.py:444
  447.4 36.3 %collective-permute-start.66 = (bf16[256,2048]{1,0:T(8,128)(2,1)}, bf16[256,2048]{1,0:T(8,128)(2,1)S(1)}, u32[]{:S(2)}, u32[]{:S(2)}) collective-permute-start(bf16[256,2048]{1,0:T(8,128)(2,1)} %pad_maximum_fusion.23), channel_id=1, source_target_pairs={{0,2},{1,3},{2,0},{3,1},{4,6},{5,7},{6,4},{7,5},{8,10},{9,11},{10,... | collective-permute-start | bytes 3145736 | tf_op jit(solution)/shard_map/ppermute | solution.py:444
  465.3 24.7 %collective-permute-start.68 = (bf16[2,128,2048]{2,1,0:T(8,128)(2,1)S(1)}, bf16[2,128,2048]{2,1,0:T(8,128)(2,1)S(1)}, u32[]{:S(2)}, u32[]{:S(2)}) collective-permute-start(bf16[2,128,2048]{2,1,0:T(8,128)(2,1)S(1)} %fusion.35), channel_id=1, source_target_pairs={{0,4},{4,0},{8,12},{12,8},{16,20},{20,16},{24,28},{28,24},{1,5},{5... | collective-permute-start | bytes 3145736 | tf_op jit(solution)/shard_map/ppermute | solution.py:444
  467.1 27.9 %collective-permute-start.67 = (bf16[256,2048]{1,0:T(8,128)(2,1)}, bf16[256,2048]{1,0:T(8,128)(2,1)S(1)}, u32[]{:S(2)}, u32[]{:S(2)}) collective-permute-start(bf16[256,2048]{1,0:T(8,128)(2,1)} %pad_maximum_fusion.24), channel_id=1, source_target_pairs={{0,2},{1,3},{2,0},{3,1},{4,6},{5,7},{6,4},{7,5},{8,10},{9,11},{10,... | collective-permute-start | bytes 3145736 | tf_op jit(solution)/shard_map/ppermute | solution.py:444
  495.4 23.8 %collective-permute-start.71 = (bf16[128,2048]{1,0:T(8,128)(2,1)S(1)}, bf16[128,2048]{1,0:T(8,128)(2,1)S(1)}, u32[]{:S(2)}, u32[]{:S(2)}) collective-permute-start(bf16[128,2048]{1,0:T(8,128)(2,1)S(1)} %fusion.82), channel_id=1, source_target_pairs={{0,2},{1,3},{2,0},{3,1},{4,6},{5,7},{6,4},{7,5},{8,10},{9,11},{10,... | collective-permute-start | bytes 1572872 | tf_op jit(solution)/shard_map/ppermute | solution.py:444
  545.2 31.9 %collective-permute-start.75 = (bf16[2,128,2048]{2,1,0:T(8,128)(2,1)}, bf16[2,128,2048]{2,1,0:T(8,128)(2,1)S(1)}, u32[]{:S(2)}, u32[]{:S(2)}) collective-permute-start(bf16[2,128,2048]{2,1,0:T(8,128)(2,1)} %fusion.36), channel_id=1, source_target_pairs={{0,4},{4,0},{8,12},{12,8},{16,20},{20,16},{24,28},{28,24},{1,5},{5... | collective-permute-start | bytes 3145736 | tf_op jit(solution)/shard_map/ppermute | solution.py:444
  598.9 31.8 %collective-permute-start.81 = (bf16[2,2,128,2048]{3,2,0,1:T(8,128)(2,1)S(1)}, bf16[2,2,128,2048]{3,2,0,1:T(8,128)(2,1)S(1)}, u32[]{:S(2)}, u32[]{:S(2)}) collective-permute-start(bf16[2,2,128,2048]{3,2,0,1:T(8,128)(2,1)S(1)} %copy.264), channel_id=1, source_target_pairs={{0,1},{1,0},{2,3},{3,2},{4,5},{5,4},{6,7},{7,6},{8,9},{9,8},{10,11... | collective-permute-start | bytes 6291464 | tf_op jit(solution)/shard_map/ppermute | solution.py:444
  605.4 25.3 %collective-permute-start.80 = (bf16[2,128,2048]{2,1,0:T(8,128)(2,1)S(1)}, bf16[2,128,2048]{2,1,0:T(8,128)(2,1)S(1)}, u32[]{:S(2)}, u32[]{:S(2)}) collective-permute-start(bf16[2,128,2048]{2,1,0:T(8,128)(2,1)S(1)} %fusion.37), channel_id=1, source_target_pairs={{0,2},{1,3},{2,0},{3,1},{4,6},{5,7},{6,4},{7,5},{8,10},{9,11},{10,... | collective-permute-start | bytes 3145736 | tf_op jit(solution)/shard_map/ppermute | solution.py:444
  632.8 34.4 %collective-permute-start.84 = (bf16[2,128,2048]{2,1,0:T(8,128)(2,1)}, bf16[2,128,2048]{2,1,0:T(8,128)(2,1)}, u32[]{:S(2)}, u32[]{:S(2)}) collective-permute-start(bf16[2,128,2048]{2,1,0:T(8,128)(2,1)} %fusion.39), channel_id=1, source_target_pairs={{0,4},{4,0},{8,12},{12,8},{16,20},{20,16},{24,28},{28,24},{1,5},{5... | collective-permute-start | bytes 3145736 | tf_op jit(solution)/shard_map/ppermute | solution.py:444
  638.3 28.9 %collective-permute-start.83 = (bf16[2,128,2048]{2,1,0:T(8,128)(2,1)S(1)}, bf16[2,128,2048]{2,1,0:T(8,128)(2,1)S(1)}, u32[]{:S(2)}, u32[]{:S(2)}) collective-permute-start(bf16[2,128,2048]{2,1,0:T(8,128)(2,1)S(1)} %fusion.38), channel_id=1, source_target_pairs={{0,2},{1,3},{2,0},{3,1},{4,6},{5,7},{6,4},{7,5},{8,10},{9,11},{10,... | collective-permute-start | bytes 3145736 | tf_op jit(solution)/shard_map/ppermute | solution.py:444
  639.4 27.8 %all-to-all-start.1 = ((f32[8,2,128]{2,1,0:T(2,128)}), f32[8,2,128]{2,1,0:T(2,128)S(1)}, u32[]{:S(2)}, u32[]{:S(2)}) async-start(f32[8,2,128]{2,1,0:T(2,128)} %gather_fusion), calls=%async_computation.1 | async-start | bytes 16384 | tf_op jit(solution)/shard_map/all_to_all | solution.py:964
  736.3 35.5 %collective-permute-start.93 = (bf16[128,2048]{1,0:T(8,128)(2,1)}, bf16[128,2048]{1,0:T(8,128)(2,1)}, u32[]{:S(2)}, u32[]{:S(2)}) collective-permute-start(bf16[128,2048]{1,0:T(8,128)(2,1)} %fusion.51), channel_id=1, source_target_pairs={{0,8},{4,12},{8,16},{12,20},{16,24},{20,28},{24,0},{28,4},{1,9},{5... | collective-permute-start | bytes 1572872 | tf_op jit(solution)/shard_map/ppermute | solution.py:461
  740.7 31.0 %collective-permute-start.92 = (bf16[2,128,2048]{2,1,0:T(8,128)(2,1)}, bf16[2,128,2048]{2,1,0:T(8,128)(2,1)}, u32[]{:S(2)}, u32[]{:S(2)}) collective-permute-start(bf16[2,128,2048]{2,1,0:T(8,128)(2,1)} %fusion.40), channel_id=1, source_target_pairs={{0,2},{1,3},{2,0},{3,1},{4,6},{5,7},{6,4},{7,5},{8,10},{9,11},{10,... | collective-permute-start | bytes 3145736 | tf_op jit(solution)/shard_map/ppermute | solution.py:444
  748.6 67.1 %all-to-all-start.2 = ((bf16[2,88,2048]{1,0,2:T(2,128)(2,1)}), bf16[2,88,2048]{1,0,2:T(2,128)(2,1)}, u32[]{:S(2)}, u32[]{:S(2)}) async-start(bf16[2,88,2048]{1,0,2:T(2,128)(2,1)} %copy.271), calls=%async_computation.2 | async-start | bytes 2097152 | tf_op jit(solution)/shard_map/all_to_all | solution.py:1007
  772.8 46.5 %collective-permute-start.97 = (bf16[2,512,256]{2,1,0:T(8,128)(2,1)}, bf16[2,512,256]{2,1,0:T(8,128)(2,1)}, u32[]{:S(2)}, u32[]{:S(2)}) collective-permute-start(bf16[2,512,256]{2,1,0:T(8,128)(2,1)} %pad_maximum_fusion.47), channel_id=1, source_target_pairs={{0,4},{4,0},{8,12},{12,8},{16,20},{20,16},{24,28},{28,24},{1,5},{5... | collective-permute-start | bytes 1572872 | tf_op jit(solution)/shard_map/ppermute | solution.py:444
  775.6 43.7 %collective-permute-start.96 = (bf16[2,512,256]{2,1,0:T(8,128)(2,1)}, bf16[2,512,256]{2,1,0:T(8,128)(2,1)}, u32[]{:S(2)}, u32[]{:S(2)}) collective-permute-start(bf16[2,512,256]{2,1,0:T(8,128)(2,1)} %pad_maximum_fusion.46), channel_id=1, source_target_pairs={{0,4},{4,0},{8,12},{12,8},{16,20},{20,16},{24,28},{28,24},{1,5},{5... | collective-permute-start | bytes 1572872 | tf_op jit(solution)/shard_map/ppermute | solution.py:444
  778.3 41.0 %collective-permute-start.95 = (bf16[128,2048]{1,0:T(8,128)(2,1)}, bf16[128,2048]{1,0:T(8,128)(2,1)}, u32[]{:S(2)}, u32[]{:S(2)}) collective-permute-start(bf16[128,2048]{1,0:T(8,128)(2,1)} %fusion.87), channel_id=1, source_target_pairs={{0,4},{4,0},{8,12},{12,8},{16,20},{20,16},{24,28},{28,24},{1,5},{5... | collective-permute-start | bytes 1572872 | tf_op jit(solution)/shard_map/ppermute | solution.py:444
  784.0 35.3 %collective-permute-start.94 = (bf16[2,128,2048]{2,1,0:T(8,128)(2,1)}, bf16[2,128,2048]{2,1,0:T(8,128)(2,1)}, u32[]{:S(2)}, u32[]{:S(2)}) collective-permute-start(bf16[2,128,2048]{2,1,0:T(8,128)(2,1)} %fusion.41), channel_id=1, source_target_pairs={{0,2},{1,3},{2,0},{3,1},{4,6},{5,7},{6,4},{7,5},{8,10},{9,11},{10,... | collective-permute-start | bytes 3145736 | tf_op jit(solution)/shard_map/ppermute | solution.py:444
  876.5 51.5 %collective-permute-start.108 = (bf16[2,160,2048]{2,1,0:T(8,128)(2,1)S(1)}, bf16[2,160,2048]{2,1,0:T(8,128)(2,1)}, u32[]{:S(2)}, u32[]{:S(2)}) collective-permute-start(bf16[2,160,2048]{2,1,0:T(8,128)(2,1)S(1)} %dynamic-slice_bitcast_fusion), channel_id=1, source_target_pairs={{0,1},{1,0},{2,3},{3,2},{4,5},{5,4},{6,7},{7,6},{8,9},{9,8},{10,11... | collective-permute-start | bytes 3932168 | tf_op jit(solution)/shard_map/ppermute | solution.py:444
  878.7 28.9 %collective-permute-start.127 = (bf16[512,256]{1,0:T(8,128)(2,1)}, bf16[512,256]{1,0:T(8,128)(2,1)}, u32[]{:S(2)}, u32[]{:S(2)}) collective-permute-start(bf16[512,256]{1,0:T(8,128)(2,1)} %fusion.90), channel_id=1, source_target_pairs={{0,8},{4,12},{8,16},{12,20},{16,24},{20,28},{24,0},{28,4},{1,9},{5... | collective-permute-start | bytes 786440 | tf_op jit(solution)/shard_map/ppermute | solution.py:461
  884.9 29.6 %collective-permute-start.118 = (bf16[2,256,768]{2,1,0:T(8,128)(2,1)}, bf16[2,256,768]{2,1,0:T(8,128)(2,1)}, u32[]{:S(2)}, u32[]{:S(2)}) collective-permute-start(bf16[2,256,768]{2,1,0:T(8,128)(2,1)} %pad_maximum_fusion.39), channel_id=1, source_target_pairs={{0,4},{4,0},{8,12},{12,8},{16,20},{20,16},{24,28},{28,24},{1,5},{5... | collective-permute-start | bytes 2359304 | tf_op jit(solution)/shard_map/ppermute | solution.py:444
  886.6 29.7 %collective-permute-start.104 = (bf16[2,128,2048]{2,1,0:T(8,128)(2,1)S(1)}, bf16[2,128,2048]{2,1,0:T(8,128)(2,1)}, u32[]{:S(2)}, u32[]{:S(2)}) collective-permute-start(bf16[2,128,2048]{2,1,0:T(8,128)(2,1)S(1)} %fusion.33), channel_id=1, source_target_pairs={{0,1},{1,0},{2,3},{3,2},{4,5},{5,4},{6,7},{7,6},{8,9},{9,8},{10,11... | collective-permute-start | bytes 3145736 | tf_op jit(solution)/shard_map/ppermute | solution.py:444
  938.5 24.4 %collective-permute-start.121 = (bf16[256,768]{1,0:T(8,128)(2,1)S(1)}, bf16[256,768]{1,0:T(8,128)(2,1)S(1)}, u32[]{:S(2)}, u32[]{:S(2)}) collective-permute-start(bf16[256,768]{1,0:T(8,128)(2,1)S(1)} %fusion.72), channel_id=1, source_target_pairs={{0,8},{4,12},{8,16},{12,20},{16,24},{20,28},{24,0},{28,4},{1,9},{5... | collective-permute-start | bytes 1179656 | tf_op jit(solution)/shard_map/ppermute | solution.py:461
  (282 other events, 3316.1 us)
